TPU v7x, 32 devices: a whole 2x2x4 slice. The times are simulated.
32 devices in a mesh: rep: 8 (over z, core), exp: 4 (over y, x).
Axes of the slice: x: 2, y: 2, z: 4, core: 2. Of those that a mesh axis runs over, the one named last changes fastest.
Arguments:
- tokens: bfloat16 [12608, 768], P(('rep', 'exp')), may hold values from -6 to 6
- routes: int32 [12608, 2], P(('rep', 'exp')), may hold values from 0 to 3, all different within a row
- out_grad: bfloat16 [12608, 768], P(('rep', 'exp')), may hold values from -6 to 6
- attn_qkv: bfloat16 [768, 2304], P('exp'), may hold values from -0.21875 to 0.21875
- attn_out: bfloat16 [768, 768], P('exp'), may hold values from -1.5 to 1.5
- router: bfloat16 [768, 4], P('exp'), may hold values from -0.15625 to 0.15625
- norm_gains: bfloat16 [2, 768], P(None, 'exp'), may hold values from 0.25 to 1.75
- dense_biases: bfloat16 [5, 768], P(None, 'exp'), may hold values from -1.796875 to 1.796875
- expert_in: bfloat16 [4, 768, 3072], P('exp'), may hold values from -0.21875 to 0.21875
- expert_in_bias: bfloat16 [4, 3072], P('exp'), may hold values from -0.59765625 to 0.59765625
- expert_out: bfloat16 [4, 3072, 768], P('exp'), may hold values from -0.21875 to 0.21875
- expert_out_bias: bfloat16 [4, 768], P('exp'), may hold values from -3 to 3
Outputs:
- output: bfloat16 [12608, 768], P(('rep', 'exp'))
- grad_input: bfloat16 [12608, 768], P(('rep', 'exp'))
- grad_attn_qkv: float32 [768, 2304], P('exp')
- grad_attn_out: float32 [768, 768], P('exp')
- grad_router: float32 [768, 4], P('exp')
- grad_norm_gains: float32 [2, 768], P(None, 'exp')
- grad_dense_biases: float32 [5, 768], P(None, 'exp')
- grad_expert_in: float32 [4, 768, 3072], P('exp', None, 'rep')
- grad_expert_in_bias: float32 [4, 3072], P('exp', 'rep')
- grad_expert_out: float32 [4, 3072, 768], P('exp', 'rep')
- grad_expert_out_bias: float32 [4, 768], P('exp', 'rep')
Inputs may be any that keep to these rules, and one draw needn't show every extreme that they name: `routes`: each row names two different experts; every expert is named by some row.
All inputs are finite; a program needn't handle non-finite values.
Results may differ from a plain program's by a relative error of at most 0.028.
Values may be sent and summed in bfloat16 or wider, within the bound.
A program may use at most 192 MiB of HBM per device.

v0:
```python
from functools import partial
import math

import jax
import jax.numpy as jnp
from jax import lax
from jax.sharding import PartitionSpec as P

HEADS = 12
HEAD_DIM = 64
SEQ = 197


norm_eps = 1e-06


def layer_norm(values, gain_row, shift_row):
    center = values - jnp.mean(values, -1, keepdims=True)
    spread = jnp.mean(center * center, -1, keepdims=True)
    return center * lax.rsqrt(spread + norm_eps) * gain_row + shift_row


def matmul(first_op, second_op):
    return jnp.dot(first_op, second_op, preferred_element_type=jnp.float32)


def on_device(
    tokens,
    routes,
    out_grad,
    attn_qkv,
    attn_out,
    router,
    norm_gains,
    dense_biases,
    expert_in,
    expert_in_bias,
    expert_out,
    expert_out_bias,
):
    model_width = tokens.shape[1]
    tok_rows = tokens.shape[0]
    experts = router.shape[1]
    images = tok_rows // SEQ
    capacity = (18 * tok_rows + 8 * experts - 1) // (8 * experts)
    scale = 1.0 / math.sqrt(HEAD_DIM)
    four_shape = (images, SEQ, HEADS, HEAD_DIM)
    gathered = (
        lax.all_gather(attn_qkv, "exp", axis=0, tiled=True),
        lax.all_gather(attn_out, "exp", axis=0, tiled=True),
        lax.all_gather(router, "exp", axis=0, tiled=True),
        lax.all_gather(norm_gains, "exp", axis=1, tiled=True),
        lax.all_gather(dense_biases, "exp", axis=1, tiled=True),
    )
    w_qkv = gathered[0]
    w_proj = gathered[1]
    w_route = gathered[2]
    gains_all = gathered[3].astype(jnp.float32)
    biases_all = gathered[4].astype(jnp.float32)
    inputs = tokens.astype(jnp.float32)
    normed_low = layer_norm(inputs, gains_all[0], biases_all[0]).astype(jnp.bfloat16)
    qkv_all = matmul(normed_low, w_qkv)
    query_four = (qkv_all[:, :model_width] + biases_all[1]).astype(jnp.bfloat16).reshape(four_shape)
    key_four = qkv_all[:, model_width : 2 * model_width].astype(jnp.bfloat16).reshape(four_shape)
    value_four = (
        (qkv_all[:, 2 * model_width :] + biases_all[2]).astype(jnp.bfloat16).reshape(four_shape)
    )
    scores = (
        jnp.einsum("ishd,ithd->ihst", query_four, key_four, preferred_element_type=jnp.float32)
        * scale
    )
    top_score = jnp.max(scores, -1, keepdims=True)
    log_total = top_score + jnp.log(jnp.sum(jnp.exp(scores - top_score), -1, keepdims=True))
    probs_low = jnp.exp(scores - log_total).astype(jnp.bfloat16)
    context = jnp.einsum(
        "ihst,ithd->ishd", probs_low, value_four, preferred_element_type=jnp.float32
    )
    context_low = context.reshape(tok_rows, model_width).astype(jnp.bfloat16)
    resid_one = inputs + (matmul(context_low, w_proj) + biases_all[3])
    second_low = layer_norm(resid_one, gains_all[1], biases_all[4]).astype(jnp.bfloat16)
    route_probs = jax.nn.softmax(matmul(second_low, w_route), -1)
    gates = jnp.take_along_axis(route_probs, routes, 1)
    pair_expert = jnp.concatenate([routes[:, 0], routes[:, 1]])
    expert_ids = jnp.arange(experts, dtype=jnp.int32)
    onehot = (pair_expert[:, None] == expert_ids[None, :]).astype(jnp.int32)
    position = jnp.sum((jnp.cumsum(onehot, 0) - onehot) * onehot, 1)
    kept_pair = position < capacity
    total_slots = experts * capacity
    slot_index = jnp.where(kept_pair, pair_expert * capacity + position, total_slots)
    safe_index = jnp.minimum(slot_index, total_slots - 1)
    pair_gate = jnp.concatenate([gates[:, 0], gates[:, 1]])
    pair_weight = jnp.where(kept_pair, pair_gate, 0.0)
    send_rows = jnp.concatenate([second_low, second_low])
    send_buffer = (
        jnp.zeros((total_slots, model_width), jnp.bfloat16)
        .at[slot_index]
        .set(send_rows, mode="drop")
    )
    send_buffer = send_buffer.reshape(experts, capacity, model_width)
    w_first = expert_in[0]
    b_first = expert_in_bias[0].astype(jnp.float32)
    w_second = expert_out[0]
    b_second = expert_out_bias[0].astype(jnp.float32)
    received = lax.all_to_all(send_buffer, "exp", split_axis=0, concat_axis=0, tiled=True)
    row_block = received.reshape(-1, model_width)
    hidden = matmul(row_block, w_first) + b_first
    active = jax.nn.gelu(hidden, approximate=False).astype(jnp.bfloat16)
    result = (matmul(active, w_second) + b_second).astype(jnp.bfloat16).reshape(received.shape)
    returned = lax.all_to_all(result, "exp", split_axis=0, concat_axis=0, tiled=True)
    returned, received_all = (returned, received)
    pair_output = returned.reshape(total_slots, model_width)[safe_index].astype(jnp.float32)
    contrib = pair_weight[:, None] * pair_output
    mixture = contrib[:tok_rows] + contrib[tok_rows:]
    output = (resid_one + mixture).astype(jnp.bfloat16)
    grad_out = out_grad.astype(jnp.float32)
    grad_twice = jnp.concatenate([grad_out, grad_out])
    gate_grad = jnp.where(kept_pair, jnp.sum(grad_twice * pair_output, 1), 0.0)
    result_grad = (pair_weight[:, None] * grad_twice).astype(jnp.bfloat16)
    grad_buffer = (
        jnp.zeros((total_slots, model_width), jnp.bfloat16)
        .at[slot_index]
        .set(result_grad, mode="drop")
    )
    grad_buffer = grad_buffer.reshape(experts, capacity, model_width)
    grad_received = lax.all_to_all(grad_buffer, "exp", split_axis=0, concat_axis=0, tiled=True)
    row_block = received_all.reshape(-1, model_width)
    hidden = matmul(row_block, w_first) + b_first
    gelu_pair = jax.vjp(partial(jax.nn.gelu, approximate=False), hidden)
    active_low = gelu_pair[0].astype(jnp.bfloat16)
    result_rows = grad_received.reshape(-1, model_width)
    grad_w_second = matmul(active_low.T, result_rows)
    grad_b_second = jnp.sum(result_rows.astype(jnp.float32), 0)
    active_grad = matmul(result_rows, w_second.T)
    hidden_grad = gelu_pair[1](active_grad)[0].astype(jnp.bfloat16)
    grad_w_first = matmul(row_block.T, hidden_grad)
    grad_b_first = jnp.sum(hidden_grad.astype(jnp.float32), 0)
    input_rows = matmul(hidden_grad, w_first.T).astype(jnp.bfloat16).reshape(received_all.shape)
    grad_back = lax.all_to_all(input_rows, "exp", split_axis=0, concat_axis=0, tiled=True)
    pair_back = jnp.where(
        kept_pair[:, None],
        grad_back.reshape(total_slots, model_width)[safe_index].astype(jnp.float32),
        0.0,
    )
    second_grad = pair_back[:tok_rows] + pair_back[tok_rows:]
    gate_two = jnp.stack([gate_grad[:tok_rows], gate_grad[tok_rows:]], 1)
    route_match = (routes[:, :, None] == expert_ids[None, None, :]).astype(jnp.float32)
    prob_grad = jnp.sum(gate_two[:, :, None] * route_match, 1)
    logit_grad = route_probs * (prob_grad - jnp.sum(prob_grad * route_probs, 1, keepdims=True))
    logit_low = logit_grad.astype(jnp.bfloat16)
    grad_router = matmul(second_low.T, logit_low)
    second_grad = second_grad + matmul(logit_low, w_route.T)
    norm_second = jax.vjp(layer_norm, resid_one, gains_all[1], biases_all[4])
    resid_back, gain_two, shift_two = norm_second[1](second_grad)
    resid_grad = grad_out + resid_back
    proj_grad = resid_grad.astype(jnp.bfloat16)
    grad_bias_out = jnp.sum(proj_grad.astype(jnp.float32), 0)
    grad_proj = matmul(context_low.T, proj_grad)
    context_grad = matmul(proj_grad, w_proj.T).astype(jnp.bfloat16).reshape(four_shape)
    scores = (
        jnp.einsum("ishd,ithd->ihst", query_four, key_four, preferred_element_type=jnp.float32)
        * scale
    )
    probs_att = jnp.exp(scores - log_total)
    probs_low = probs_att.astype(jnp.bfloat16)
    value_grad = jnp.einsum(
        "ihst,ishd->ithd", probs_low, context_grad, preferred_element_type=jnp.float32
    ).astype(jnp.bfloat16)
    prob_back = jnp.einsum(
        "ishd,ithd->ihst", context_grad, value_four, preferred_element_type=jnp.float32
    )
    score_grad = (
        probs_att * (prob_back - jnp.sum(prob_back * probs_att, -1, keepdims=True))
    ).astype(jnp.bfloat16)
    query_grad = (
        jnp.einsum("ihst,ithd->ishd", score_grad, key_four, preferred_element_type=jnp.float32)
        * scale
    ).astype(jnp.bfloat16)
    key_grad = (
        jnp.einsum("ihst,ishd->ithd", score_grad, query_four, preferred_element_type=jnp.float32)
        * scale
    ).astype(jnp.bfloat16)
    query_flat = query_grad.reshape(tok_rows, model_width)
    value_flat = value_grad.reshape(tok_rows, model_width)
    qkv_grad = jnp.concatenate([query_flat, key_grad.reshape(tok_rows, model_width), value_flat], 1)
    grad_qkv = matmul(normed_low.T, qkv_grad)
    normed_grad = matmul(qkv_grad, w_qkv.T)
    norm_first = jax.vjp(layer_norm, inputs, gains_all[0], biases_all[0])
    input_back, gain_one, shift_one = norm_first[1](normed_grad)
    grad_input = (resid_grad + input_back).astype(jnp.bfloat16)
    grad_gains = jnp.stack([gain_one, gain_two])
    grad_biases = jnp.stack(
        [
            shift_one,
            jnp.sum(query_flat.astype(jnp.float32), 0),
            jnp.sum(value_flat.astype(jnp.float32), 0),
            grad_bias_out,
            shift_two,
        ]
    )
    summed = (
        lax.psum(grad_qkv.astype(jnp.bfloat16), "rep").astype(jnp.float32),
        lax.psum(grad_proj.astype(jnp.bfloat16), "rep").astype(jnp.float32),
        lax.psum(grad_router.astype(jnp.bfloat16), "rep").astype(jnp.float32),
        lax.psum(grad_gains.astype(jnp.bfloat16), "rep").astype(jnp.float32),
        lax.psum(grad_biases.astype(jnp.bfloat16), "rep").astype(jnp.float32),
    )
    dense_out = (
        lax.psum_scatter(
            summed[0].astype(jnp.bfloat16), "exp", scatter_dimension=0, tiled=True
        ).astype(jnp.float32),
        lax.psum_scatter(
            summed[1].astype(jnp.bfloat16), "exp", scatter_dimension=0, tiled=True
        ).astype(jnp.float32),
        lax.psum_scatter(
            summed[2].astype(jnp.bfloat16), "exp", scatter_dimension=0, tiled=True
        ).astype(jnp.float32),
        lax.psum_scatter(
            summed[3].astype(jnp.bfloat16), "exp", scatter_dimension=1, tiled=True
        ).astype(jnp.float32),
        lax.psum_scatter(
            summed[4].astype(jnp.bfloat16), "exp", scatter_dimension=1, tiled=True
        ).astype(jnp.float32),
    )
    expert_parts = (
        lax.psum_scatter(
            grad_w_first[None].astype(jnp.bfloat16), "rep", scatter_dimension=2, tiled=True
        ).astype(jnp.float32),
        lax.psum_scatter(
            grad_b_first[None].astype(jnp.bfloat16), "rep", scatter_dimension=1, tiled=True
        ).astype(jnp.float32),
        lax.psum_scatter(
            grad_w_second[None].astype(jnp.bfloat16), "rep", scatter_dimension=1, tiled=True
        ).astype(jnp.float32),
        lax.psum_scatter(
            grad_b_second[None].astype(jnp.bfloat16), "rep", scatter_dimension=1, tiled=True
        ).astype(jnp.float32),
    )
    return (
        output,
        grad_input,
        dense_out[0],
        dense_out[1],
        dense_out[2],
        dense_out[3],
        dense_out[4],
        expert_parts[0],
        expert_parts[1],
        expert_parts[2],
        expert_parts[3],
    )


def solution(mesh):
    in_specs = (
        P(("rep", "exp"), None),
        P(("rep", "exp"), None),
        P(("rep", "exp"), None),
        P("exp", None),
        P("exp", None),
        P("exp", None),
        P(None, "exp"),
        P(None, "exp"),
        P("exp", None, None),
        P("exp", None),
        P("exp", None, None),
        P("exp", None),
    )
    out_specs = (
        P(("rep", "exp"), None),
        P(("rep", "exp"), None),
        P("exp", None),
        P("exp", None),
        P("exp", None),
        P(None, "exp"),
        P(None, "exp"),
        P("exp", None, "rep"),
        P("exp", "rep"),
        P("exp", "rep", None),
        P("exp", "rep"),
    )
    return jax.shard_map(
        on_device, mesh=mesh, in_specs=in_specs, out_specs=out_specs, check_vma=False
    )
```

profile of v0, /device:TPU:0, one launch (start us, length us, event | category | flops | bytes accessed | tf_op | source)
XLA Modules:
  0.0 704.2 jit_solution(6630411404808025383)
XLA Ops:
  11.9 9.6 %all-gather = bf16[4,192,2]{1,2,0:T(2,128)(2,1)S(1)} all-gather(bf16[1,192,2]{1,2,0:T(2,128)(2,1)} %bitcast.152), channel_id=1, replica_groups=mesh['rep'=8,'exp'=4] {'exp'}, dimensions={0}, use_global_device_ids=true | all-gather | bytes 3840 | tf_op jit(solution)/shard_map/all_gather | solution.py:52
  24.2 8.2 %all-gather.1 = bf16[4,192,5]{1,2,0:T(8,128)(2,1)S(1)} all-gather(bf16[1,192,5]{1,2,0:T(8,128)(2,1)S(1)} %bitcast.150), channel_id=1, replica_groups=mesh['rep'=8,'exp'=4] {'exp'}, dimensions={0}, use_global_device_ids=true | all-gather | bytes 9600 | tf_op jit(solution)/shard_map/all_gather | solution.py:53
  32.5 27.5 %all-gather.6.cloned.1.call-done = bf16[768,2304]{1,0:T(8,128)(2,1)} async-done(((bf16[192,2304]{1,0:T(8,128)(2,1)}), bf16[768,2304]{1,0:T(8,128)(2,1)}) %all-gather.6.cloned.1.call-update) | async-done | bytes 3538960 | tf_op jit(solution)/shard_map/all_gather | solution.py:49
  84.6 4.9 all-gather.8.cloned.1.call-done
  93.0 8.0 %scatter_custom_fusion = bf16[888,768]{1,0:T(8,128)(2,1)S(1)} fusion(s32[788]{0:T(1024)S(1)} %get-tuple-element.26, bf16[394,768]{1,0:T(8,128)(2,1)S(1)} %add_convert_fusion.3, bf16[]{:T(256)} %constant.155, bf16[]{:T(256)} %constant.25.clone.1), kind=kCustom, calls=%fused_computation.95 | custom fusion | flops 2420736 | bytes 1978372 | tf_op jit(solution)/shard_map/scatter | solution.py:97
  106.2 17.3 %all-to-all-done = bf16[4,222,768]{2,1,0:T(8,128)(2,1)S(1)} async-done(((bf16[4,222,768]{2,1,0:T(8,128)(2,1)}), bf16[4,222,768]{2,1,0:T(8,128)(2,1)S(1)}, u32[]{:S(2)}, u32[]{:S(2)}) %all-to-all-start) | async-done | bytes 1364000 | tf_op jit(solution)/shard_map/all_to_all | solution.py:104
  125.0 32.2 %multiply_convert_fusion = (bf16[888,3072]{1,0:T(8,128)(2,1)S(1)}, f32[888,3072]{1,0:T(8,128)}, f32[888,3072]{1,0:T(8,128)}) fusion(f32[3072]{0:T(1024)S(1)} %bitcast.143, bf16[888,768]{1,0:T(8,128)(2,1)} %reshape.303, bf16[1,768,3072]{2,1,0:T(8,128)(2,1)} %param.20), kind=kOutput, calls=%fused_computation.8 | convolution fusion | flops 4370153472 | bytes 33374208 | tf_op jit(solution)/shard_map/dot_general | solution.py:24
  159.6 5.6 add_convert_fusion.1
  168.1 4.5 all-to-all-start.1
  172.5 19.8 %all-gather.2 = bf16[4,192,4]{1,2,0:T(4,128)(2,1)S(1)} all-gather(bf16[1,192,4]{1,2,0:T(4,128)(2,1)S(1)} %bitcast.151), channel_id=1, replica_groups=mesh['rep'=8,'exp'=4] {'exp'}, dimensions={0}, use_global_device_ids=true | all-gather | bytes 7680 | tf_op jit(solution)/shard_map/all_gather | solution.py:51
  200.8 10.6 %gather_fusion.2 = f32[788]{0:T(1024)S(1)} fusion(f32[394,4]{0,1:T(4,128)S(1)} %get-tuple-element.37, s32[788]{0:T(1024)S(1)} %reshape.337), kind=kCustom, calls=%fused_computation.2 | custom fusion | bytes 12608 | tf_op jit(solution)/shard_map/jit(take_along_axis)/gather | solution.py:82
  211.8 7.6 %scatter_custom_fusion.1 = bf16[888,768]{1,0:T(8,128)(2,1)S(1)} fusion(s32[788]{0:T(1024)} %copy-done.56, f32[394,768]{1,0:T(8,128)S(1)} %convert_element_type.219, f32[]{:T(128)} %constant.49.clone.1, f32[788]{0:T(1024)S(1)} %maximum_select_fusion, bf16[]{:T(256)} %constant.25.clone.1), kind=kCustom, calls=%fused_computation.94 | custom fusion | flops 1815552 | bytes 2578512 | tf_op jit(solution)/shard_map/scatter | solution.py:122
  220.8 19.4 %all_to_all.20 = bf16[4,222,768]{2,1,0:T(8,128)(2,1)S(1)} all-to-all(bf16[4,222,768]{2,1,0:T(8,128)(2,1)} %reshape.306), channel_id=1, replica_groups=mesh['rep'=8,'exp'=4] {'exp'}, dimensions={0} | all-to-all | bytes 2727936 | tf_op jit(solution)/shard_map/all_to_all | solution.py:125
  241.8 16.4 %fusion.86 = (bf16[3072]{0:T(1024)(128)(2,1)S(1)}, bf16[888,3072]{1,0:T(8,128)(2,1)}) fusion(f32[888,3072]{1,0:T(8,128)} %get-tuple-element.41, bf16[888,768]{1,0:T(8,128)(2,1)} %reshape.307, bf16[1,3072,768]{2,1,0:T(8,128)(2,1)} %param.22, f32[888,3072]{1,0:T(8,128)} %get-tuple-element.55, f32[3072]{0:T(1024)S(1)} %bitcast.144), kind=kOutput, calls=%fused_computation.177 | convolution fusion | flops 4233753600 | bytes 33380352 | tf_op jit(solution)/shard_map/dot_general | solution.py:24
  258.2 7.0 fusion.28
  272.0 11.6 %all-to-all-done.3 = bf16[4,222,768]{2,1,0:T(8,128)(2,1)S(1)} async-done(((bf16[4,222,768]{2,1,0:T(8,128)(2,1)}), bf16[4,222,768]{2,1,0:T(8,128)(2,1)S(1)}, u32[]{:S(2)}, u32[]{:S(2)}) %all-to-all-start.3) | async-done | bytes 1364000 | tf_op jit(solution)/shard_map/all_to_all | solution.py:138
  306.7 4.1 multiply_reduce_fusion
  325.0 4.1 convolution_convert_fusion
  334.0 5.5 fusion.73
  343.3 33.2 %reduce-scatter.24.cloned.1.call-done = bf16[192,2304]{1,0:T(8,128)(2,1)} async-done(((bf16[768,2304]{1,0:T(8,128)(2,1)}), bf16[192,2304]{1,0:T(8,128)(2,1)}) %reduce-scatter.24.cloned.1.call-update) | async-done | bytes 884752 | tf_op jit(solution)/shard_map/reduce_scatter | solution.py:208
  376.6 9.5 %fusion.14 = bf16[1,768,3072]{2,1,0:T(8,128)(2,1)} fusion(bf16[888,768]{1,0:T(8,128)(2,1)S(1)} %copy-done.24, bf16[888,3072]{1,0:T(8,128)(2,1)} %get-tuple-element.67), kind=kOutput, calls=%fused_computation.38 | convolution fusion | flops 4192468992 | bytes 11538432 | tf_op jit(solution)/shard_map/dot_general | solution.py:24
  386.1 20.4 %copy.183 = bf16[1,768,3072]{1,0,2:T(2,128)(2,1)} copy(bf16[1,768,3072]{2,1,0:T(8,128)(2,1)} %fusion.14) | data formatting | bytes 9437184
  406.4 6.7 copy.208
  414.5 9.8 %fusion.15 = bf16[1,3072,768]{2,1,0:T(8,128)(2,1)} fusion(bf16[888,3072]{1,0:T(8,128)(2,1)} %copy-done.60, bf16[888,768]{1,0:T(8,128)(2,1)S(1)} %copy-done.25), kind=kOutput, calls=%fused_computation.39 | convolution fusion | flops 4192468992 | bytes 11538432 | tf_op jit(solution)/shard_map/dot_general | solution.py:24
  425.4 11.3 %reduce-scatter.32.cloned.1.call-done = bf16[96,1]{1,0:T(8,128)(2,1)} async-done(((bf16[768,1]{1,0:T(8,128)(2,1)}), bf16[96,1]{1,0:T(8,128)(2,1)}) %reduce-scatter.32.cloned.1.call-update) | async-done | bytes 208
  438.0 31.2 %reduce-scatter.30.cloned.1.call-done = bf16[384,1]{1,0:T(8,128)(2,1)} async-done(((bf16[3072,1]{1,0:T(8,128)(2,1)}), bf16[384,1]{1,0:T(8,128)(2,1)}) %reduce-scatter.30.cloned.1.call-update) | async-done | bytes 784
  473.5 21.0 %reduce-scatter.36.cloned.1.call-done = bf16[192,2]{1,0:T(8,128)(2,1)} async-done(((bf16[768,2]{1,0:T(8,128)(2,1)}), bf16[192,2]{1,0:T(8,128)(2,1)}) %reduce-scatter.36.cloned.1.call-update) | async-done | bytes 784
  495.4 25.9 %reduce-scatter.38.cloned.1.call-done = bf16[192,5]{1,0:T(8,128)(2,1)} async-done(((bf16[768,5]{1,0:T(8,128)(2,1)}), bf16[192,5]{1,0:T(8,128)(2,1)}) %reduce-scatter.38.cloned.1.call-update) | async-done | bytes 1936
  522.1 16.3 %all-reduce.1 = (bf16[192,4]{0,1:T(4,128)(2,1)S(1)}, bf16[2,192]{1,0:T(2,128)(2,1)S(1)}, bf16[5,192]{1,0:T(8,128)(2,1)S(1)}) all-reduce(bf16[192,4]{0,1:T(4,128)(2,1)S(1)} %copy.190, bf16[2,192]{1,0:T(2,128)(2,1)S(1)} %copy.192, bf16[5,192]{1,0:T(8,128)(2,1)S(1)} %copy.194), channel_id=1, replica_groups=mesh['rep'=8,'exp'=4] {'rep'}, use_global_device_ids=true, to_apply=%region_25.26 | all-reduce | flops 2112 | bytes 8448 | tf_op jit(solution)/shard_map/psum | solution.py:203
  540.3 43.0 %all-reduce.5.cloned.1.call-done = (bf16[192,2304]{1,0:T(8,128)(2,1)}, bf16[192,768]{1,0:T(8,128)(2,1)}) async-done(((bf16[192,2304]{1,0:T(8,128)(2,1)}, bf16[192,768]{1,0:T(8,128)(2,1)}), (bf16[192,2304]{1,0:T(8,128)(2,1)}, bf16[192,768]{1,0:T(8,128)(2,1)})) %all-reduce.5.cloned.1.call-update) | async-done | bytes 1179664 | tf_op jit(solution)/shard_map/psum | solution.py:201
  587.5 52.0 %reduce-scatter.28.cloned.1.call-done = bf16[384,768]{1,0:T(8,128)(2,1)} async-done(((bf16[3072,768]{1,0:T(8,128)(2,1)}), bf16[384,768]{1,0:T(8,128)(2,1)}) %reduce-scatter.28.cloned.1.call-update) | async-done | bytes 589840
  644.0 51.0 %reduce-scatter.22.cloned.1.call-done = bf16[1,384,768]{2,1,0:T(8,128)(2,1)} async-done(((bf16[1,3072,768]{2,1,0:T(8,128)(2,1)}), bf16[1,384,768]{2,1,0:T(8,128)(2,1)}) %reduce-scatter.22.cloned.1.call-update) | async-done | bytes 589840 | tf_op jit(solution)/shard_map/reduce_scatter | solution.py:231
  (301 shorter events, 133.4 us)
Async XLA Ops:
  7.2 52.8 %copy-start.11 = (bf16[394,768]{1,0:T(8,128)(2,1)S(1)}, bf16[394,768]{1,0:T(8,128)(2,1)}, u32[]{:S(2)}) copy-start(bf16[394,768]{1,0:T(8,128)(2,1)} %param.12) | copy-start | bytes 1815556
  7.2 52.8 %all-gather.6.cloned.1.call-start = ((), (), s32[]{:S(2)}) async-start(), calls=%async_computation.13 | async-start | bytes 4423680 | tf_op jit(solution)/shard_map/all_gather | solution.py:49
  7.9 81.6 %all-gather.8.cloned.1.call-start = ((), (), s32[]{:S(2)}) async-start(), calls=%async_computation.14 | async-start | bytes 1474560 | tf_op jit(solution)/shard_map/all_gather | solution.py:50
  9.9 53.8 %copy-start.41 = (f32[394]{0:T(512)}, f32[394]{0:T(512)S(1)}, u32[]{:S(2)}) copy-start(f32[394]{0:T(512)S(1)} %broadcast_multiply_fusion.1) | copy-start | bytes 4732
  11.4 52.4 %copy-start.49 = (f32[394]{0:T(512)}, f32[394]{0:T(512)S(1)}, u32[]{:S(2)}) copy-start(f32[394]{0:T(512)S(1)} %fusion.65) | copy-start | bytes 4732
  21.6 42.1 %copy-start.33 = (f32[768]{0:T(1024)}, f32[768]{0:T(1024)S(1)}, u32[]{:S(2)}) copy-start(f32[768]{0:T(1024)S(1)} %get-tuple-element.24) | copy-start | bytes 9220
  21.6 70.3 %copy-start.37 = (f32[768]{0:T(1024)}, f32[768]{0:T(1024)S(1)}, u32[]{:S(2)}) copy-start(f32[768]{0:T(1024)S(1)} %get-tuple-element.23) | copy-start | bytes 9220
  24.1 68.8 %copy-start.56 = (s32[788]{0:T(1024)}, s32[788]{0:T(1024)S(1)}, u32[]{:S(2)}) copy-start(s32[788]{0:T(1024)S(1)} %get-tuple-element.26) | copy-start | bytes 9460
  32.5 31.2 %copy-start.54 = (f32[768]{0:T(1024)}, f32[768]{0:T(1024)S(1)}, u32[]{:S(2)}) copy-start(f32[768]{0:T(1024)S(1)} %get-tuple-element.22) | copy-start | bytes 9220
  93.0 99.9 %copy-start.9 = (bf16[394,768]{1,0:T(8,128)(2,1)}, bf16[394,768]{1,0:T(8,128)(2,1)S(1)}, u32[]{:S(2)}) copy-start(bf16[394,768]{1,0:T(8,128)(2,1)S(1)} %add_convert_fusion.3) | copy-start | bytes 1815556
  102.5 57.2 %slice-start.2 = ((s8[4718592]{0:T(1024)(128)(4,1)}), s8[524288]{0:T(1024)(128)(4,1)S(1)}, s32[]{:S(2)}) async-start(s8[4718592]{0:T(1024)(128)(4,1)} %bitcast.153), calls=%async_computation.27 | async-start | bytes 1048576
  102.5 21.1 %all-to-all-start = ((bf16[4,222,768]{2,1,0:T(8,128)(2,1)}), bf16[4,222,768]{2,1,0:T(8,128)(2,1)S(1)}, u32[]{:S(2)}, u32[]{:S(2)}) async-start(bf16[4,222,768]{2,1,0:T(8,128)(2,1)} %reshape.302), calls=%async_computation | async-start | bytes 2752512 | tf_op jit(solution)/shard_map/all_to_all | solution.py:104
  125.0 34.6 %slice-start.3 = ((s8[4718592]{0:T(1024)(128)(4,1)}), s8[4194304]{0:T(1024)(128)(4,1)S(1)}, s32[]{:S(2)}) async-start(s8[4718592]{0:T(1024)(128)(4,1)} %bitcast.153), calls=%async_computation.28 | async-start | bytes 8388608
  165.2 27.2 %copy-start.32 = (s32[394,2]{0,1:T(2,128)S(1)}, s32[394,2]{0,1:T(2,128)}, u32[]{:S(2)}) copy-start(s32[394,2]{0,1:T(2,128)} %param.13) | copy-start | bytes 9460
  165.2 27.5 %copy-start.18 = (bf16[394,768]{1,0:T(8,128)(2,1)S(1)}, bf16[394,768]{1,0:T(8,128)(2,1)}, u32[]{:S(2)}) copy-start(bf16[394,768]{1,0:T(8,128)(2,1)} %param.14) | copy-start | bytes 1815556
  168.1 24.8 %copy-start.51 = (s32[788]{0:T(1024)S(1)}, s32[788]{0:T(1024)}, u32[]{:S(2)}) copy-start(s32[788]{0:T(1024)} %get-tuple-element.25) | copy-start | bytes 9460
  168.1 25.2 %all-to-all-start.1 = ((bf16[4,222,768]{2,1,0:T(8,128)(2,1)}), bf16[4,222,768]{2,1,0:T(8,128)(2,1)}, u32[]{:S(2)}, u32[]{:S(2)}) async-start(bf16[4,222,768]{2,1,0:T(8,128)(2,1)} %reshape.304), calls=%async_computation.1 | async-start | bytes 2752512 | tf_op jit(solution)/shard_map/all_to_all | solution.py:109
  220.8 37.3 %slice-start.4 = ((s8[4718592]{0:T(1024)(128)(4,1)}), s8[524288]{0:T(1024)(128)(4,1)S(1)}, s32[]{:S(2)}) async-start(s8[4718592]{0:T(1024)(128)(4,1)} %bitcast.155), calls=%async_computation.29 | async-start | bytes 1048576
  266.6 17.0 %all-to-all-start.3 = ((bf16[4,222,768]{2,1,0:T(8,128)(2,1)}), bf16[4,222,768]{2,1,0:T(8,128)(2,1)S(1)}, u32[]{:S(2)}, u32[]{:S(2)}) async-start(bf16[4,222,768]{2,1,0:T(8,128)(2,1)} %reshape.308), calls=%async_computation.3 | async-start | bytes 2752512 | tf_op jit(solution)/shard_map/all_to_all | solution.py:138
  270.2 73.1 %reduce-scatter.26.cloned.1.call-start = ((), (), s32[]{:S(2)}) async-start(), calls=%async_computation.17 | async-start | bytes 1474560 | tf_op jit(solution)/shard_map/reduce_scatter | solution.py:211
  295.5 81.0 %reduce-scatter.24.cloned.1.call-start = ((), (), s32[]{:S(2)}) async-start(), calls=%async_computation.16 | async-start | bytes 4423680 | tf_op jit(solution)/shard_map/reduce_scatter | solution.py:208
  329.1 95.2 %reduce-scatter.34.cloned.1.call-start = ((), (), s32[]{:S(2)}) async-start(), calls=%async_computation.21 | async-start | bytes 245760
  331.3 105.5 %reduce-scatter.32.cloned.1.call-start = ((), (), s32[]{:S(2)}) async-start(), calls=%async_computation.20 | async-start | bytes 221184
  332.5 136.8 %reduce-scatter.30.cloned.1.call-start = ((), (), s32[]{:S(2)}) async-start(), calls=%async_computation.19 | async-start | bytes 884736
  333.9 160.6 %reduce-scatter.36.cloned.1.call-start = ((), (), s32[]{:S(2)}) async-start(), calls=%async_computation.22 | async-start | bytes 245760
  339.5 37.1 %copy-start.24 = (bf16[888,768]{1,0:T(8,128)(2,1)S(1)}, bf16[888,768]{1,0:T(8,128)(2,1)}, u32[]{:S(2)}) copy-start(bf16[888,768]{1,0:T(8,128)(2,1)} %reshape.303) | copy-start | bytes 4091908
  342.1 179.2 %reduce-scatter.38.cloned.1.call-start = ((), (), s32[]{:S(2)}) async-start(), calls=%async_computation.23 | async-start | bytes 245760
  343.2 240.0 %all-reduce.5.cloned.1.call-start = ((), (), s32[]{:S(2)}) async-start(), calls=%async_computation.24 | async-start | bytes 2359296 | tf_op jit(solution)/shard_map/psum | solution.py:201
  376.5 263.0 %reduce-scatter.28.cloned.1.call-start = ((), (), s32[]{:S(2)}) async-start(), calls=%async_computation.18 | async-start | bytes 5308416
  413.2 281.9 %reduce-scatter.22.cloned.1.call-start = ((), (), s32[]{:S(2)}) async-start(), calls=%async_computation.15 | async-start | bytes 5308416 | tf_op jit(solution)/shard_map/reduce_scatter | solution.py:231
  424.3 46.5 %copy-start.4 = (f32[394,768]{1,0:T(8,128)S(1)}, f32[394,768]{1,0:T(8,128)}, u32[]{:S(2)}) copy-start(f32[394,768]{1,0:T(8,128)} %copy-done.3) | copy-start | bytes 3631108
  424.3 46.5 %copy-start.20 = (bf16[394,768]{1,0:T(8,128)(2,1)S(1)}, bf16[394,768]{1,0:T(8,128)(2,1)}, u32[]{:S(2)}) copy-start(bf16[394,768]{1,0:T(8,128)(2,1)} %param.14) | copy-start | bytes 1815556
  (50 other events, 198.7 us)
Sparse Core Ops, SparseCore 0:
  9.9 50.0 all-gather.5
  61.8 27.7 all-gather.7
  295.7 28.5 reduce-scatter.25
  329.3 47.2 reduce-scatter.23
  379.7 23.9 reduce-scatter.33
  406.4 30.2 reduce-scatter.31
  439.7 29.5 reduce-scatter.29
  472.0 22.4 reduce-scatter.35
  497.3 23.9 reduce-scatter.37
  523.5 59.6 all-reduce.4
  585.6 53.9 reduce-scatter.27
  641.7 53.2 reduce-scatter.21
where the time goes:
time: 715 us; the launch traced here: 704 us
  waiting for transfers between devices  332 us (46%)
  local copies, waits for them, and re-layouts  116 us (16%)
  matrix products  112 us (16%)
  blocking collectives  73.3 us (10%)
  other arithmetic  43.2 us (6%)
  between operations  15.6 us (2%)
  starting transfers between devices  12.4 us (2%)
    unnamed x18, waiting for transfers between devices  143 us
    dot_general x15, matrix products, matmul(): return jnp.dot(first_op, second_op, preferred_element_type=jnp.float32)  99.7 us
    unnamed x152, local copies, waits for them, and re-layouts  53.9 us
    reduce_scatter x1, waiting for transfers between devices, on_device(): lax.psum_scatter(grad_w_second[None].astype(jnp.bfloat16), 'rep', scatter...  51 us
    psum x1, waiting for transfers between devices, on_device(): lax.psum(grad_qkv.astype(jnp.bfloat16), 'rep').astype(jnp.float32)  43 us
    reduce_scatter x1, waiting for transfers between devices, on_device(): lax.psum_scatter(summed[0].astype(jnp.bfloat16), 'exp', scatter_dimension...  33.2 us
    all_gather x1, waiting for transfers between devices, on_device(): lax.all_gather(attn_qkv, 'exp', axis=0, tiled=True)  27.5 us
    all_gather x1, blocking collectives, on_device(): lax.all_gather(router, 'exp', axis=0, tiled=True)  19.8 us
  transfers between devices with their start and end apart: 15, of which 12 were waited for; matrix products, arithmetic and copies ran while one was open for 20% of the time, Pallas kernels for 0%

commit v1 on v0

v1 whole, which is shorter than its diff:
```python
from functools import partial
import math

import jax
import jax.numpy as jnp
from jax import lax
from jax.experimental import pallas as pl
from jax.experimental.pallas import tpu as pltpu
from jax.sharding import PartitionSpec as P

HEAD_DIM = 64
SEQ = 197
EPS = 1e-06
BF = jnp.bfloat16
F32 = jnp.float32
MESH = pl.DeviceIdType.MESH


def up(value, step):
    return (value + step - 1) // step * step


def mm(a, b):
    return lax.dot_general(a, b, (((1,), (0,)), ((), ())), preferred_element_type=F32)


def mm_nt(a, b):
    return lax.dot_general(a, b, (((1,), (1,)), ((), ())), preferred_element_type=F32)


def mm_tn(a, b):
    return lax.dot_general(a, b, (((0,), (0,)), ((), ())), preferred_element_type=F32)


def iota(shape, dim):
    return lax.broadcasted_iota(jnp.int32, shape, dim)


def rows_at(index, size):
    return pl.ds(pl.multiple_of(index * size, size), size)


def normalize(values, gain, shift):
    center = values - jnp.mean(values, -1, keepdims=True)
    spread = jnp.mean(center * center, -1, keepdims=True)
    return center * lax.rsqrt(spread + EPS) * gain + shift


class Sizes:
    def __init__(self, mesh, tok_rows, width, ff):
        self.n_exp = mesh.shape["exp"]
        self.n_rep = mesh.shape["rep"]
        self.tok = tok_rows
        self.images = tok_rows // SEQ
        self.seq = up(SEQ, 16)
        self.rows = self.images * self.seq
        self.d = width
        self.ff = ff
        self.experts = self.n_exp
        self.cap = (18 * tok_rows + 8 * self.experts - 1) // (8 * self.experts)
        self.slots = up(self.cap, 16)
        self.all_slots = self.slots * self.experts
        self.shard = width // self.n_exp
        self.shard_pad = up(self.shard, 128)
        self.ep = up(self.experts, 8)
        self.small = up(8 + self.ep, 16)
        self.pairs = width // 128


def pad_matrix(sz):
    row = iota((sz.rows, sz.tok), 0)
    col = iota((sz.rows, sz.tok), 1)
    want = jnp.full((sz.rows, sz.tok), -1, jnp.int32)
    for image in range(sz.images):
        inside = (row >= image * sz.seq) & (row < image * sz.seq + SEQ)
        want = jnp.where(inside, row - image * (sz.seq - SEQ), want)
    return (want == col).astype(F32).astype(BF)


def front_kernel(
    sz,
    tok_ref,
    grad_ref,
    routes_ref,
    wq_shard,
    wp_shard,
    sm_shard,
    xr,
    gr,
    gater,
    qkv,
    pall,
    ctx,
    resid,
    second,
    normed,
    probs,
    wq,
    wp,
    smf,
    gpad,
    pmat,
    xs,
    gs,
    gates,
    smg,
    wq_sem,
    wp_sem,
    cq_sem,
    cp_sem,
    sm_sem,
    g_sem,
    x_sem,
    ga_sem,
):
    me_r = lax.axis_index("rep")
    me = lax.axis_index("exp")
    n = sz.n_exp
    core = lax.rem(me_r, 2)
    sibling = me_r + 1 - 2 * core

    barrier = pltpu.get_barrier_semaphore()
    for k in range(1, n):
        pl.semaphore_signal(
            barrier, inc=1, device_id=(me_r, lax.rem(me + k, n)), device_id_type=MESH
        )
    pl.semaphore_signal(barrier, inc=1, device_id=(sibling, me), device_id_type=MESH)
    pl.semaphore_wait(barrier, n)

    def to_peer(src, dst, sems, k):
        return pltpu.make_async_remote_copy(
            src_ref=src,
            dst_ref=dst,
            send_sem=sems.at[0, k],
            recv_sem=sems.at[1, k],
            device_id=(me_r, lax.rem(me + k, n)),
            device_id_type=MESH,
        )

    def to_sibling(ref, sems, k):
        return pltpu.make_async_remote_copy(
            src_ref=ref,
            dst_ref=ref,
            send_sem=sems.at[0, k],
            recv_sem=sems.at[1, k],
            device_id=(sibling, me),
            device_id_type=MESH,
        )

    hq, hp = 3 * sz.d // 2, sz.d // 2
    own = rows_at(me, sz.shard)
    half_q = pl.ds(pl.multiple_of(core * hq, 128), hq)
    half_p = pl.ds(pl.multiple_of(core * hp, 128), hp)
    other_q = pl.ds(pl.multiple_of((1 - core) * hq, 128), hq)
    other_p = pl.ds(pl.multiple_of((1 - core) * hp, 128), hp)

    smg[me] = sm_shard[...]
    for k in range(1, n):
        to_peer(sm_shard, smg.at[me], sm_sem, k).start()
    for k in range(1, n):
        to_peer(wq_shard.at[:, half_q], wq.at[own, half_q], wq_sem, k).start()
    for k in range(1, n):
        to_peer(wp_shard.at[:, half_p], wp.at[own, half_p], wp_sem, k).start()
    wq[own, :] = wq_shard[...]
    wp[own, :] = wp_shard[...]

    r1 = routes_ref[0:1, :]
    r2 = routes_ref[1:2, :]
    ids = iota((sz.ep, sz.rows), 0)
    oh1 = (r1 == ids).astype(F32)
    oh2 = (r2 == ids).astype(F32)
    before = (
        (iota((sz.rows, sz.rows), 0) < iota((sz.rows, sz.rows), 1))
        .astype(F32)
        .astype(BF)
    )
    pos1 = mm(oh1.astype(BF), before)
    pos2 = mm(oh2.astype(BF), before) + jnp.sum(oh1, 1, keepdims=True)
    place = oh1 * pos1 + oh2 * pos2
    kept = (oh1 + oh2 > 0.5) & (place < sz.cap - 0.5)
    slot = jnp.where(kept, place, -1.0).astype(jnp.int32)
    slot_ids = iota((sz.slots, sz.rows), 0)
    for e in range(sz.experts):
        pmat[e * sz.slots : (e + 1) * sz.slots, :] = (
            (slot_ids == slot[e : e + 1, :]).astype(F32).astype(BF)
        )

    spread = pad_matrix(sz)
    gpad[...] = mm(spread, grad_ref[...]).astype(BF)
    for e in range(sz.experts):
        block = slice(e * sz.slots, (e + 1) * sz.slots)
        gs[block, :] = mm(pmat[block, :], gpad[...]).astype(BF)
    slots_me = rows_at(me, sz.slots)
    for k in range(1, n):
        dst = rows_at(lax.rem(me + k, n), sz.slots)
        to_peer(gs.at[dst, :], gr.at[slots_me, :], g_sem, k).start()
    gr[slots_me, :] = gs[slots_me, :]

    x = mm(spread, tok_ref[...])
    for k in range(1, n):
        src = lax.rem(me + n - k, n)
        to_peer(sm_shard, smg.at[src], sm_sem, k).wait_recv()
    acc = jnp.zeros((sz.small, sz.d), F32)
    for j in range(n):
        r = iota((sz.shard_pad, sz.d), 0)
        c = iota((sz.shard_pad, sz.d), 1)
        pick = ((c == r + j * sz.shard) & (r < sz.shard)).astype(F32).astype(BF)
        acc = acc + mm(smg[j], pick)
    smf[...] = acc
    normed[...] = normalize(x, acc[0:1, :], acc[2:3, :]).astype(BF)

    for k in range(1, n):
        theirs = rows_at(lax.rem(me + n - k, n), sz.shard)
        part = wq.at[theirs, half_q]
        to_peer(wq_shard.at[:, half_q], part, wq_sem, k).wait_recv()
        to_sibling(part, cq_sem, k).start()
    for k in range(1, n):
        theirs = rows_at(lax.rem(me + n - k, n), sz.shard)
        to_sibling(wq.at[theirs, other_q], cq_sem, k).wait_recv()
    for j, bias_row in ((0, 3), (1, None), (2, 4)):
        cols = slice(j * sz.d, (j + 1) * sz.d)
        out = mm(normed[...], wq[:, cols])
        if bias_row is not None:
            out = out + smf[bias_row : bias_row + 1, :]
        qkv[:, cols] = out.astype(BF)

    scale = 1.0 / math.sqrt(HEAD_DIM)
    lane = iota((sz.seq, 128), 1)
    live = iota((sz.seq, sz.seq), 1) < SEQ

    def pair_step(pair, carry):
        for image in range(sz.images):
            rows = slice(image * sz.seq, (image + 1) * sz.seq)
            q2 = qkv[rows, pl.ds(pl.multiple_of(pair * 128, 128), 128)]
            k2 = qkv[rows, pl.ds(pl.multiple_of(sz.d + pair * 128, 128), 128)]
            v2 = qkv[rows, pl.ds(pl.multiple_of(2 * sz.d + pair * 128, 128), 128)]
            total = jnp.zeros((sz.seq, 128), F32)
            for half in range(2):
                mask = (lane >= half * 64) & (lane < half * 64 + 64)
                s = mm_nt(jnp.where(mask, q2, jnp.zeros_like(q2)), k2) * scale
                s = jnp.where(live, s, -1e30)
                e = jnp.exp(s - jnp.max(s, -1, keepdims=True))
                p = (e / jnp.sum(e, -1, keepdims=True)).astype(BF)
                pall[(image * sz.pairs + pair) * 2 + half] = p
                total = total + mm(p, jnp.where(mask, v2, jnp.zeros_like(v2)))
            ctx[rows, pl.ds(pl.multiple_of(pair * 128, 128), 128)] = total.astype(BF)
        return carry

    lax.fori_loop(0, sz.pairs, pair_step, 0)

    for k in range(1, n):
        theirs = rows_at(lax.rem(me + n - k, n), sz.shard)
        part = wp.at[theirs, half_p]
        to_peer(wp_shard.at[:, half_p], part, wp_sem, k).wait_recv()
        to_sibling(part, cp_sem, k).start()
    for k in range(1, n):
        theirs = rows_at(lax.rem(me + n - k, n), sz.shard)
        to_sibling(wp.at[theirs, other_p], cp_sem, k).wait_recv()
    res = (
        mm(spread, tok_ref[...])
        + mm(ctx[...], wp[...])
        + smf[5:6, :]
    )
    resid[...] = res
    low = normalize(res, smf[1:2, :], smf[6:7, :]).astype(BF)
    second[...] = low

    for e in range(sz.experts):
        block = slice(e * sz.slots, (e + 1) * sz.slots)
        xs[block, :] = mm(pmat[block, :], second[...]).astype(BF)
    for k in range(1, n):
        dst = rows_at(lax.rem(me + k, n), sz.slots)
        to_peer(xs.at[dst, :], xr.at[slots_me, :], x_sem, k).start()
    xr[slots_me, :] = xs[slots_me, :]

    small_low = smf[...].astype(BF)
    logit_rows = mm_nt(small_low, low)[8 : 8 + sz.ep, :]
    logit_rows = jnp.where(iota((sz.ep, sz.rows), 0) < sz.experts, logit_rows, -1e30)
    e_rows = jnp.exp(logit_rows - jnp.max(logit_rows, 0, keepdims=True))
    prob_rows = e_rows / jnp.sum(e_rows, 0, keepdims=True)
    hi = prob_rows.astype(BF)
    left = prob_rows - hi.astype(F32)
    mid = left.astype(BF)
    low3 = (left - mid.astype(F32)).astype(BF)
    for e in range(sz.experts):
        block = pmat[e * sz.slots : (e + 1) * sz.slots, :]
        gates[e] = mm_nt(hi, block) + mm_nt(mid, block) + mm_nt(low3, block)
    for k in range(1, n):
        to_peer(
            gates.at[lax.rem(me + k, n)], gater.at[me], ga_sem, k
        ).start()
    gater[me] = gates[me]
    logit_cols = mm_nt(low, small_low)
    col = iota((sz.rows, sz.small), 1)
    logit_cols = jnp.where((col >= 8) & (col < 8 + sz.experts), logit_cols, -1e30)
    e_cols = jnp.exp(logit_cols - jnp.max(logit_cols, 1, keepdims=True))
    probs[...] = e_cols / jnp.sum(e_cols, 1, keepdims=True)

    for k in range(1, n):
        src = lax.rem(me + n - k, n)
        dst = rows_at(lax.rem(me + k, n), sz.slots)
        theirs = rows_at(src, sz.slots)
        shard_rows = rows_at(src, sz.shard)
        to_peer(gs.at[dst, :], gr.at[theirs, :], g_sem, k).wait()
        to_peer(xs.at[dst, :], xr.at[theirs, :], x_sem, k).wait()
        to_peer(gates.at[lax.rem(me + k, n)], gater.at[src], ga_sem, k).wait()
        to_peer(sm_shard, smg.at[src], sm_sem, k).wait_send()
        to_peer(
            wq_shard.at[:, half_q], wq.at[shard_rows, half_q], wq_sem, k
        ).wait_send()
        to_peer(
            wp_shard.at[:, half_p], wp.at[shard_rows, half_p], wp_sem, k
        ).wait_send()
        to_sibling(wq.at[shard_rows, half_q], cq_sem, k).wait_send()
        to_sibling(wp.at[shard_rows, half_p], cp_sem, k).wait_send()


def front(sz, tokens, grad, routes, wq, wp, small):
    vmem = pl.BlockSpec(memory_space=pltpu.VMEM)
    rows, d, slots = sz.rows, sz.d, sz.all_slots
    outs = [
        ((slots, d), BF),
        ((slots, d), BF),
        ((sz.n_exp, sz.ep, sz.slots), F32),
        ((rows, 3 * d), BF),
        ((sz.images * sz.pairs * 2, sz.seq, sz.seq), BF),
        ((rows, d), BF),
        ((rows, d), F32),
        ((rows, d), BF),
        ((rows, d), BF),
        ((rows, sz.small), F32),
        ((d, 3 * d), BF),
        ((d, d), BF),
        ((sz.small, d), F32),
        ((rows, d), BF),
        ((slots, rows), BF),
    ]
    sems = pltpu.SemaphoreType.DMA((2, sz.n_exp))
    return pl.pallas_call(
        partial(front_kernel, sz),
        name="front",
        out_shape=[jax.ShapeDtypeStruct(s, t) for s, t in outs],
        in_specs=[vmem] * 6,
        out_specs=[vmem] * len(outs),
        scratch_shapes=[
            pltpu.VMEM((slots, d), BF),
            pltpu.VMEM((slots, d), BF),
            pltpu.VMEM((sz.n_exp, sz.ep, sz.slots), F32),
            pltpu.VMEM((sz.n_exp, sz.small, sz.shard_pad), BF),
        ]
        + [sems] * 8,
        compiler_params=pltpu.CompilerParams(
            collective_id=0, has_side_effects=True, vmem_limit_bytes=56 << 20
        ),
    )(tokens, grad, routes, wq, wp, small)


def on_device(
    mesh,
    tokens,
    routes,
    out_grad,
    attn_qkv,
    attn_out,
    router,
    norm_gains,
    dense_biases,
    expert_in,
    expert_in_bias,
    expert_out,
    expert_out_bias,
):
    sz = Sizes(mesh, tokens.shape[0], tokens.shape[1], expert_in.shape[2])
    d = sz.d
    scale = 1.0 / math.sqrt(HEAD_DIM)
    routes_pad = jnp.pad(
        routes.T.reshape(2, sz.images, SEQ),
        ((0, 6), (0, 0), (0, sz.seq - SEQ)),
        constant_values=-1,
    ).reshape(8, sz.rows)
    small = jnp.concatenate(
        [norm_gains, dense_biases, jnp.zeros((1, sz.shard), BF), router.T], 0
    )
    small = jnp.pad(
        small, ((0, sz.small - small.shape[0]), (0, sz.shard_pad - sz.shard))
    )
    (xr, gr, gater, qkv, pall, ctx, resid, second, normed, probs, wq, wp, smf, gpad, pmat) = front(
        sz, tokens, out_grad, routes_pad, attn_qkv, attn_out, small
    )
    me = lax.axis_index("exp")
    n = sz.n_exp
    gate_rows = lax.dynamic_index_in_dim(gater, me, 1, keepdims=False)
    d_res = (gate_rows.reshape(-1, 1) * gr.astype(F32)).astype(BF)
    w1, w2 = expert_in[0], expert_out[0]
    b1, b2 = expert_in_bias[0].astype(F32), expert_out_bias[0].astype(F32)
    hidden = mm(xr, w1) + b1
    act32, back = jax.vjp(partial(jax.nn.gelu, approximate=False), hidden)
    act = act32.astype(BF)
    result = (mm(act, w2) + b2).astype(BF)
    d_act = mm_nt(d_res, w2)
    d_hid = back(d_act)[0].astype(BF)
    gw2 = mm_tn(act, d_res)
    gb2 = jnp.sum(d_res.astype(F32), 0)
    gw1 = mm_tn(xr, d_hid)
    gb1 = jnp.sum(d_hid.astype(F32), 0)
    row_grad = mm_nt(d_hid, w1).astype(BF)
    ret = lax.all_to_all(result, "exp", split_axis=0, concat_axis=0, tiled=True)
    bck = lax.all_to_all(row_grad, "exp", split_axis=0, concat_axis=0, tiled=True)
    g32 = gpad.astype(F32)
    out = resid
    prob_grad = []
    p3 = probs[:, 8 : 8 + sz.experts]
    for e in range(sz.experts):
        blk = slice(e * sz.slots, (e + 1) * sz.slots)
        po = mm_tn(pmat[blk], ret[blk])
        out = out + p3[:, e : e + 1] * po
        prob_grad.append(jnp.sum(g32 * po, 1))
    pg = jnp.stack(prob_grad, 1)
    lg = (p3 * (pg - jnp.sum(pg * p3, 1, keepdims=True))).astype(BF)
    router_all = smf[8 : 8 + sz.experts].astype(BF)
    second_grad = mm_tn(pmat, bck) + mm(lg, router_all)
    g_router = mm_tn(second, lg)
    ln2 = jax.vjp(normalize, resid, smf[1], smf[6])[1](second_grad)
    resid_grad = g32 + ln2[0]
    pgd = resid_grad.astype(BF)
    gp = mm_tn(ctx, pgd)
    gbo = jnp.sum(pgd.astype(F32), 0)
    cg = mm_nt(pgd, wp).astype(BF)
    heads = d // HEAD_DIM
    four = (sz.images, sz.seq, heads, HEAD_DIM)
    q, k, v = (qkv[:, i * d : (i + 1) * d].reshape(four) for i in range(3))
    cg4 = cg.reshape(four)
    pa = pall.reshape(sz.images, heads, sz.seq, sz.seq)
    es = partial(jnp.einsum, preferred_element_type=F32)
    vg = es("ihst,ishd->ithd", pa, cg4).astype(BF)
    pb = es("ishd,ithd->ihst", cg4, v)
    p32 = pa.astype(F32)
    sg = (p32 * (pb - jnp.sum(pb * p32, -1, keepdims=True))).astype(BF)
    qg = (es("ihst,ithd->ishd", sg, k) * scale).astype(BF)
    kg = (es("ihst,ishd->ithd", sg, q) * scale).astype(BF)
    flat = lambda z: z.reshape(sz.rows, d)
    qkvg = jnp.concatenate([flat(qg), flat(kg), flat(vg)], 1)
    gq = mm_tn(normed, qkvg)
    ng = mm_nt(qkvg, wq)
    x = jnp.pad(tokens.astype(F32).reshape(sz.images, SEQ, d), ((0, 0), (0, sz.seq - SEQ), (0, 0))).reshape(sz.rows, d)
    ln1 = jax.vjp(normalize, x, smf[0], smf[2])[1](ng)
    gin = (resid_grad + ln1[0]).astype(BF)
    unpad = lambda z: z.reshape(sz.images, sz.seq, d)[:, :SEQ].reshape(sz.tok, d)
    gains = jnp.stack([ln1[1], ln2[1]])
    biases = jnp.stack([ln1[2], jnp.sum(flat(qg).astype(F32), 0), jnp.sum(flat(vg).astype(F32), 0), gbo, ln2[2]])
    smallg = jnp.concatenate([gains, biases, g_router.T], 0)
    def dense(z, dim):
        z = lax.psum(z.astype(BF), "rep")
        return lax.psum_scatter(z, "exp", scatter_dimension=dim, tiled=True).astype(F32)
    sg_out = dense(smallg, 1)
    def rsr(z, dim):
        return lax.psum_scatter(z[None].astype(BF), "rep", scatter_dimension=dim, tiled=True).astype(F32)
    return (
        unpad(out.astype(BF)), unpad(gin), dense(gq, 0), dense(gp, 0), sg_out[7:].T, sg_out[:2], sg_out[2:7],
        rsr(gw1, 2), rsr(gb1, 1), rsr(gw2, 1), rsr(gb2, 1),
    )


def solution(mesh):
    both = P(("rep", "exp"), None)
    rows = P("exp", None)
    cols = P(None, "exp")
    cube = P("exp", None, None)
    in_specs = (both, both, both, rows, rows, rows, cols, cols, cube, rows, cube, rows)
    out_specs = (
        both,
        both,
        rows,
        rows,
        rows,
        cols,
        cols,
        P("exp", None, "rep"),
        P("exp", "rep"),
        P("exp", "rep", None),
        P("exp", "rep"),
    )
    return jax.shard_map(
        partial(on_device, mesh),
        mesh=mesh,
        in_specs=in_specs,
        out_specs=out_specs,
        check_vma=False,
    )
```

time: 715 us -> 559 us (0.78)
  waiting for transfers between devices: 332 us -> 225 us
  Pallas kernels: 0 us -> 69 us
  blocking collectives: 73.3 us -> 16.5 us
  local copies, waits for them, and re-layouts: 116 us -> 80.7 us
  other arithmetic: 43.2 us -> 19.6 us
    pallas_call x0 -> x1, Pallas kernels: none -> 69 us  [front(): pl.pallas_call(partial(front_kernel, sz), name='front', out_shape=[jax.Sh...]
    unnamed x18 -> x12, waiting for transfers between devices: 143 us -> 89.7 us
    all_gather x3 -> x0, blocking collectives: 37.6 us -> none  [the longest x1 19.8 us: on_device(): lax.all_gather(router, 'exp', axis=0, tiled=True)]
    all_gather x2 -> x0, waiting for transfers between devices: 32.4 us -> none  [the longest x1 27.5 us: on_device(): lax.all_gather(attn_qkv, 'exp', axis=0, tiled=True)]
    all_to_all x3 -> x2, waiting for transfers between devices: 29 us -> 2.31 us  [the longest x1 2.3 us: on_device(): lax.all_to_all(row_grad, 'exp', split_axis=0, concat_axis=0, tiled=True)]
    all_to_all x1 -> x0, blocking collectives: 19.4 us -> none  [on_device(): lax.all_to_all(grad_buffer, 'exp', split_axis=0, concat_axis=0, tiled=True)]
    gather x7 -> x0, local copies, waits for them, and re-layouts: 18.9 us -> none  [the longest x5 11.1 us: on_device(): gates = jnp.take_along_axis(route_probs, routes, 1)]
    scatter x2 -> x0, other arithmetic: 15.6 us -> none  [the longest x1 8 us: on_device(): send_buffer = jnp.zeros((total_slots, model_width), jnp.bfloat16).at[slot...]
  transfers between devices with their start and end apart: 15 -> 10, of which waited for: 12 -> 7; matrix products, arithmetic and copies ran while one was open for 20% -> 28% of each run, Pallas kernels for 0% -> 0%
where the time goes in v1:
time: 559 us; the launch traced here: 554 us
  waiting for transfers between devices  225 us (40%)
  matrix products  117 us (21%)
  local copies, waits for them, and re-layouts  80.7 us (14%)
  Pallas kernels  69 us (12%)
  other arithmetic  19.6 us (4%)
  blocking collectives  16.5 us (3%)
  between operations  14.9 us (3%)
  starting transfers between devices  10.1 us (2%)
    unnamed x12, waiting for transfers between devices  89.7 us
    pallas_call x1, Pallas kernels, front(): pl.pallas_call(partial(front_kernel, sz), name='front', out_shape=[jax.Sh...  69 us
    reduce_scatter x1, waiting for transfers between devices, rsr(): lax.psum_scatter(z[None].astype(BF), 'rep', scatter_dimension=dim, tiled=...  51.2 us
    psum x1, waiting for transfers between devices, dense(): z = lax.psum(z.astype(BF), 'rep')  42.8 us
    unnamed x62, local copies, waits for them, and re-layouts  42.3 us
    dot_general x3, matrix products, mm(): lax.dot_general(a, b, (((1,), (0,)), ((), ())), preferred_element_type=F32)  40 us
    reduce_scatter x2, waiting for transfers between devices, dense(): lax.psum_scatter(z, 'exp', scatter_dimension=dim, tiled=True).astype(F32)  39.5 us
    dot_general x10, matrix products, mm_tn(): lax.dot_general(a, b, (((0,), (0,)), ((), ())), preferred_element_type=F32)  37.6 us
  transfers between devices with their start and end apart: 10, of which 7 were waited for; matrix products, arithmetic and copies ran while one was open for 28% of the time, Pallas kernels for 0%

profile of v1, /device:TPU:0, one launch (start us, length us, event | category | flops | bytes accessed | tf_op | source)
XLA Modules:
  0.0 553.6 jit_solution(16032779709871662348)
XLA Ops:
  11.5 69.0 %front.1 = (bf16[896,768]{1,0:T(8,128)(2,1)}, bf16[896,768]{1,0:T(8,128)(2,1)}, f32[4,8,224]{2,1,0:T(8,128)}, bf16[416,2304]{1,0:T(8,128)(2,1)}, bf16[24,208,208...) custom-call(bf16[394,768]{1,0:T(8,128)(2,1)} %tok_ref.1, ...), custom_call_target="tpu_custom_call" | custom-call | tf_op jit(solution)/shard_map/front/pallas_call | solution.py:339
  80.6 32.4 %multiply_convert_fusion = (bf16[896,3072]{1,0:T(8,128)(2,1)S(1)}, f32[896,3072]{1,0:T(8,128)}, f32[896,3072]{1,0:T(8,128)}) fusion(f32[3072]{0:T(1024)S(1)} %bitcast.122, bf16[896,768]{1,0:T(8,128)(2,1)} %get-tuple-element.29, bf16[1,768,3072]{2,1,0:T(8,128)(2,1)} %param.20), kind=kOutput, calls=%fused_computation.3 | convolution fusion | flops 4409524224 | bytes 33632256 | tf_op jit(solution)/shard_map/dot_general | solution.py:24
  113.0 5.5 add_convert_fusion.1
  118.6 4.7 all-to-all-start
  125.7 2.4 fusion.53
  130.1 3.1 copy.71
  133.2 3.1 reshape.221
  138.3 16.7 %fusion.56 = (bf16[3072]{0:T(1024)(128)(2,1)S(1)}, bf16[896,3072]{1,0:T(8,128)(2,1)}) fusion(f32[896,3072]{1,0:T(8,128)} %get-tuple-element.64, bf16[1,3072,768]{2,1,0:T(8,128)(2,1)} %param.22, bf16[896,768]{1,0:T(8,128)(2,1)} %get-tuple-element.32, f32[896]{0:T(1024)S(1)} %mul.226, f32[896,3072]{1,0:T(8,128)} %get-tuple-element.70, f32[3072]{0:T(1024)S(1)} %bitcast.123), kind=kOutput, calls=%fused_computation.124 | convolution fusion | flops 4273959936 | bytes 33641984 | tf_op jit(solution)/shard_map/dot_general | solution.py:28
  154.9 9.5 %fusion.22 = bf16[896,768]{1,0:T(8,128)(2,1)} fusion(bf16[896,3072]{1,0:T(8,128)(2,1)} %get-tuple-element.80, bf16[1,768,3072]{2,1,0:T(8,128)(2,1)} %param.20), kind=kOutput, calls=%fused_computation.44 | convolution fusion | flops 4228546560 | bytes 11599872 | tf_op jit(solution)/shard_map/dot_general | solution.py:28
  164.5 4.3 all-to-all-start.1
  173.7 3.5 fusion.28
  183.3 2.3 all-to-all-done.1
  185.6 3.7 multiply_reduce_fusion
  197.0 3.1 convolution_convert_fusion.3
  200.3 2.4 fusion.6
  207.9 3.2 reshape.207
  211.1 2.3 fusion.54
  215.2 3.2 reshape.205
  222.0 3.9 convolution_convert_fusion.2
  232.0 6.4 %fusion.48 = (bf16[768]{0:T(1024)(128)(2,1)S(1)}, f32[416]{0:T(512)S(1)}, bf16[768]{0:T(1024)(128)(2,1)S(1)}, f32[416,768]{1,0:T(8,128)}) fusion(f32[416,768]{1,0:T(8,128)} %bitcast_subtract_fusion, f32[768]{0:T(1024)S(1)} %get-tuple-element.55, f32[416]{0:T(512)S(1)} %rsqrt.21, f32[416]{0:T(512)S(1)} %div.45, bf16[2,197,768]{2,1,0:T(8,128)(2,1)S(1)} %reshape.209, ...), kind=kOutput, calls=%fused_computation.118 | convolution fusion | flops 1475074176 | bytes 8628096 | tf_op jit(solution)/shard_map/dot_general | solution.py:28
  240.0 39.4 %reduce-scatter.18.cloned.1.call-done = bf16[192,2304]{1,0:T(8,128)(2,1)} async-done(((bf16[768,2304]{1,0:T(8,128)(2,1)}), bf16[192,2304]{1,0:T(8,128)(2,1)}) %reduce-scatter.18.cloned.1.call-update) | async-done | bytes 884752 | tf_op jit(solution)/shard_map/reduce_scatter | solution.py:454
  279.5 9.0 %fusion.16 = bf16[1,768,3072]{2,1,0:T(8,128)(2,1)} fusion(bf16[896,768]{1,0:T(8,128)(2,1)} %get-tuple-element.29, bf16[896,3072]{1,0:T(8,128)(2,1)} %get-tuple-element.80), kind=kOutput, calls=%fused_computation.33 | convolution fusion | flops 4230217728 | bytes 11599872 | tf_op jit(solution)/shard_map/dot_general | solution.py:32
  288.4 20.4 %copy.93 = bf16[1,768,3072]{1,0,2:T(2,128)(2,1)} copy(bf16[1,768,3072]{2,1,0:T(8,128)(2,1)} %fusion.16) | data formatting | bytes 9437184
  308.8 6.7 %copy.115 = bf16[3072,1,768]{2,0,1:T(8,128)(2,1)} copy(bf16[3072,1,768]{2,1,0:T(2,128)(2,1)} %bitcast.110) | data formatting | bytes 9437184
  315.6 9.8 %fusion.17 = bf16[1,3072,768]{2,1,0:T(8,128)(2,1)} fusion(bf16[896,3072]{1,0:T(8,128)(2,1)} %copy-done.24, bf16[896,768]{1,0:T(8,128)(2,1)S(1)} %copy-done.14, f32[896]{0:T(1024)S(1)} %mul.226), kind=kOutput, calls=%fused_computation.34 | convolution fusion | flops 4232282112 | bytes 11603456 | tf_op jit(solution)/shard_map/dot_general | solution.py:32
  326.9 18.1 %reduce-scatter.24.cloned.1.call-done = bf16[384,1]{1,0:T(8,128)(2,1)} async-done(((bf16[3072,1]{1,0:T(8,128)(2,1)}), bf16[384,1]{1,0:T(8,128)(2,1)}) %reduce-scatter.24.cloned.1.call-update) | async-done | bytes 784
  351.9 18.5 %reduce-scatter.28.cloned.1.call-done = bf16[192,11]{1,0:T(8,128)(2,1)} async-done(((bf16[768,11]{1,0:T(8,128)(2,1)}), bf16[192,11]{1,0:T(8,128)(2,1)}) %reduce-scatter.28.cloned.1.call-update) | async-done | bytes 4240
  371.3 16.5 %psum.26 = bf16[11,192]{1,0:T(8,128)(2,1)S(1)} all-reduce(bf16[11,192]{1,0:T(8,128)(2,1)S(1)} %copy.100), channel_id=1, replica_groups=mesh['rep'=8,'exp'=4] {'rep'}, use_global_device_ids=true, to_apply=%region_25.26 | all-reduce | flops 2112 | bytes 8448 | tf_op jit(solution)/shard_map/psum | solution.py:453
  389.6 42.8 %all-reduce.6.cloned.1.call-done = (bf16[192,2304]{1,0:T(8,128)(2,1)}, bf16[192,768]{1,0:T(8,128)(2,1)}) async-done(((bf16[192,2304]{1,0:T(8,128)(2,1)}, bf16[192,768]{1,0:T(8,128)(2,1)}), (bf16[192,2304]{1,0:T(8,128)(2,1)}, bf16[192,768]{1,0:T(8,128)(2,1)})) %all-reduce.6.cloned.1.call-update) | async-done | bytes 1179664 | tf_op jit(solution)/shard_map/psum | solution.py:453
  432.4 2.5 convert_element_type.168
  435.8 52.9 %reduce-scatter.22.cloned.1.call-done = bf16[384,768]{1,0:T(8,128)(2,1)} async-done(((bf16[3072,768]{1,0:T(8,128)(2,1)}), bf16[384,768]{1,0:T(8,128)(2,1)}) %reduce-scatter.22.cloned.1.call-update) | async-done | bytes 589840
  493.2 51.2 %reduce-scatter.16.cloned.1.call-done = bf16[1,384,768]{2,1,0:T(8,128)(2,1)} async-done(((bf16[1,3072,768]{2,1,0:T(8,128)(2,1)}), bf16[1,384,768]{2,1,0:T(8,128)(2,1)}) %reduce-scatter.16.cloned.1.call-update) | async-done | bytes 589840 | tf_op jit(solution)/shard_map/reduce_scatter | solution.py:457
  (158 shorter events, 65.9 us)
Async XLA Ops:
  80.6 32.5 %copy-start.21 = (bf16[1,3072,768]{2,1,0:T(8,128)(2,1)S(1)}, bf16[1,3072,768]{2,1,0:T(8,128)(2,1)}, u32[]{:S(2)}) copy-start(bf16[1,3072,768]{2,1,0:T(8,128)(2,1)} %param.22) | copy-start | bytes 14155780
  113.0 5.5 copy-start.24
  118.6 4.7 copy-start.5
  118.6 5.3 copy-start.7
  118.6 45.9 %all-to-all-start = ((bf16[4,224,768]{2,1,0:T(8,128)(2,1)}), bf16[4,224,768]{2,1,0:T(8,128)(2,1)}, u32[]{:S(2)}, u32[]{:S(2)}) async-start(bf16[4,224,768]{2,1,0:T(8,128)(2,1)} %bitcast.115), calls=%async_computation | async-start | bytes 2752512 | tf_op jit(solution)/shard_map/all_to_all | solution.py:407
  164.5 21.1 %all-to-all-start.1 = ((bf16[4,224,768]{2,1,0:T(8,128)(2,1)}), bf16[4,224,768]{2,1,0:T(8,128)(2,1)}, u32[]{:S(2)}, u32[]{:S(2)}) async-start(bf16[4,224,768]{2,1,0:T(8,128)(2,1)} %bitcast.116), calls=%async_computation.1 | async-start | bytes 2752512 | tf_op jit(solution)/shard_map/all_to_all | solution.py:408
  168.8 71.2 %reduce-scatter.20.cloned.1.call-start = ((), (), s32[]{:S(2)}) async-start(), calls=%async_computation.11 | async-start | bytes 1474560 | tf_op jit(solution)/shard_map/reduce_scatter | solution.py:454
  169.2 3.1 copy-start.18
  169.2 4.5 copy-start.8
  169.2 4.5 copy-start.12
  185.6 3.8 copy-start.9
  189.3 2.7 copy-start.22
  200.1 79.3 %reduce-scatter.18.cloned.1.call-start = ((), (), s32[]{:S(2)}) async-start(), calls=%async_computation.10 | async-start | bytes 4423680 | tf_op jit(solution)/shard_map/reduce_scatter | solution.py:454
  202.7 2.5 copy-start.6
  203.8 1.5 copy-start
  206.2 4.9 copy-start.1
  213.5 4.9 copy-start.4
  219.1 1.3 copy-start.11
  219.1 1.4 copy-start.10
  220.3 1.7 copy-start.23
  220.5 1.4 copy-start.20
  225.9 1.3 copy-start.14
  225.9 4.0 copy-start.13
  225.9 99.5 %reduce-scatter.26.cloned.1.call-start = ((), (), s32[]{:S(2)}) async-start(), calls=%async_computation.14 | async-start | bytes 221184
  228.4 116.6 %reduce-scatter.24.cloned.1.call-start = ((), (), s32[]{:S(2)}) async-start(), calls=%async_computation.13 | async-start | bytes 884736
  229.9 140.6 %reduce-scatter.28.cloned.1.call-start = ((), (), s32[]{:S(2)}) async-start(), calls=%async_computation.15 | async-start | bytes 245760
  232.0 6.4 %copy-start.16 = (bf16[416,768]{1,0:T(8,128)(2,1)S(1)}, bf16[416,768]{1,0:T(8,128)(2,1)}, u32[]{:S(2)}) copy-start(bf16[416,768]{1,0:T(8,128)(2,1)} %get-tuple-element.40) | copy-start | bytes 1916932
  239.9 192.5 %all-reduce.6.cloned.1.call-start = ((), (), s32[]{:S(2)}) async-start(), calls=%async_computation.16 | async-start | bytes 2359296 | tf_op jit(solution)/shard_map/psum | solution.py:453
  279.4 209.3 %reduce-scatter.22.cloned.1.call-start = ((), (), s32[]{:S(2)}) async-start(), calls=%async_computation.12 | async-start | bytes 5308416
  315.6 228.8 %reduce-scatter.16.cloned.1.call-start = ((), (), s32[]{:S(2)}) async-start(), calls=%async_computation.9 | async-start | bytes 5308416 | tf_op jit(solution)/shard_map/reduce_scatter | solution.py:457
  325.4 23.0 %copy-start.3 = (f32[416,768]{1,0:T(8,128)S(1)}, f32[416,768]{1,0:T(8,128)}, u32[]{:S(2)}) copy-start(f32[416,768]{1,0:T(8,128)} %copy-done.2) | copy-start | bytes 3833860
  432.4 2.5 copy-start.19
  (3 other events, 3.0 us)
Sparse Core Ops, SparseCore 0:
  200.2 28.8 reduce-scatter.19
  232.1 47.2 reduce-scatter.17
  282.2 30.2 reduce-scatter.25
  315.3 29.6 reduce-scatter.23
  348.2 22.1 reduce-scatter.27
  372.7 59.6 all-reduce.5
  434.7 53.9 reduce-scatter.21
  491.0 53.2 reduce-scatter.15

commit v2 on v1

--- a/solution.py
+++ b/solution.py
@@ -65,6 +65,13 @@
         self.ep = up(self.experts, 8)
         self.small = up(8 + self.ep, 16)
         self.pairs = width // 128
+        self.nz = self.n_rep // 2
+        self.fs = ff // self.n_rep
+        self.fs_rows = self.fs + 16
+        self.blocks = 4
+        self.row_block = self.all_slots // self.blocks
+        self.part = 2 * self.shard // self.nz
+        self.scatter = self.part % 16 == 0
 
 
 def pad_matrix(sz):
@@ -86,8 +93,7 @@
     wp_shard,
     sm_shard,
     xr,
-    gr,
-    gater,
+    dres,
     qkv,
     pall,
     ctx,
@@ -99,7 +105,10 @@
     wp,
     smf,
     gpad,
+    comb,
     pmat,
+    gr,
+    gater,
     xs,
     gs,
     gates,
@@ -185,6 +194,12 @@
             (slot_ids == slot[e : e + 1, :]).astype(F32).astype(BF)
         )
 
+    eye = (iota((sz.rows, sz.rows), 0) == iota((sz.rows, sz.rows), 1)).astype(F32)
+    slot_cols = mm_nt(eye.astype(BF), slot.astype(F32).astype(BF)).astype(jnp.int32)
+    lane_ids = iota((sz.rows, sz.slots), 1)
+    for e in range(sz.experts):
+        comb[e] = (slot_cols[:, e : e + 1] == lane_ids).astype(F32).astype(BF)
+
     spread = pad_matrix(sz)
     gpad[...] = mm(spread, grad_ref[...]).astype(BF)
     for e in range(sz.experts):
@@ -241,7 +256,7 @@
                 s = jnp.where(live, s, -1e30)
                 e = jnp.exp(s - jnp.max(s, -1, keepdims=True))
                 p = (e / jnp.sum(e, -1, keepdims=True)).astype(BF)
-                pall[(image * sz.pairs + pair) * 2 + half] = p
+                pall[pair, image * 2 + half] = p
                 total = total + mm(p, jnp.where(mask, v2, jnp.zeros_like(v2)))
             ctx[rows, pl.ds(pl.multiple_of(pair * 128, 128), 128)] = total.astype(BF)
         return carry
@@ -300,10 +315,20 @@
         src = lax.rem(me + n - k, n)
         dst = rows_at(lax.rem(me + k, n), sz.slots)
         theirs = rows_at(src, sz.slots)
+        to_peer(gs.at[dst, :], gr.at[theirs, :], g_sem, k).wait()
+        to_peer(gates.at[lax.rem(me + k, n)], gater.at[src], ga_sem, k).wait()
+    square = iota((sz.slots, sz.slots), 0) == iota((sz.slots, sz.slots), 1)
+    for j in range(n):
+        block = slice(j * sz.slots, (j + 1) * sz.slots)
+        row = gater[j, pl.ds(me, 1), :]
+        gate = jnp.sum(jnp.where(square, row, 0.0), 1, keepdims=True)
+        dres[block, :] = (gate * gr[block, :].astype(F32)).astype(BF)
+    for k in range(1, n):
+        src = lax.rem(me + n - k, n)
+        dst = rows_at(lax.rem(me + k, n), sz.slots)
+        theirs = rows_at(src, sz.slots)
         shard_rows = rows_at(src, sz.shard)
-        to_peer(gs.at[dst, :], gr.at[theirs, :], g_sem, k).wait()
         to_peer(xs.at[dst, :], xr.at[theirs, :], x_sem, k).wait()
-        to_peer(gates.at[lax.rem(me + k, n)], gater.at[src], ga_sem, k).wait()
         to_peer(sm_shard, smg.at[src], sm_sem, k).wait_send()
         to_peer(
             wq_shard.at[:, half_q], wq.at[shard_rows, half_q], wq_sem, k
@@ -321,9 +346,8 @@
     outs = [
         ((slots, d), BF),
         ((slots, d), BF),
-        ((sz.n_exp, sz.ep, sz.slots), F32),
         ((rows, 3 * d), BF),
-        ((sz.images * sz.pairs * 2, sz.seq, sz.seq), BF),
+        ((sz.pairs, sz.images * 2, sz.seq, sz.seq), BF),
         ((rows, d), BF),
         ((rows, d), F32),
         ((rows, d), BF),
@@ -333,7 +357,7 @@
         ((d, d), BF),
         ((sz.small, d), F32),
         ((rows, d), BF),
-        ((slots, rows), BF),
+        ((sz.experts, rows, sz.slots), BF),
     ]
     sems = pltpu.SemaphoreType.DMA((2, sz.n_exp))
     return pl.pallas_call(
@@ -343,6 +367,9 @@
         in_specs=[vmem] * 6,
         out_specs=[vmem] * len(outs),
         scratch_shapes=[
+            pltpu.VMEM((slots, rows), BF),
+            pltpu.VMEM((slots, d), BF),
+            pltpu.VMEM((sz.n_exp, sz.ep, sz.slots), F32),
             pltpu.VMEM((slots, d), BF),
             pltpu.VMEM((slots, d), BF),
             pltpu.VMEM((sz.n_exp, sz.ep, sz.slots), F32),
@@ -353,6 +380,700 @@
             collective_id=0, has_side_effects=True, vmem_limit_bytes=56 << 20
         ),
     )(tokens, grad, routes, wq, wp, small)
+
+
+def unpad_matrix(sz):
+    row = iota((sz.tok, sz.rows), 0)
+    col = iota((sz.tok, sz.rows), 1)
+    want = row
+    for image in range(1, sz.images):
+        want = jnp.where(row >= image * SEQ, row + image * (sz.seq - SEQ), want)
+    return (want == col).astype(F32).astype(BF)
+
+
+def normalize_back(values, gain, cot):
+    center = values - jnp.mean(values, -1, keepdims=True)
+    spread = jnp.mean(center * center, -1, keepdims=True)
+    inv = lax.rsqrt(spread + EPS)
+    unit = center * inv
+    scaled = cot * gain
+    grad = inv * (
+        scaled
+        - jnp.mean(scaled, -1, keepdims=True)
+        - unit * jnp.mean(scaled * unit, -1, keepdims=True)
+    )
+    return grad, jnp.sum(cot * unit, 0, keepdims=True), jnp.sum(cot, 0, keepdims=True)
+
+
+def gelu_parts(h):
+    t = 1.0 / (1.0 + (0.3275911 / math.sqrt(2.0)) * jnp.abs(h))
+    bell = jnp.exp(-0.5 * h * h)
+    poly = t * (
+        0.127414796
+        + t * (-0.142248368 + t * (0.7107068705 + t * (-0.7265760135 + t * 0.5307027145)))
+    )
+    tail = poly * bell
+    return jnp.where(h >= 0, 1.0 - tail, tail), bell * (1.0 / math.sqrt(2.0 * math.pi))
+
+
+def rest_kernel(
+    sz,
+    xr,
+    dres,
+    qkv,
+    pall,
+    ctx,
+    resid,
+    second,
+    normed,
+    probs,
+    smf,
+    gpad,
+    comb,
+    tok_ref,
+    b1_ref,
+    b2_ref,
+    wq_hbm,
+    wp_hbm,
+    w1_hbm,
+    w2_hbm,
+    out_ref,
+    gin_ref,
+    o_w1,
+    o_w2,
+    o_dense,
+    o_small,
+    w1,
+    w2,
+    xt,
+    act,
+    dhid,
+    res_acc,
+    row_acc,
+    res_send,
+    row_send,
+    ret,
+    bck,
+    t1,
+    t2,
+    v1,
+    v2,
+    u1,
+    u2,
+    pbuf,
+    r1,
+    r2,
+    z1,
+    z2,
+    sm,
+    smr,
+    sme,
+    sme_r,
+    smz_r,
+    wsem,
+    psem,
+    t_sem,
+    u_sem,
+    ret_sem,
+    bck_sem,
+    d1_sem,
+    d2_sem,
+    z1_sem,
+    z2_sem,
+    z3_sem,
+    s1_sem,
+    s2_sem,
+    s3_sem,
+):
+    me_r = lax.axis_index("rep")
+    me = lax.axis_index("exp")
+    n, nz, fs, d = sz.n_exp, sz.nz, sz.fs, sz.d
+    core = lax.rem(me_r, 2)
+    z = lax.div(me_r, 2)
+    sibling = me_r + 1 - 2 * core
+
+    loads = []
+    for i, (src, dst) in enumerate(((w1_hbm, w1), (w2_hbm, w2))):
+        cp = pltpu.make_async_copy(src, dst, wsem.at[i])
+        cp.start()
+        loads.append(cp)
+
+    barrier = pltpu.get_barrier_semaphore()
+    for k in range(1, n):
+        pl.semaphore_signal(
+            barrier, inc=1, device_id=(me_r, lax.rem(me + k, n)), device_id_type=MESH
+        )
+    for k in range(1, nz):
+        pl.semaphore_signal(
+            barrier,
+            inc=1,
+            device_id=(lax.rem(me_r + 2 * k, 2 * nz), me),
+            device_id_type=MESH,
+        )
+    pl.semaphore_signal(barrier, inc=1, device_id=(sibling, me), device_id_type=MESH)
+    pl.semaphore_wait(barrier, n - 1 + nz)
+
+    def remote(src, dst, send, recv, rep, exp):
+        return pltpu.make_async_remote_copy(
+            src_ref=src,
+            dst_ref=dst,
+            send_sem=send,
+            recv_sem=recv,
+            device_id=(rep, exp),
+            device_id_type=MESH,
+        )
+
+    def to_peer(src, dst, sems, k):
+        return remote(
+            src, dst, sems.at[0, k], sems.at[1, k], me_r, lax.rem(me + k, n)
+        )
+
+    def to_z(src, dst, sems, k):
+        return remote(
+            src, dst, sems.at[0, k], sems.at[1, k], lax.rem(me_r + 2 * k, 2 * nz), me
+        )
+
+    cut = sz.d
+    xta = res_send.at[0:d, :]
+    xta[...] = xr[0:cut, :].T
+    xt[...] = xr[cut:, :].T
+    lower = 1 - lax.div(z, (nz + 1) // 2)
+    bias2 = jnp.sum(dres[...].astype(F32), 0, keepdims=True)
+    for cp in loads:
+        cp.wait()
+
+    def w1_part(f):
+        return w1[:, pl.ds(pl.multiple_of(f * fs, 128), fs)]
+
+    def compute(f):
+        w2f_rows = pl.ds(pl.multiple_of(f * fs, 16), fs)
+        bias = b1_ref[pl.ds(f, 1), :]
+        for b in range(sz.blocks):
+            rows = slice(b * sz.row_block, (b + 1) * sz.row_block)
+            h = mm(xr[rows, :], w1_part(f)) + bias
+            cdf, pdf = gelu_parts(h)
+            da = mm_nt(dres[rows, :], w2[w2f_rows, :])
+            a = (h * cdf).astype(BF)
+            dh = (da * (cdf + h * pdf)).astype(BF)
+            act[rows, :] = a
+            dhid[rows, :] = dh
+            res_acc[rows, :] += mm(a, w2[w2f_rows, :])
+            row_acc[rows, :] += mm_nt(dh, w1_part(f))
+
+    def grad1(rows):
+        part = mm(xta[rows, :], dhid[0:cut, :])
+        return part + mm(xt[rows, :], dhid[cut:, :])
+
+    def grad2(cols):
+        return mm_tn(act[:, cols], dres[...])
+
+    def extra():
+        gb = jnp.sum(dhid[...].astype(F32), 0, keepdims=True)
+        row = iota((16, d), 0)
+        wide = jnp.concatenate([gb, jnp.zeros((1, d - fs), F32)], 1)
+        return jnp.where(row == 0, wide, jnp.where(row == 1, bias2, 0.0))
+
+    def t_copies(dest):
+        return (
+            remote(t1, v1.at[dest], t_sem.at[0, 0, dest], t_sem.at[1, 0, dest], sibling, me),
+            remote(t2, v2.at[dest], t_sem.at[0, 1, dest], t_sem.at[1, 1, dest], sibling, me),
+        )
+
+    def landing(way, step, at):
+        if way == 0:
+            return nz - 2 - step + at
+        return at + step + 2 - nz if step < nz - 2 else nz
+
+    def u_copies(src1, src2, way, step, target, slot):
+        return (
+            remote(src1, u1.at[slot], u_sem.at[0, 0, way, step], u_sem.at[1, 0, way, step], target, me),
+            remote(src2, u2.at[slot], u_sem.at[0, 1, way, step], u_sem.at[1, 1, way, step], target, me),
+        )
+
+    res_acc[...] = jnp.zeros_like(res_acc)
+    row_acc[...] = jnp.zeros_like(row_acc)
+
+    parts1 = [slice(i, i + d // 2) for i in (0, d // 2)]
+    parts2 = [slice(i, i + 128) for i in range(0, fs, 128)]
+
+    def dest_of(i):
+        return lower * (nz - 1 - i) + (1 - lower) * i
+
+    def slice_step(i, carry):
+        dest = dest_of(i)
+
+        compute(dest * 2 + 1 - core)
+        for rows in parts1:
+            t1[rows, :] = grad1(rows).astype(BF)
+        for rows in parts2:
+            t2[rows, :] = grad2(rows).astype(BF)
+        t2[fs:, :] = extra().astype(BF)
+        for cp in t_copies(dest):
+            cp.start()
+        compute(dest * 2 + core)
+        for cp in t_copies(dest):
+            cp.wait()
+        for rows in parts1:
+            v1[dest, rows, :] = (v1[dest, rows, :].astype(F32) + grad1(rows)).astype(BF)
+        for rows in parts2:
+            v2[dest, rows, :] = (v2[dest, rows, :].astype(F32) + grad2(rows)).astype(BF)
+        v2[dest, fs:, :] = (v2[dest, fs:, :].astype(F32) + extra()).astype(BF)
+
+        @pl.when((z == 0) & (i <= nz - 2))
+        def _():
+            for cp in u_copies(v1.at[dest], v2.at[dest], 0, i, me_r + 2, dest):
+                cp.start()
+
+        @pl.when((z == nz - 1) & (i < nz - 2))
+        def _():
+            for cp in u_copies(v1.at[dest], v2.at[dest], 1, i, me_r - 2, dest):
+                cp.start()
+
+        @pl.when((z == nz - 1) & (i == nz - 2))
+        def _():
+            for cp in u_copies(v1.at[dest], v2.at[dest], 1, i, me_r - 2, nz):
+                cp.start()
+
+        return carry
+
+    lax.fori_loop(0, nz, slice_step, 0)
+
+    row_send[...] = row_acc[...].astype(BF)
+    slots_me = rows_at(me, sz.slots)
+
+    def peer_slots(k):
+        return rows_at(lax.rem(me + k, n), sz.slots)
+
+    for k in range(1, n):
+        to_peer(row_send.at[peer_slots(k), :], bck.at[slots_me, :], bck_sem, k).start()
+    bck[slots_me, :] = row_send[slots_me, :]
+    res_send[...] = (res_acc[...] + b2_ref[...]).astype(BF)
+    for k in range(1, n):
+        to_peer(res_send.at[peer_slots(k), :], ret.at[slots_me, :], ret_sem, k).start()
+    ret[slots_me, :] = res_send[slots_me, :]
+    dense_loads = []
+    for i, (src, cols) in enumerate(((wq_hbm, slice(0, 3 * d)), (wp_hbm, slice(3 * d, 4 * d)))):
+        cp = pltpu.make_async_copy(src, w1.at[:, cols], wsem.at[i])
+        cp.start()
+        dense_loads.append(cp)
+
+    def z_round(s):
+        for way in range(2):
+            zz = z if way == 0 else nz - 1 - z
+            dest = nz - 1 - s + zz if way == 0 else z - (nz - 1 - s)
+            target = me_r + 2 if way == 0 else me_r - 2
+
+            @pl.when((zz >= 1) & (zz <= s))
+            def _():
+                here = landing(way, s - 1, z)
+                there = landing(way, s, z + 1 if way == 0 else z - 1)
+                a1, a2 = u1.at[here], u2.at[here]
+                for cp in u_copies(a1, a2, way, s - 1, target, here):
+                    cp.wait_recv()
+                u1[here] = (u1[here].astype(F32) + v1[dest].astype(F32)).astype(BF)
+                u2[here] = (u2[here].astype(F32) + v2[dest].astype(F32)).astype(BF)
+                for cp in u_copies(a1, a2, way, s, target, there):
+                    cp.start()
+
+    if nz > 2:
+        z_round(1)
+
+    for k in range(1, n):
+        theirs = rows_at(lax.rem(me + n - k, n), sz.slots)
+        to_peer(row_send.at[peer_slots(k), :], bck.at[theirs, :], bck_sem, k).wait()
+    for k in range(1, n):
+        theirs = rows_at(lax.rem(me + n - k, n), sz.slots)
+        to_peer(res_send.at[peer_slots(k), :], ret.at[theirs, :], ret_sem, k).wait()
+    mixed = res_acc.at[0 : sz.rows, :]
+    sgrad = res_acc.at[sz.rows : 2 * sz.rows, :]
+    mixed[...] = resid[...]
+    prob_grads = []
+    total = jnp.zeros((sz.rows, 1), F32)
+    for e in range(sz.experts):
+        block = slice(e * sz.slots, (e + 1) * sz.slots)
+        p = probs[:, 8 + e : 9 + e]
+        rows_out = mm(comb[e], ret[block, :])
+        mixed[...] += p * rows_out
+        pg = jnp.sum(gpad[...].astype(F32) * rows_out, 1, keepdims=True)
+        prob_grads.append(pg)
+        total = total + pg * p
+    out_ref[...] = mm(unpad_matrix(sz), mixed[...].astype(BF)).astype(BF)
+    lane = iota((sz.rows, sz.small), 1)
+    logit_grad = jnp.zeros((sz.rows, sz.small), F32)
+    for e in range(sz.experts):
+        logit_grad = jnp.where(lane == 8 + e, prob_grads[e] - total, logit_grad)
+    logit_low = (probs[...] * logit_grad).astype(BF)
+    sgrad[...] = mm(logit_low, smf[...].astype(BF))
+    for e in range(sz.experts):
+        sgrad[...] += mm(comb[e], bck[e * sz.slots : (e + 1) * sz.slots, :])
+    back2, gain2, shift2 = normalize_back(resid[...], smf[1:2, :], sgrad[...])
+    rgrad = row_acc.at[0 : sz.rows, :]
+    rgrad[...] = gpad[...].astype(F32) + back2
+    low = rgrad[...].astype(BF)
+    bias_out = jnp.sum(low.astype(F32), 0, keepdims=True)
+    dense = w2
+    dense[3 * d : 4 * d, :] = mm_tn(ctx[...], low).astype(BF)
+    for cp in dense_loads:
+        cp.wait()
+    dq_ref = res_send.at[0 : sz.rows, :]
+    dk_ref = res_send.at[sz.rows : 2 * sz.rows, :]
+    dv_ref = row_send.at[0 : sz.rows, :]
+    cgrad = row_send.at[sz.rows : 2 * sz.rows, :]
+    dqkv = (dq_ref, dk_ref, dv_ref)
+
+    def load_probs(pair):
+        slot = lax.rem(pair, 2)
+        return pltpu.make_async_copy(pall.at[pair], pbuf.at[slot], psem.at[slot])
+
+    cgrad[...] = mm_nt(low, w1[:, 3 * d : 4 * d]).astype(BF)
+    sm[...] = mm_tn(logit_low, second[...])
+
+    for s in range(2, nz - 1):
+        z_round(s)
+
+    scale = 1.0 / math.sqrt(HEAD_DIM)
+    half_lane = iota((sz.seq, 128), 1)
+    load_probs(0).start()
+
+    def pair_step(pair, carry):
+        load_probs(pair).wait()
+
+        @pl.when(pair + 1 < sz.pairs)
+        def _():
+            load_probs(pair + 1).start()
+
+        for image in range(sz.images):
+            rows = slice(image * sz.seq, (image + 1) * sz.seq)
+            at = [pl.ds(pl.multiple_of(j * d + pair * 128, 128), 128) for j in range(3)]
+            q2, k2, v2_ = (qkv[rows, at[j]] for j in range(3))
+            c2 = cgrad[rows, at[0]]
+            dq = jnp.zeros((sz.seq, 128), F32)
+            dk = jnp.zeros((sz.seq, 128), F32)
+            dv = jnp.zeros((sz.seq, 128), F32)
+            for half in range(2):
+                mask = (half_lane >= half * 64) & (half_lane < half * 64 + 64)
+                zero = jnp.zeros_like(q2)
+                ch = jnp.where(mask, c2, zero)
+                p = pbuf[lax.rem(pair, 2), image * 2 + half]
+                dv = dv + mm_tn(p, ch)
+                pb = mm_nt(ch, v2_)
+                p32 = p.astype(F32)
+                mix = jnp.sum(pb * p32, -1, keepdims=True)
+                ds = (p32 * (pb - mix)).astype(BF)
+                dq = dq + mm(ds, jnp.where(mask, k2, zero))
+                dk = dk + mm_tn(ds, jnp.where(mask, q2, zero))
+            dq_ref[rows, at[0]] = (dq * scale).astype(BF)
+            dk_ref[rows, at[0]] = (dk * scale).astype(BF)
+            dv_ref[rows, at[0]] = dv.astype(BF)
+        return carry
+
+    lax.fori_loop(0, sz.pairs, pair_step, 0)
+
+    for j in range(3):
+        cols = slice(j * d, (j + 1) * d)
+        dense[cols, :] = mm_tn(normed[...], dqkv[j][...]).astype(BF)
+    keep = pl.ds(pl.multiple_of(core * 2 * d, 16), 2 * d)
+    give = pl.ds(pl.multiple_of((1 - core) * 2 * d, 16), 2 * d)
+    first = remote(dense.at[give, :], r1, d1_sem.at[0], d1_sem.at[1], sibling, me)
+    first.start()
+
+    ngrad = mixed
+    ngrad[...] = mm_nt(dq_ref[...], w1[:, 0:d])
+    for j in range(1, 3):
+        ngrad[...] += mm_nt(dqkv[j][...], w1[:, j * d : (j + 1) * d])
+    x = mm(pad_matrix(sz), tok_ref[...])
+    back1, gain1, shift1 = normalize_back(x, smf[0:1, :], ngrad[...])
+    gin_ref[...] = mm(unpad_matrix(sz), (rgrad[...] + back1).astype(BF)).astype(BF)
+    bias_q = jnp.sum(dq_ref[...].astype(F32), 0, keepdims=True)
+    bias_v = jnp.sum(dv_ref[...].astype(F32), 0, keepdims=True)
+    row = iota((sz.small, d), 0)
+    small = sm[...]
+    for i, value in enumerate((gain1, gain2, shift1, bias_q, bias_v, bias_out, shift2)):
+        small = jnp.where(row == i, value, small)
+    sm[...] = small
+    smb = sme.at[n]
+    smb[...] = small.astype(BF)
+    s_first = remote(smb, smr, s1_sem.at[0], s1_sem.at[1], sibling, me)
+    s_first.start()
+
+    first.wait()
+    dense[keep, :] = (dense[keep, :].astype(F32) + r1[...].astype(F32)).astype(BF)
+
+    def block_rows(j, e):
+        return pl.ds(pl.multiple_of(core * 2 * d + j * d + e * sz.shard, 16), sz.shard)
+
+    def peer_blocks(k):
+        e = lax.rem(me + k, n)
+        return [
+            remote(
+                dense.at[block_rows(j, e), :],
+                r2.at[k - 1, pl.ds(j * sz.shard, sz.shard), :],
+                d2_sem.at[0, j, k],
+                d2_sem.at[1, j, k],
+                me_r,
+                e,
+            )
+            for j in range(2)
+        ]
+
+    for k in range(1, n):
+        for cp in peer_blocks(k):
+            cp.start()
+    s_first.wait()
+    chip_small = (sm[...] + smr[...].astype(F32)).astype(BF)
+    for e in range(n):
+        r = iota((sz.shard_pad, d), 0)
+        c = iota((sz.shard_pad, d), 1)
+        pick = ((c == r + e * sz.shard) & (r < sz.shard)).astype(F32).astype(BF)
+        sme[e, :, 0 : sz.shard_pad] = mm_nt(chip_small, pick).astype(BF)
+    for k in range(1, n):
+        to_peer(
+            sme.at[lax.rem(me + k, n), :, 0 : sz.shard_pad], sme_r.at[k], s2_sem, k
+        ).start()
+
+    def z_last(way, sums):
+        zz = z if way == 0 else nz - 1 - z
+        target = me_r + 2 if way == 0 else me_r - 2
+
+        @pl.when(zz >= 1)
+        def _():
+            here = landing(way, nz - 2, z)
+            for cp in u_copies(u1.at[here], u2.at[here], way, nz - 2, target, here):
+                cp.wait_recv()
+            v1[z] = (v1[z].astype(F32) + u1[here].astype(F32)).astype(BF)
+            v2[z] = (v2[z].astype(F32) + u2[here].astype(F32)).astype(BF)
+
+    z_last(0, None)
+    z_last(1, None)
+    stores = [
+        pltpu.make_async_copy(v1.at[z], o_w1, wsem.at[0]),
+        pltpu.make_async_copy(v2.at[z], o_w2, wsem.at[1]),
+    ]
+    for cp in stores:
+        cp.start()
+
+    for k in range(1, n):
+        for cp in peer_blocks(k):
+            cp.wait()
+    for j in range(2):
+        part = slice(j * sz.shard, (j + 1) * sz.shard)
+        acc = dense[block_rows(j, me), :].astype(F32)
+        for k in range(1, n):
+            acc = acc + r2[k - 1, part, :].astype(F32)
+        z1[part, :] = acc.astype(BF)
+    acc = sme[me, :, 0 : sz.shard_pad].astype(F32)
+    for k in range(1, n):
+        to_peer(
+            sme.at[lax.rem(me + k, n), :, 0 : sz.shard_pad], sme_r.at[k], s2_sem, k
+        ).wait()
+        acc = acc + sme_r[k].astype(F32)
+    smz_r[0] = acc.astype(BF)
+    for k in range(1, nz):
+        to_z(smz_r.at[0], smz_r.at[k], s3_sem, k).start()
+
+    half = pl.ds(pl.multiple_of(core * 2 * sz.shard, 16), 2 * sz.shard)
+    base = core * 2 * sz.shard
+    if sz.scatter:
+        part = sz.part
+
+        def part_rows(zi):
+            return pl.ds(pl.multiple_of(zi * part, 16), part)
+
+        def out_rows(zi):
+            return pl.ds(pl.multiple_of(base + zi * part, 16), part)
+
+        for k in range(1, nz):
+            to_z(z1.at[part_rows(lax.rem(z + k, nz)), :], z2.at[k - 1], z1_sem, k).start()
+        acc = z1[part_rows(z), :].astype(F32)
+        for k in range(1, nz):
+            to_z(z1.at[part_rows(lax.rem(z + k, nz)), :], z2.at[k - 1], z1_sem, k).wait()
+            acc = acc + z2[k - 1].astype(F32)
+        o_dense[out_rows(z), :] = acc.astype(BF)
+        for k in range(1, nz):
+            to_z(o_dense.at[out_rows(z), :], o_dense.at[out_rows(z), :], z2_sem, k).start()
+        for k in range(1, nz):
+            theirs = lax.rem(z + nz - k, nz)
+            to_z(o_dense.at[out_rows(theirs), :], o_dense.at[out_rows(theirs), :], z2_sem, k).wait()
+    else:
+        for k in range(1, nz):
+            to_z(z1, z2.at[k - 1], z1_sem, k).start()
+        acc = z1[...].astype(F32)
+        for k in range(1, nz):
+            to_z(z1, z2.at[k - 1], z1_sem, k).wait()
+            acc = acc + z2[k - 1].astype(F32)
+        o_dense[half, :] = acc.astype(BF)
+    last = remote(o_dense.at[half, :], o_dense.at[half, :], z3_sem.at[0], z3_sem.at[1], sibling, me)
+    last.start()
+    acc = smz_r[0].astype(F32)
+    for k in range(1, nz):
+        to_z(smz_r.at[0], smz_r.at[k], s3_sem, k).wait()
+        acc = acc + smz_r[k].astype(F32)
+    o_small[...] = acc
+    other = pl.ds(pl.multiple_of((1 - core) * 2 * sz.shard, 16), 2 * sz.shard)
+    last.wait_send()
+    remote(o_dense.at[other, :], o_dense.at[other, :], z3_sem.at[0], z3_sem.at[1], sibling, me).wait_recv()
+
+    for cp in stores:
+        cp.wait()
+    for s in range(nz - 1):
+        for way in range(2):
+            zz = z if way == 0 else nz - 1 - z
+            target = me_r + 2 if way == 0 else me_r - 2
+
+            @pl.when(zz <= s)
+            def _():
+                for cp in u_copies(v1.at[0], v2.at[0], way, s, target, 0):
+                    cp.wait_send()
+
+
+def rest(sz, state, tokens, b1, b2, wq, wp, w1, w2):
+    vmem = pl.BlockSpec(memory_space=pltpu.VMEM)
+    hbm = pl.BlockSpec(memory_space=pl.ANY)
+    rows, d, slots, fs, nz, n = sz.rows, sz.d, sz.all_slots, sz.fs, sz.nz, sz.n_exp
+    dma = pltpu.SemaphoreType.DMA
+    outs = [
+        ((sz.tok, d), BF),
+        ((sz.tok, d), BF),
+        ((d, fs), BF),
+        ((sz.fs_rows, d), BF),
+        ((4 * sz.shard, d), BF),
+        ((sz.small, sz.shard_pad), F32),
+    ]
+    scratch = [
+        pltpu.VMEM(w1.shape, BF),
+        pltpu.VMEM(w2.shape, BF),
+        pltpu.VMEM((d, slots - d), BF),
+        pltpu.VMEM((slots, fs), BF),
+        pltpu.VMEM((slots, fs), BF),
+        pltpu.VMEM((slots, d), F32),
+        pltpu.VMEM((slots, d), F32),
+        pltpu.VMEM((slots, d), BF),
+        pltpu.VMEM((slots, d), BF),
+        pltpu.VMEM((slots, d), BF),
+        pltpu.VMEM((slots, d), BF),
+        pltpu.VMEM((d, fs), BF),
+        pltpu.VMEM((sz.fs_rows, d), BF),
+        pltpu.VMEM((nz, d, fs), BF),
+        pltpu.VMEM((nz, sz.fs_rows, d), BF),
+        pltpu.VMEM((nz + 1, d, fs), BF),
+        pltpu.VMEM((nz + 1, sz.fs_rows, d), BF),
+        pltpu.VMEM((2, 2 * sz.images, sz.seq, sz.seq), BF),
+        pltpu.VMEM((2 * d, d), BF),
+        pltpu.VMEM((n - 1, 2 * sz.shard, d), BF),
+        pltpu.VMEM((2 * sz.shard, d), BF),
+        pltpu.VMEM((nz - 1, sz.part if sz.scatter else 2 * sz.shard, d), BF),
+        pltpu.VMEM((sz.small, d), F32),
+        pltpu.VMEM((sz.small, d), BF),
+        pltpu.VMEM((n + 1, sz.small, d), BF),
+        pltpu.VMEM((n, sz.small, sz.shard_pad), BF),
+        pltpu.VMEM((nz, sz.small, sz.shard_pad), BF),
+        dma((2,)),
+        dma((2,)),
+        dma((2, 2, nz)),
+        dma((2, 2, 2, nz - 1)),
+        dma((2, n)),
+        dma((2, n)),
+        dma((2,)),
+        dma((2, 2, n)),
+        dma((2, nz)),
+        dma((2, nz)),
+        dma((2,)),
+        dma((2,)),
+        dma((2, n)),
+        dma((2, nz)),
+    ]
+    return pl.pallas_call(
+        partial(rest_kernel, sz),
+        name="rest",
+        out_shape=[jax.ShapeDtypeStruct(s, t) for s, t in outs],
+        in_specs=[vmem] * 3 + [hbm] + [vmem] * (len(state) - 1) + [hbm] * 4,
+        out_specs=[vmem, vmem, hbm, hbm, vmem, vmem],
+        scratch_shapes=scratch,
+        compiler_params=pltpu.CompilerParams(
+            collective_id=1, has_side_effects=True, vmem_limit_bytes=62 << 20
+        ),
+    )(*state, tokens, b1, b2, wq, wp, w1, w2)
+
+
+def plain_rest(sz, state, tokens, w1, b1, w2, b2):
+    xr, dres, qkv, pall, ctx, resid, second, normed, probs, smf, gpad, comb, wq, wp = state
+    d, n = sz.d, sz.experts
+    scale = 1.0 / math.sqrt(HEAD_DIM)
+    h = mm(xr, w1) + b1
+    cdf, pdf = gelu_parts(h)
+    act = (h * cdf).astype(BF)
+    result = (mm(act, w2) + b2).astype(BF)
+    dhid = (mm_nt(dres, w2) * (cdf + h * pdf)).astype(BF)
+    row_grad = mm_nt(dhid, w1).astype(BF)
+    swap = partial(
+        lax.all_to_all, axis_name="exp", split_axis=0, concat_axis=0, tiled=True
+    )
+    ret = swap(result).reshape(n, sz.slots, d)
+    bck = swap(row_grad).reshape(n, sz.slots, d)
+    g32 = gpad.astype(F32)
+    p = probs[:, 8 : 8 + n]
+    picked = jnp.einsum("ets,esd->etd", comb, ret, preferred_element_type=F32)
+    mixed = resid + jnp.einsum("te,etd->td", p, picked, precision="highest")
+    pg = jnp.sum(g32[None] * picked, -1).T
+    lg = (p * (pg - jnp.sum(pg * p, 1, keepdims=True))).astype(BF)
+    sgrad = mm(lg, smf[8 : 8 + n].astype(BF))
+    sgrad = sgrad + jnp.einsum("ets,esd->td", comb, bck, preferred_element_type=F32)
+    back2, gain2, shift2 = normalize_back(resid, smf[1:2], sgrad)
+    rgrad = g32 + back2
+    low = rgrad.astype(BF)
+    cgrad = mm_nt(low, wp).astype(BF)
+    four = (sz.images, sz.seq, d // HEAD_DIM, HEAD_DIM)
+    q, k, v, c = (
+        a.reshape(four)
+        for a in (qkv[:, :d], qkv[:, d : 2 * d], qkv[:, 2 * d :], cgrad)
+    )
+    prob = pall.reshape(sz.pairs, sz.images, 2, sz.seq, sz.seq)
+    prob = prob.transpose(1, 0, 2, 3, 4).reshape(sz.images, -1, sz.seq, sz.seq)
+    product = partial(jnp.einsum, preferred_element_type=F32)
+    dv = product("ihst,ishd->ithd", prob, c).astype(BF)
+    pb = product("ishd,ithd->ihst", c, v)
+    p32 = prob.astype(F32)
+    ds = (p32 * (pb - jnp.sum(pb * p32, -1, keepdims=True))).astype(BF)
+    dq = (product("ihst,ithd->ishd", ds, k) * scale).astype(BF)
+    dk = (product("ihst,ishd->ithd", ds, q) * scale).astype(BF)
+    dqkv = jnp.concatenate([a.reshape(sz.rows, d) for a in (dq, dk, dv)], 1)
+    x = mm(pad_matrix(sz), tokens)
+    back1, gain1, shift1 = normalize_back(x, smf[0:1], mm_nt(dqkv, wq))
+    gin = (rgrad + back1).astype(BF)
+    sums = jnp.sum(dqkv.astype(F32), 0, keepdims=True)
+    small = jnp.concatenate(
+        [gain1, gain2, shift1, sums[:, :d], sums[:, 2 * d :]]
+        + [jnp.sum(low.astype(F32), 0, keepdims=True), shift2, mm_tn(lg, second)]
+    )
+
+    def dense(grad, dim):
+        total = lax.psum(grad.astype(BF), "rep")
+        total = lax.psum_scatter(total, "exp", scatter_dimension=dim, tiled=True)
+        return total.astype(F32)
+
+    def owned(grad, dim):
+        total = lax.psum_scatter(
+            grad[None].astype(BF), "rep", scatter_dimension=dim, tiled=True
+        )
+        return total.astype(F32)
+
+    def unpad(rows):
+        return rows.reshape(sz.images, sz.seq, d)[:, :SEQ].reshape(sz.tok, d)
+
+    sums = dense(small, 1)
+    return (
+        unpad(mixed.astype(BF)),
+        unpad(gin),
+        dense(mm_tn(normed, dqkv), 0),
+        dense(mm_tn(ctx, low), 0),
+        sums[7:].T,
+        sums[0:2],
+        sums[2:7],
+        owned(mm_tn(xr, dhid), 2),
+        owned(jnp.sum(dhid.astype(F32), 0), 1),
+        owned(mm_tn(act, dres), 1),
+        owned(jnp.sum(dres.astype(F32), 0), 1),
+    )
 
 
 def on_device(
@@ -371,8 +1092,7 @@
     expert_out_bias,
 ):
     sz = Sizes(mesh, tokens.shape[0], tokens.shape[1], expert_in.shape[2])
-    d = sz.d
-    scale = 1.0 / math.sqrt(HEAD_DIM)
+    d, fs = sz.d, sz.fs
     routes_pad = jnp.pad(
         routes.T.reshape(2, sz.images, SEQ),
         ((0, 6), (0, 0), (0, sz.seq - SEQ)),
@@ -384,80 +1104,43 @@
     small = jnp.pad(
         small, ((0, sz.small - small.shape[0]), (0, sz.shard_pad - sz.shard))
     )
-    (xr, gr, gater, qkv, pall, ctx, resid, second, normed, probs, wq, wp, smf, gpad, pmat) = front(
+    (xr, dres, qkv, pall, ctx, resid, second, normed, probs, wq, wp, smf, gpad, comb) = front(
         sz, tokens, out_grad, routes_pad, attn_qkv, attn_out, small
     )
-    me = lax.axis_index("exp")
-    n = sz.n_exp
-    gate_rows = lax.dynamic_index_in_dim(gater, me, 1, keepdims=False)
-    d_res = (gate_rows.reshape(-1, 1) * gr.astype(F32)).astype(BF)
     w1, w2 = expert_in[0], expert_out[0]
-    b1, b2 = expert_in_bias[0].astype(F32), expert_out_bias[0].astype(F32)
-    hidden = mm(xr, w1) + b1
-    act32, back = jax.vjp(partial(jax.nn.gelu, approximate=False), hidden)
-    act = act32.astype(BF)
-    result = (mm(act, w2) + b2).astype(BF)
-    d_act = mm_nt(d_res, w2)
-    d_hid = back(d_act)[0].astype(BF)
-    gw2 = mm_tn(act, d_res)
-    gb2 = jnp.sum(d_res.astype(F32), 0)
-    gw1 = mm_tn(xr, d_hid)
-    gb1 = jnp.sum(d_hid.astype(F32), 0)
-    row_grad = mm_nt(d_hid, w1).astype(BF)
-    ret = lax.all_to_all(result, "exp", split_axis=0, concat_axis=0, tiled=True)
-    bck = lax.all_to_all(row_grad, "exp", split_axis=0, concat_axis=0, tiled=True)
-    g32 = gpad.astype(F32)
-    out = resid
-    prob_grad = []
-    p3 = probs[:, 8 : 8 + sz.experts]
-    for e in range(sz.experts):
-        blk = slice(e * sz.slots, (e + 1) * sz.slots)
-        po = mm_tn(pmat[blk], ret[blk])
-        out = out + p3[:, e : e + 1] * po
-        prob_grad.append(jnp.sum(g32 * po, 1))
-    pg = jnp.stack(prob_grad, 1)
-    lg = (p3 * (pg - jnp.sum(pg * p3, 1, keepdims=True))).astype(BF)
-    router_all = smf[8 : 8 + sz.experts].astype(BF)
-    second_grad = mm_tn(pmat, bck) + mm(lg, router_all)
-    g_router = mm_tn(second, lg)
-    ln2 = jax.vjp(normalize, resid, smf[1], smf[6])[1](second_grad)
-    resid_grad = g32 + ln2[0]
-    pgd = resid_grad.astype(BF)
-    gp = mm_tn(ctx, pgd)
-    gbo = jnp.sum(pgd.astype(F32), 0)
-    cg = mm_nt(pgd, wp).astype(BF)
-    heads = d // HEAD_DIM
-    four = (sz.images, sz.seq, heads, HEAD_DIM)
-    q, k, v = (qkv[:, i * d : (i + 1) * d].reshape(four) for i in range(3))
-    cg4 = cg.reshape(four)
-    pa = pall.reshape(sz.images, heads, sz.seq, sz.seq)
-    es = partial(jnp.einsum, preferred_element_type=F32)
-    vg = es("ihst,ishd->ithd", pa, cg4).astype(BF)
-    pb = es("ishd,ithd->ihst", cg4, v)
-    p32 = pa.astype(F32)
-    sg = (p32 * (pb - jnp.sum(pb * p32, -1, keepdims=True))).astype(BF)
-    qg = (es("ihst,ithd->ishd", sg, k) * scale).astype(BF)
-    kg = (es("ihst,ishd->ithd", sg, q) * scale).astype(BF)
-    flat = lambda z: z.reshape(sz.rows, d)
-    qkvg = jnp.concatenate([flat(qg), flat(kg), flat(vg)], 1)
-    gq = mm_tn(normed, qkvg)
-    ng = mm_nt(qkvg, wq)
-    x = jnp.pad(tokens.astype(F32).reshape(sz.images, SEQ, d), ((0, 0), (0, sz.seq - SEQ), (0, 0))).reshape(sz.rows, d)
-    ln1 = jax.vjp(normalize, x, smf[0], smf[2])[1](ng)
-    gin = (resid_grad + ln1[0]).astype(BF)
-    unpad = lambda z: z.reshape(sz.images, sz.seq, d)[:, :SEQ].reshape(sz.tok, d)
-    gains = jnp.stack([ln1[1], ln2[1]])
-    biases = jnp.stack([ln1[2], jnp.sum(flat(qg).astype(F32), 0), jnp.sum(flat(vg).astype(F32), 0), gbo, ln2[2]])
-    smallg = jnp.concatenate([gains, biases, g_router.T], 0)
-    def dense(z, dim):
-        z = lax.psum(z.astype(BF), "rep")
-        return lax.psum_scatter(z, "exp", scatter_dimension=dim, tiled=True).astype(F32)
-    sg_out = dense(smallg, 1)
-    def rsr(z, dim):
-        return lax.psum_scatter(z[None].astype(BF), "rep", scatter_dimension=dim, tiled=True).astype(F32)
+    if fs % 128 or sz.all_slots % 128 or sz.all_slots <= d:
+        state = (xr, dres, qkv, pall, ctx, resid, second, normed, probs, smf, gpad, comb, wq, wp)
+        bias1, bias2 = expert_in_bias.astype(F32), expert_out_bias.astype(F32)
+        return plain_rest(sz, state, tokens, w1, bias1, w2, bias2)
+    b1 = expert_in_bias.astype(F32).reshape(sz.n_rep, fs)
+    out, gin, g1, g2, dense, sg = rest(
+        sz,
+        (xr, dres, qkv, pall, ctx, resid, second, normed, probs, smf, gpad, comb),
+        tokens,
+        b1,
+        expert_out_bias.astype(F32),
+        wq,
+        wp,
+        w1,
+        w2,
+    )
+    me_r = lax.axis_index("rep")
+    sh = sz.shard
+    dense = dense.astype(F32).reshape(4, sh, d)
+    g2 = g2.astype(F32)
+    own = d // sz.n_rep
     return (
-        unpad(out.astype(BF)), unpad(gin), dense(gq, 0), dense(gp, 0), sg_out[7:].T, sg_out[:2], sg_out[2:7],
-        rsr(gw1, 2), rsr(gb1, 1), rsr(gw2, 1), rsr(gb2, 1),
+        out,
+        gin,
+        jnp.concatenate([dense[0], dense[1], dense[2]], 1),
+        dense[3],
+        sg[8 : 8 + sz.experts, :sh].T,
+        sg[0:2, :sh],
+        sg[2:7, :sh],
+        g1[None].astype(F32),
+        g2[fs : fs + 1, : fs],
+        g2[None, : fs],
+        lax.dynamic_slice(g2, (fs + 1, me_r * own), (1, own)),
     )
 
 

time: 559 us -> 249 us (0.45)
  waiting for transfers between devices: 225 us -> 0 us
  Pallas kernels: 69 us -> 233 us
  matrix products: 117 us -> 0 us
  local copies, waits for them, and re-layouts: 80.7 us -> 10.7 us
  blocking collectives: 16.5 us -> 0 us
  other arithmetic: 19.6 us -> 3.9 us
  between operations: 14.9 us -> 0.72 us
  starting transfers between devices: 10.1 us -> 0 us
    pallas_call x0 -> x1, Pallas kernels: none -> 164 us  [rest(): pl.pallas_call(partial(rest_kernel, sz), name='rest', out_shape=[jax.Shap...]
    dot_general x21 -> x0, matrix products: 117 us -> none  [the longest x3 40 us: mm(): lax.dot_general(a, b, (((1,), (0,)), ((), ())), preferred_element_type=F32)]
    reduce_scatter x3 -> x0, waiting for transfers between devices: 90.6 us -> none  [the longest x1 51.2 us: rsr(): lax.psum_scatter(z[None].astype(BF), 'rep', scatter_dimension=dim, tiled=...]
    unnamed x12 -> x0, waiting for transfers between devices: 89.7 us -> none
    psum x1 -> x0, waiting for transfers between devices: 42.8 us -> none  [dense(): z = lax.psum(z.astype(BF), 'rep')]
    unnamed x62 -> x16, local copies, waits for them, and re-layouts: 42.3 us -> 1.67 us
    reshape x16 -> x1, local copies, waits for them, and re-layouts: 23.2 us -> 0.6 us  [on_device(): b1 = expert_in_bias.astype(F32).reshape(sz.n_rep, fs)]
    psum x1 -> x0, blocking collectives: 16.5 us -> none  [dense(): z = lax.psum(z.astype(BF), 'rep')]
  transfers between devices with their start and end apart: 10 -> 0, of which waited for: 7 -> 0; matrix products, arithmetic and copies ran while one was open for 28% -> 0% of each run, Pallas kernels for 0% -> 0%
where the time goes in v2:
time: 249 us; the launch traced here: 248 us
  Pallas kernels  233 us (94%)
  local copies, waits for them, and re-layouts  10.7 us (4%)
  other arithmetic  3.9 us (2%)
    pallas_call x1, Pallas kernels, rest(): pl.pallas_call(partial(rest_kernel, sz), name='rest', out_shape=[jax.Shap...  164 us
    pallas_call x1, Pallas kernels, front(): pl.pallas_call(partial(front_kernel, sz), name='front', out_shape=[jax.Sh...  69.2 us

profile of v2, /device:TPU:0, one launch (start us, length us, event | category | flops | bytes accessed | tf_op | source)
XLA Modules:
  0.0 248.1 jit_solution(9387672381129172444)
XLA Ops:
  0.6 0.0 copy-start.5
  0.7 0.0 copy-start.6
  0.7 0.8 reshape.44
  1.5 0.7 reshape.45.routes_ref
  2.1 0.1 pad.15.clone
  2.2 0.8 pad_maximum_fusion.1
  3.0 0.6 pad.9.sm_shard
  3.6 69.2 %front.1 = (bf16[896,768]{1,0:T(8,128)(2,1)}, bf16[896,768]{1,0:T(8,128)(2,1)}, bf16[416,2304]{1,0:T(8,128)(2,1)}, bf16[6,4,208,208]{3,2,1,0:T(8,128)(2,1)}, bf1...) custom-call(bf16[394,768]{1,0:T(8,128)(2,1)} %tok_ref.3, ...), custom_call_target="tpu_custom_call" | custom-call | tf_op jit(solution)/shard_map/front/pallas_call | solution.py:363
  72.8 0.0 copy-done.5
  72.8 0.6 reshape.49.b1_ref
  73.4 0.0 copy-done.6
  73.4 0.6 convert_element_type.18.b2_ref
  74.0 163.6 %rest.1 = (bf16[394,768]{1,0:T(8,128)(2,1)}, bf16[394,768]{1,0:T(8,128)(2,1)}, bf16[768,384]{1,0:T(8,128)(2,1)}, bf16[400,768]{1,0:T(8,128)(2,1)}, bf16[768,768]{1,0:T(8,128)(2,1)}, /*index=5*/f32[16,256]{1,0:T(8,128)}) custom-call(bf16[896,768]{1,0:T(8,128)(2,1)} %get-tuple-element.31.xr, bf16[896,768]{1,0:T(8,128)(2,1)} %get-tuple-element.32.dres, ...), custom_call_target="tpu_custom_call" | custom-call | tf_op jit(solution)/shard_map/rest/pallas_call | solution.py:985
  237.6 2.3 fusion
  239.9 0.0 copy-start
  239.9 1.3 pad_maximum_fusion
  241.2 0.0 copy-done
  241.2 0.1 convert_element_type.22
  241.3 0.0 copy-start.3
  241.3 1.1 slice_bitcast_fusion
  242.4 0.6 constant_dynamic-slice_fusion
  243.0 0.0 copy-done.3
  243.0 1.1 bitcast_convert_fusion
  244.1 0.0 copy-done.4
  244.1 0.6 slice.37
  244.7 0.6 slice_bitcast_fusion.1
  245.3 0.6 slice.36
  245.8 0.6 slice.44
  246.4 0.0 copy-done.2
  246.4 0.8 copy.25
  247.2 0.0 copy-done.1
  247.2 0.8 copy.26
  (5 shorter events, 0.1 us)
Async XLA Ops:
  0.6 72.1 %copy-start.5 = (bf16[1,3072]{1,0:T(2,128)(2,1)S(1)}, bf16[1,3072]{1,0:T(2,128)(2,1)}, u32[]{:S(2)}) copy-start(bf16[1,3072]{1,0:T(2,128)(2,1)} %param.21) | copy-start | bytes 18436
  0.7 72.8 %copy-start.6 = (bf16[1,768]{1,0:T(2,128)(2,1)S(1)}, bf16[1,768]{1,0:T(2,128)(2,1)}, u32[]{:S(2)}) copy-start(bf16[1,768]{1,0:T(2,128)(2,1)} %param.23) | copy-start | bytes 4612
  239.9 1.3 copy-start
  241.3 1.7 copy-start.3
  242.4 1.7 copy-start.4
  242.4 4.0 %copy-start.2 = (bf16[394,768]{1,0:T(8,128)(2,1)S(1)}, bf16[394,768]{1,0:T(8,128)(2,1)}, u32[]{:S(2)}) copy-start(bf16[394,768]{1,0:T(8,128)(2,1)} %get-tuple-element.66) | copy-start | bytes 1815556
  243.0 4.3 %copy-start.1 = (bf16[394,768]{1,0:T(8,128)(2,1)S(1)}, bf16[394,768]{1,0:T(8,128)(2,1)}, u32[]{:S(2)}) copy-start(bf16[394,768]{1,0:T(8,128)(2,1)} %get-tuple-element.67) | copy-start | bytes 1815556

commit v3 on v2

v3 whole, which is shorter than its diff:
```python
from functools import partial
import math

import jax
import jax.numpy as jnp
from jax import lax
from jax.experimental import pallas as pl
from jax.experimental.pallas import tpu as pltpu
from jax.sharding import PartitionSpec as P

HEAD_DIM = 64
SEQ = 197
EPS = 1e-06
BF = jnp.bfloat16
F32 = jnp.float32
MESH = pl.DeviceIdType.MESH


def up(value, step):
    return (value + step - 1) // step * step


def mm(a, b):
    return lax.dot_general(a, b, (((1,), (0,)), ((), ())), preferred_element_type=F32)


def mm_nt(a, b):
    return lax.dot_general(a, b, (((1,), (1,)), ((), ())), preferred_element_type=F32)


def mm_tn(a, b):
    return lax.dot_general(a, b, (((0,), (0,)), ((), ())), preferred_element_type=F32)


def iota(shape, dim):
    return lax.broadcasted_iota(jnp.int32, shape, dim)


def rows_at(index, size):
    return pl.ds(pl.multiple_of(index * size, size), size)


def normalize(values, gain, shift):
    center = values - jnp.mean(values, -1, keepdims=True)
    spread = jnp.mean(center * center, -1, keepdims=True)
    return center * lax.rsqrt(spread + EPS) * gain + shift


class Sizes:
    def __init__(self, mesh, tok_rows, width, ff):
        self.n_exp = mesh.shape["exp"]
        self.n_rep = mesh.shape["rep"]
        self.tok = tok_rows
        self.images = tok_rows // SEQ
        self.seq = up(SEQ, 16)
        self.rows = self.images * self.seq
        self.d = width
        self.ff = ff
        self.experts = self.n_exp
        self.cap = (18 * tok_rows + 8 * self.experts - 1) // (8 * self.experts)
        self.slots = up(self.cap, 16)
        self.all_slots = self.slots * self.experts
        self.shard = width // self.n_exp
        self.shard_pad = up(self.shard, 128)
        self.ep = up(self.experts, 8)
        self.small = up(8 + self.ep, 16)
        self.pairs = width // 128
        self.nz = self.n_rep // 2
        self.fs = ff // self.n_rep
        self.fs_rows = self.fs + 16
        self.part = self.shard // self.nz
        self.groups = self.pairs // 2
        self.chunks = self.groups + 1


def pad_matrix(sz):
    row = iota((sz.rows, sz.tok), 0)
    col = iota((sz.rows, sz.tok), 1)
    want = jnp.full((sz.rows, sz.tok), -1, jnp.int32)
    for image in range(sz.images):
        inside = (row >= image * sz.seq) & (row < image * sz.seq + SEQ)
        want = jnp.where(inside, row - image * (sz.seq - SEQ), want)
    return (want == col).astype(F32).astype(BF)


def unpad_matrix(sz):
    row = iota((sz.tok, sz.rows), 0)
    col = iota((sz.tok, sz.rows), 1)
    want = row
    for image in range(1, sz.images):
        want = jnp.where(row >= image * SEQ, row + image * (sz.seq - SEQ), want)
    return (want == col).astype(F32).astype(BF)


def front_kernel(
    sz,
    tok_ref,
    grad_ref,
    routes_ref,
    wq_shard,
    wp_shard,
    router_ref,
    gains_ref,
    biases_ref,
    xr,
    dres,
    qkv,
    pall,
    ctx_t,
    resid,
    second,
    normed_t,
    probs,
    wq,
    wp,
    smf,
    gpad,
    comb,
    ctx,
    normed,
    pmat,
    gr,
    gater,
    xs,
    gs,
    gates,
    routers,
    gains,
    biases,
    wq_sem,
    wp_sem,
    zq_sem,
    zp_sem,
    cq_sem,
    cp_sem,
    sm_sem,
    g_sem,
    x_sem,
    ga_sem,
):
    me_r = lax.axis_index("rep")
    me = lax.axis_index("exp")
    n = sz.n_exp
    core = lax.rem(me_r, 2)
    sibling = me_r + 1 - 2 * core
    odd = lax.rem(lax.div(me_r, 2), 2)
    partner = me_r + 2 - 4 * odd

    barrier = pltpu.get_barrier_semaphore()
    for k in range(1, n):
        pl.semaphore_signal(
            barrier, inc=1, device_id=(me_r, lax.rem(me + k, n)), device_id_type=MESH
        )
    for rep in (sibling, partner):
        pl.semaphore_signal(barrier, inc=1, device_id=(rep, me), device_id_type=MESH)
    pl.semaphore_wait(barrier, n + 1)

    def remote(src, dst, send, recv, rep, exp):
        return pltpu.make_async_remote_copy(
            src_ref=src,
            dst_ref=dst,
            send_sem=send,
            recv_sem=recv,
            device_id=(rep, exp),
            device_id_type=MESH,
        )

    def to_peer(src, dst, sems, k):
        return remote(
            src, dst, sems.at[0, k], sems.at[1, k], me_r, lax.rem(me + k, n)
        )

    class Gather:
        def __init__(self, shard, full, width, peer_sem, layer_sem, twin_sem):
            self.shard, self.full = shard, full
            self.piece = width // 6
            self.peer_sem, self.layer_sem, self.twin_sem = peer_sem, layer_sem, twin_sem

        def cols(self, side, first, count):
            start = side * 3 * self.piece + first * self.piece
            return pl.ds(pl.multiple_of(start, 128), count * self.piece)

        def rows(self, k):
            return rows_at(lax.rem(me + n - k, n), sz.shard)

        def peer(self, k):
            cols = self.cols(core, odd, 2)
            return to_peer(
                self.shard.at[:, cols],
                self.full.at[rows_at(me, sz.shard), cols],
                self.peer_sem,
                k,
            )

        def layer(self, k, mine=True):
            part = 2 * odd if mine else 2 - 2 * odd
            piece = self.full.at[self.rows(k), self.cols(core, part, 1)]
            sem = self.layer_sem
            return remote(piece, piece, sem.at[0, k], sem.at[1, k], partner, me)

        def twin(self, k, late, side):
            first, count = (2 - 2 * odd, 1) if late else (odd, 2)
            piece = self.full.at[self.rows(k), self.cols(side, first, count)]
            sem = self.twin_sem
            return remote(
                piece, piece, sem.at[0, late, k], sem.at[1, late, k], sibling, me
            )

        def start(self):
            for k in range(1, n):
                self.peer(k).start()
            self.full[rows_at(me, sz.shard), :] = self.shard[...]

        def forward(self):
            for k in range(1, n):
                self.peer(k).wait_recv()
                self.layer(k).start()
                self.twin(k, 0, core).start()

        def finish(self):
            for k in range(1, n):
                self.layer(k, False).wait_recv()
                self.twin(k, 1, core).start()
            for k in range(1, n):
                for late in range(2):
                    self.twin(k, late, 1 - core).wait_recv()

        def drain(self):
            for k in range(1, n):
                self.peer(k).wait_send()
                self.layer(k).wait_send()
                for late in range(2):
                    self.twin(k, late, core).wait_send()

    gather_q = Gather(wq_shard, wq, 3 * sz.d, wq_sem, zq_sem, cq_sem)
    gather_p = Gather(wp_shard, wp, sz.d, wp_sem, zp_sem, cp_sem)

    def small_sends(k):
        return [
            to_peer(src, dst.at[me], sm_sem.at[i], k)
            for i, (src, dst) in enumerate(
                ((gains_ref, gains), (biases_ref, biases), (router_ref, routers))
            )
        ]

    for k in range(1, n):
        for cp in small_sends(k):
            cp.start()
    gather_q.start()
    gains[me] = gains_ref[...]
    biases[me] = biases_ref[...]
    routers[me] = router_ref[...]

    choice = (routes_ref[...].astype(F32) + 1.0).astype(BF)
    lines = mm_nt(choice, pad_matrix(sz)).astype(jnp.int32) - 1
    ids = iota((sz.ep, sz.rows), 0)
    oh1 = (lines[0:1, :] == ids).astype(F32)
    oh2 = (lines[1:2, :] == ids).astype(F32)
    before = (
        (iota((sz.rows, sz.rows), 0) < iota((sz.rows, sz.rows), 1))
        .astype(F32)
        .astype(BF)
    )
    pos1 = mm(oh1.astype(BF), before)
    pos2 = mm(oh2.astype(BF), before) + jnp.sum(oh1, 1, keepdims=True)
    place = oh1 * pos1 + oh2 * pos2
    kept = (oh1 + oh2 > 0.5) & (place < sz.cap - 0.5)
    slot = jnp.where(kept, place, -1.0).astype(jnp.int32)
    slot_ids = iota((sz.slots, sz.rows), 0)
    for e in range(sz.experts):
        pmat[e * sz.slots : (e + 1) * sz.slots, :] = (
            (slot_ids == slot[e : e + 1, :]).astype(F32).astype(BF)
        )
    eye = (iota((sz.rows, sz.rows), 0) == iota((sz.rows, sz.rows), 1)).astype(F32)
    slot_cols = mm_nt(eye.astype(BF), slot.astype(F32).astype(BF)).astype(jnp.int32)
    lane_ids = iota((sz.rows, sz.slots), 1)
    for e in range(sz.experts):
        comb[e] = (slot_cols[:, e : e + 1] == lane_ids).astype(F32).astype(BF)

    spread = pad_matrix(sz)
    gpad[...] = mm(spread, grad_ref[...]).astype(BF)
    for e in range(sz.experts):
        block = slice(e * sz.slots, (e + 1) * sz.slots)
        gs[block, :] = mm(pmat[block, :], gpad[...]).astype(BF)
    slots_me = rows_at(me, sz.slots)
    gr[slots_me, :] = gs[slots_me, :]

    x = mm(spread, tok_ref[...])
    for k in range(1, n):
        for cp in small_sends(k):
            cp.wait_recv()
    smf[...] = jnp.zeros_like(smf)
    for j in range(n):
        r = iota((sz.shard, sz.d), 0)
        c = iota((sz.shard, sz.d), 1)
        pick = (c == r + j * sz.shard).astype(F32).astype(BF)
        smf[0:2, :] += mm(gains[j], pick)
        smf[2:7, :] += mm(biases[j], pick)
        smf[8 : 8 + sz.experts, :] += mm(routers[j], pick)
    normed[...] = normalize(x, smf[0:1, :], smf[2:3, :]).astype(BF)
    normed_t[...] = normed[...].T

    gather_q.forward()
    gather_p.start()
    gather_q.finish()
    for j, bias_row in ((0, 3), (1, None), (2, 4)):
        cols = slice(j * sz.d, (j + 1) * sz.d)
        out = mm(normed[...], wq[:, cols])
        if bias_row is not None:
            out = out + smf[bias_row : bias_row + 1, :]
        qkv[:, cols] = out.astype(BF)
    for k in range(1, n):
        dst = rows_at(lax.rem(me + k, n), sz.slots)
        to_peer(gs.at[dst, :], gr.at[slots_me, :], g_sem, k).start()

    scale = 1.0 / math.sqrt(HEAD_DIM)
    lane = iota((sz.seq, 128), 1)
    live = iota((sz.seq, sz.seq), 1) < SEQ

    def pair_step(pair, carry):
        for image in range(sz.images):
            rows = slice(image * sz.seq, (image + 1) * sz.seq)
            q2 = qkv[rows, pl.ds(pl.multiple_of(pair * 128, 128), 128)]
            k2 = qkv[rows, pl.ds(pl.multiple_of(sz.d + pair * 128, 128), 128)]
            v2 = qkv[rows, pl.ds(pl.multiple_of(2 * sz.d + pair * 128, 128), 128)]
            total = jnp.zeros((sz.seq, 128), F32)
            for half in range(2):
                mask = (lane >= half * 64) & (lane < half * 64 + 64)
                s = mm_nt(jnp.where(mask, q2, jnp.zeros_like(q2)), k2) * scale
                s = jnp.where(live, s, -1e30)
                e = jnp.exp(s - jnp.max(s, -1, keepdims=True))
                p = (e / jnp.sum(e, -1, keepdims=True)).astype(BF)
                pall[pair, image * 2 + half] = p
                total = total + mm(p, jnp.where(mask, v2, jnp.zeros_like(v2)))
            ctx[rows, pl.ds(pl.multiple_of(pair * 128, 128), 128)] = total.astype(BF)
        return carry

    lax.fori_loop(0, sz.pairs, pair_step, 0)

    gather_p.forward()
    gather_p.finish()
    res = (
        mm(spread, tok_ref[...])
        + mm(ctx[...], wp[...])
        + smf[5:6, :]
    )
    resid[...] = res
    low = normalize(res, smf[1:2, :], smf[6:7, :]).astype(BF)
    second[...] = low

    for e in range(sz.experts):
        block = slice(e * sz.slots, (e + 1) * sz.slots)
        xs[block, :] = mm(pmat[block, :], second[...]).astype(BF)
    for k in range(1, n):
        dst = rows_at(lax.rem(me + k, n), sz.slots)
        to_peer(xs.at[dst, :], xr.at[slots_me, :], x_sem, k).start()
    xr[slots_me, :] = xs[slots_me, :]

    small_low = smf[...].astype(BF)
    logit_rows = mm_nt(small_low, low)[8 : 8 + sz.ep, :]
    logit_rows = jnp.where(iota((sz.ep, sz.rows), 0) < sz.experts, logit_rows, -1e30)
    e_rows = jnp.exp(logit_rows - jnp.max(logit_rows, 0, keepdims=True))
    prob_rows = e_rows / jnp.sum(e_rows, 0, keepdims=True)
    hi = prob_rows.astype(BF)
    left = prob_rows - hi.astype(F32)
    mid = left.astype(BF)
    low3 = (left - mid.astype(F32)).astype(BF)
    for e in range(sz.experts):
        block = pmat[e * sz.slots : (e + 1) * sz.slots, :]
        gates[e] = mm_nt(hi, block) + mm_nt(mid, block) + mm_nt(low3, block)
    for k in range(1, n):
        to_peer(
            gates.at[lax.rem(me + k, n)], gater.at[me], ga_sem, k
        ).start()
    gater[me] = gates[me]
    logit_cols = mm_nt(low, small_low)
    col = iota((sz.rows, sz.small), 1)
    logit_cols = jnp.where((col >= 8) & (col < 8 + sz.experts), logit_cols, -1e30)
    e_cols = jnp.exp(logit_cols - jnp.max(logit_cols, 1, keepdims=True))
    probs[...] = e_cols / jnp.sum(e_cols, 1, keepdims=True)

    ctx_t[...] = ctx[...].T

    for k in range(1, n):
        src = lax.rem(me + n - k, n)
        dst = rows_at(lax.rem(me + k, n), sz.slots)
        theirs = rows_at(src, sz.slots)
        to_peer(gs.at[dst, :], gr.at[theirs, :], g_sem, k).wait()
        to_peer(gates.at[lax.rem(me + k, n)], gater.at[src], ga_sem, k).wait()
    square = iota((sz.slots, sz.slots), 0) == iota((sz.slots, sz.slots), 1)
    for j in range(n):
        block = slice(j * sz.slots, (j + 1) * sz.slots)
        row = gater[j, pl.ds(me, 1), :]
        gate = jnp.sum(jnp.where(square, row, 0.0), 1, keepdims=True)
        dres[block, :] = (gate * gr[block, :].astype(F32)).astype(BF)
    for k in range(1, n):
        src = lax.rem(me + n - k, n)
        dst = rows_at(lax.rem(me + k, n), sz.slots)
        theirs = rows_at(src, sz.slots)
        to_peer(xs.at[dst, :], xr.at[theirs, :], x_sem, k).wait()
        for cp in small_sends(k):
            cp.wait_send()
    gather_q.drain()
    gather_p.drain()


def front(sz, tokens, grad, routes, wq, wp, router, gains, biases):
    vmem = pl.BlockSpec(memory_space=pltpu.VMEM)
    rows, d, slots, n = sz.rows, sz.d, sz.all_slots, sz.n_exp
    outs = [
        ((slots, d), BF),
        ((slots, d), BF),
        ((rows, 3 * d), BF),
        ((sz.pairs, sz.images * 2, sz.seq, sz.seq), BF),
        ((d, rows), BF),
        ((rows, d), F32),
        ((rows, d), BF),
        ((d, rows), BF),
        ((rows, sz.small), F32),
        ((d, 3 * d), BF),
        ((d, d), BF),
        ((sz.small, d), F32),
        ((rows, d), BF),
        ((sz.experts, rows, sz.slots), BF),
    ]
    dma = pltpu.SemaphoreType.DMA
    sems = [dma((2, n))] * 4 + [dma((2, 2, n))] * 2 + [dma((3, 2, n))] + [dma((2, n))] * 3
    return pl.pallas_call(
        partial(front_kernel, sz),
        name="front",
        out_shape=[jax.ShapeDtypeStruct(s, t) for s, t in outs],
        in_specs=[vmem] * 8,
        out_specs=[vmem] * len(outs),
        scratch_shapes=[
            pltpu.VMEM((rows, d), BF),
            pltpu.VMEM((rows, d), BF),
            pltpu.VMEM((slots, rows), BF),
            pltpu.VMEM((slots, d), BF),
            pltpu.VMEM((n, sz.ep, sz.slots), F32),
            pltpu.VMEM((slots, d), BF),
            pltpu.VMEM((slots, d), BF),
            pltpu.VMEM((n, sz.ep, sz.slots), F32),
            pltpu.VMEM((n, *router.shape), BF),
            pltpu.VMEM((n, *gains.shape), BF),
            pltpu.VMEM((n, *biases.shape), BF),
        ]
        + sems,
        compiler_params=pltpu.CompilerParams(
            collective_id=0, has_side_effects=True, vmem_limit_bytes=56 << 20
        ),
    )(tokens, grad, routes, wq, wp, router, gains, biases)


def finish_kernel(sz, out, gin, g1, g2, dense, sg, *refs):
    o_out, o_gin, o_qkv, o_proj, o_router, o_gains, o_biases, o_w1, o_b1, o_w2, o_b2 = refs
    o_out[...] = out[...]
    o_gin[...] = gin[...]
    fs, sh = sz.fs, sz.shard
    o_w1[0] = g1[...].astype(F32)
    o_w2[0] = g2[0:fs, :].astype(F32)
    o_b1[...] = g2[fs : fs + 16, :].astype(F32)[0:1, 0:fs]
    own = o_b2.shape[1]
    first = lax.axis_index("rep") * own
    pick = iota((sz.d, own), 0) == iota((sz.d, own), 1) + first
    o_b2[...] = mm(g2[fs : fs + 16, :], pick.astype(F32).astype(BF))[1:2, :]
    o_proj[...] = dense[0].astype(F32)
    for g in range(sz.groups):
        for j in range(3):
            cols = slice(j * sz.d + g * 256, j * sz.d + (g + 1) * 256)
            o_qkv[:, cols] = dense[g + 1, :, j * 256 : (j + 1) * 256].astype(F32)
    o_router[...] = sg[8 : 8 + sz.experts, 0:sh]
    o_gains[...] = sg[0:2, 0:sh]
    o_biases[...] = sg[2:7, 0:sh]


def finish(sz, out, gin, g1, g2, dense, sg):
    vmem = pl.BlockSpec(memory_space=pltpu.VMEM)
    d, fs, sh = sz.d, sz.fs, sz.shard
    outs = [
        ((sz.tok, d), BF),
        ((sz.tok, d), BF),
        ((sh, 3 * d), F32),
        ((sh, d), F32),
        ((sz.experts, sh), F32),
        ((2, sh), F32),
        ((5, sh), F32),
        ((1, d, fs), F32),
        ((1, fs), F32),
        ((1, fs, d), F32),
        ((1, d // sz.n_rep), F32),
    ]
    grads = pl.pallas_call(
        partial(finish_kernel, sz),
        name="finish",
        out_shape=[jax.ShapeDtypeStruct(s, t) for s, t in outs],
        in_specs=[vmem] * 6,
        out_specs=[vmem] * len(outs),
        compiler_params=pltpu.CompilerParams(vmem_limit_bytes=62 << 20),
    )(out, gin, g1, g2, dense, sg)
    return (*grads[:4], grads[4].T, *grads[5:])


def normalize_back(values, gain, cot):
    center = values - jnp.mean(values, -1, keepdims=True)
    spread = jnp.mean(center * center, -1, keepdims=True)
    inv = lax.rsqrt(spread + EPS)
    unit = center * inv
    scaled = cot * gain
    grad = inv * (
        scaled
        - jnp.mean(scaled, -1, keepdims=True)
        - unit * jnp.mean(scaled * unit, -1, keepdims=True)
    )
    return grad, jnp.sum(cot * unit, 0, keepdims=True), jnp.sum(cot, 0, keepdims=True)


def gelu_parts(h):
    t = 1.0 / (1.0 + (0.3275911 / math.sqrt(2.0)) * jnp.abs(h))
    bell = jnp.exp(-0.5 * h * h)
    poly = t * (
        0.127414796
        + t * (-0.142248368 + t * (0.7107068705 + t * (-0.7265760135 + t * 0.5307027145)))
    )
    tail = poly * bell
    return jnp.where(h >= 0, 1.0 - tail, tail), bell * (1.0 / math.sqrt(2.0 * math.pi))


def block_kernel(
    sz,
    tok_ref,
    routes_ref,
    router_ref,
    gains_ref,
    biases_ref,
    b1_ref,
    b2_ref,
    grad_hbm,
    wq_shard,
    wp_shard,
    w1_hbm,
    w2_hbm,
    o_dense,
    o_small,
    o_out,
    o_gin,
    o_w1,
    o_w2,
    o_probs,
    o_save,
    dw,
    w2,
    stage,
    xr,
    dres,
    qkv,
    ctx_t,
    resid,
    second,
    normed_t,
    probs,
    smf,
    gpad,
    comb,
    gater,
    gates,
    routers,
    gains,
    biases,
    bias2,
    xt,
    act,
    dhid,
    res_acc,
    row_acc,
    res_send,
    row_send,
    ret,
    bck,
    qs,
    qr,
    t1,
    t2,
    v1,
    v2,
    u1,
    u2,
    pbuf,
    r1,
    r2,
    z1,
    z2,
    sm,
    smr,
    sme,
    sme_r,
    smz_r,
    wsem,
    psem,
    wq_sem,
    wp_sem,
    zq_sem,
    zp_sem,
    cq_sem,
    cp_sem,
    sm_sem,
    g_sem,
    x_sem,
    ga_sem,
    t_sem,
    u_sem,
    ret_sem,
    bck_sem,
    q_sem,
    d1_sem,
    d2_sem,
    z1_sem,
    z2_sem,
    z3_sem,
    s1_sem,
    s2_sem,
    s3_sem,
):
    me_r = lax.axis_index("rep")
    me = lax.axis_index("exp")
    n, nz, fs, d = sz.n_exp, sz.nz, sz.fs, sz.d
    core = lax.rem(me_r, 2)
    z = lax.div(me_r, 2)
    sibling = me_r + 1 - 2 * core
    odd = lax.rem(z, 2)
    partner = me_r + 2 - 4 * odd

    load_grad = pltpu.make_async_copy(grad_hbm, stage, wsem.at[0])
    load_grad.start()
    load_w2 = pltpu.make_async_copy(w2_hbm, w2, wsem.at[1])
    load_w2.start()

    barrier = pltpu.get_barrier_semaphore()
    for k in range(1, n):
        pl.semaphore_signal(
            barrier, inc=1, device_id=(me_r, lax.rem(me + k, n)), device_id_type=MESH
        )
    for k in range(1, nz):
        pl.semaphore_signal(
            barrier,
            inc=1,
            device_id=(lax.rem(me_r + 2 * k, 2 * nz), me),
            device_id_type=MESH,
        )
    pl.semaphore_signal(barrier, inc=1, device_id=(sibling, me), device_id_type=MESH)
    pl.semaphore_wait(barrier, n - 1 + nz)

    def remote(src, dst, send, recv, rep, exp):
        return pltpu.make_async_remote_copy(
            src_ref=src,
            dst_ref=dst,
            send_sem=send,
            recv_sem=recv,
            device_id=(rep, exp),
            device_id_type=MESH,
        )

    def to_peer(src, dst, sems, k):
        return remote(
            src, dst, sems.at[0, k], sems.at[1, k], me_r, lax.rem(me + k, n)
        )

    def to_z(src, dst, sems, k):
        return remote(
            src, dst, sems.at[0, k], sems.at[1, k], lax.rem(me_r + 2 * k, 2 * nz), me
        )

    normed = bck.at[0 : sz.rows, :]
    ctx = bck.at[sz.rows : 2 * sz.rows, :]
    xs, gs = res_send, row_send

    class Gather:
        def __init__(self, shard, base, width, own_sem, peer_sem, layer_sem, twin_sem):
            self.shard = shard
            self.base, self.width = base, width
            self.piece = width // 6
            self.own_sem = own_sem
            self.peer_sem, self.layer_sem, self.twin_sem = peer_sem, layer_sem, twin_sem

        def cols(self, side, first, count, base=0):
            start = base + side * 3 * self.piece + first * self.piece
            return pl.ds(pl.multiple_of(start, 128), count * self.piece)

        def own(self):
            return pltpu.make_async_copy(
                self.shard,
                dw.at[rows_at(me, sz.shard), self.base : self.base + self.width],
                self.own_sem,
            )

        def save(self):
            cols = slice(self.base, self.base + self.width)
            return pltpu.make_async_copy(dw.at[:, cols], o_save.at[:, cols], self.own_sem)

        def rows(self, k):
            return rows_at(lax.rem(me + n - k, n), sz.shard)

        def peer(self, k):
            return to_peer(
                self.shard.at[:, self.cols(core, odd, 2)],
                dw.at[rows_at(me, sz.shard), self.cols(core, odd, 2, self.base)],
                self.peer_sem,
                k,
            )

        def layer(self, k, mine=True):
            part = 2 * odd if mine else 2 - 2 * odd
            piece = dw.at[self.rows(k), self.cols(core, part, 1, self.base)]
            sem = self.layer_sem
            return remote(piece, piece, sem.at[0, k], sem.at[1, k], partner, me)

        def twin(self, k, late, side):
            first, count = (2 - 2 * odd, 1) if late else (odd, 2)
            piece = dw.at[self.rows(k), self.cols(side, first, count, self.base)]
            sem = self.twin_sem
            return remote(
                piece, piece, sem.at[0, late, k], sem.at[1, late, k], sibling, me
            )

        def start(self):
            for k in range(1, n):
                self.peer(k).start()
            self.own().start()

        def forward(self):
            for k in range(1, n):
                self.peer(k).wait_recv()
                self.layer(k).start()
                self.twin(k, 0, core).start()

        def finish(self):
            self.own().wait()
            for k in range(1, n):
                self.layer(k, False).wait_recv()
                self.twin(k, 1, core).start()
            for k in range(1, n):
                for late in range(2):
                    self.twin(k, late, 1 - core).wait_recv()

        def drain(self):
            for k in range(1, n):
                self.peer(k).wait_send()
                self.layer(k).wait_send()
                for late in range(2):
                    self.twin(k, late, core).wait_send()

    gather_q = Gather(wq_shard, 0, 3 * d, wsem.at[2], wq_sem, zq_sem, cq_sem)
    gather_p = Gather(wp_shard, 3 * d, d, wsem.at[3], wp_sem, zp_sem, cp_sem)

    def small_sends(k):
        return [
            to_peer(src, dst.at[me], sm_sem.at[i], k)
            for i, (src, dst) in enumerate(
                ((gains_ref, gains), (biases_ref, biases), (router_ref, routers))
            )
        ]

    for k in range(1, n):
        for cp in small_sends(k):
            cp.start()
    gather_q.start()
    gains[me] = gains_ref[...]
    biases[me] = biases_ref[...]
    routers[me] = router_ref[...]

    choice = (routes_ref[...].astype(F32) + 1.0).astype(BF)
    lines = mm_nt(choice, pad_matrix(sz)).astype(jnp.int32) - 1
    ids = iota((sz.ep, sz.rows), 0)
    oh1 = (lines[0:1, :] == ids).astype(F32)
    oh2 = (lines[1:2, :] == ids).astype(F32)
    before = (
        (iota((sz.rows, sz.rows), 0) < iota((sz.rows, sz.rows), 1))
        .astype(F32)
        .astype(BF)
    )
    pos1 = mm(oh1.astype(BF), before)
    pos2 = mm(oh2.astype(BF), before) + jnp.sum(oh1, 1, keepdims=True)
    place = oh1 * pos1 + oh2 * pos2
    kept = (oh1 + oh2 > 0.5) & (place < sz.cap - 0.5)
    slot = jnp.where(kept, place, -1.0).astype(jnp.int32)
    slot_ids = iota((sz.slots, sz.rows), 0)

    def picks(e):
        return (slot_ids == slot[e : e + 1, :]).astype(F32).astype(BF)

    eye = (iota((sz.rows, sz.rows), 0) == iota((sz.rows, sz.rows), 1)).astype(F32)
    slot_cols = mm_nt(eye.astype(BF), slot.astype(F32).astype(BF)).astype(jnp.int32)
    lane_ids = iota((sz.rows, sz.slots), 1)
    for e in range(sz.experts):
        comb[e] = (slot_cols[:, e : e + 1] == lane_ids).astype(F32).astype(BF)

    x = mm(pad_matrix(sz), tok_ref[...])
    load_grad.wait()
    gpad[...] = mm(pad_matrix(sz), stage[...]).astype(BF)
    for e in range(sz.experts):
        gs[e * sz.slots : (e + 1) * sz.slots, :] = mm(picks(e), gpad[...]).astype(BF)
    slots_me = rows_at(me, sz.slots)
    dres[slots_me, :] = gs[slots_me, :]

    for k in range(1, n):
        for cp in small_sends(k):
            cp.wait_recv()
    smf[...] = jnp.zeros_like(smf)
    for j in range(n):
        r = iota((sz.shard, d), 0)
        c = iota((sz.shard, d), 1)
        pick = (c == r + j * sz.shard).astype(F32).astype(BF)
        smf[0:2, :] += mm(gains[j], pick)
        smf[2:7, :] += mm(biases[j], pick)
        smf[8 : 8 + sz.experts, :] += mm(routers[j], pick)
    normed[...] = normalize(x, smf[0:1, :], smf[2:3, :]).astype(BF)
    normed_t[...] = normed[...].T

    gather_q.forward()
    gather_p.start()
    gather_q.finish()
    gather_q.save().start()
    for j, bias_row in ((0, 3), (1, None), (2, 4)):
        cols = slice(j * d, (j + 1) * d)
        value = mm(normed[...], dw[:, cols])
        if bias_row is not None:
            value = value + smf[bias_row : bias_row + 1, :]
        qkv[:, cols] = value.astype(BF)
    for k in range(1, n):
        dst = rows_at(lax.rem(me + k, n), sz.slots)
        to_peer(gs.at[dst, :], dres.at[slots_me, :], g_sem, k).start()

    scale = 1.0 / math.sqrt(HEAD_DIM)
    half_lane = iota((sz.seq, 128), 1)
    live = iota((sz.seq, sz.seq), 1) < SEQ

    def save_probs(pair):
        slot = lax.rem(pair, 2)
        return pltpu.make_async_copy(pbuf.at[slot], o_probs.at[pair], psem.at[slot])

    def forward_pair(pair, carry):
        @pl.when(pair >= 2)
        def _():
            save_probs(pair - 2).wait()

        for image in range(sz.images):
            rows = slice(image * sz.seq, (image + 1) * sz.seq)
            at = [pl.ds(pl.multiple_of(j * d + pair * 128, 128), 128) for j in range(3)]
            q2, k2, v2_ = (qkv[rows, at[j]] for j in range(3))
            total = jnp.zeros((sz.seq, 128), F32)
            for half in range(2):
                mask = (half_lane >= half * 64) & (half_lane < half * 64 + 64)
                zero = jnp.zeros_like(q2)
                s = mm_nt(jnp.where(mask, q2, zero), k2) * scale
                s = jnp.where(live, s, -1e30)
                e = jnp.exp(s - jnp.max(s, -1, keepdims=True))
                p = (e / jnp.sum(e, -1, keepdims=True)).astype(BF)
                pbuf[lax.rem(pair, 2), image * 2 + half] = p
                total = total + mm(p, jnp.where(mask, v2_, zero))
            ctx[rows, at[0]] = total.astype(BF)
        save_probs(pair).start()
        return carry

    lax.fori_loop(0, sz.pairs, forward_pair, 0)

    gather_p.forward()
    gather_p.finish()
    gather_p.save().start()
    res = (
        mm(pad_matrix(sz), tok_ref[...])
        + mm(ctx[...], dw[:, 3 * d : 4 * d])
        + smf[5:6, :]
    )
    resid[...] = res
    second[...] = normalize(res, smf[1:2, :], smf[6:7, :]).astype(BF)
    ctx_t[...] = ctx[...].T
    for k in [*range(1, n), 0]:
        rows = rows_at(lax.rem(me + k, n), sz.slots)
        line = slot[0:1, :]
        for e in range(1, sz.experts):
            line = jnp.where(lax.rem(me + k, n) == e, slot[e : e + 1, :], line)
        pick = (slot_ids == line).astype(F32).astype(BF)
        xs[rows, :] = mm(pick, second[...]).astype(BF)
        if k:
            to_peer(xs.at[rows, :], xr.at[slots_me, :], x_sem, k).start()
        else:
            xr[slots_me, :] = xs[slots_me, :]
    for gather in (gather_q, gather_p):
        gather.drain()
        gather.save().wait()
    load_w1 = pltpu.make_async_copy(w1_hbm, dw, wsem.at[0])
    load_w1.start()

    small_low = smf[...].astype(BF)
    low = second[...]
    logit_rows = mm_nt(small_low, low)[8 : 8 + sz.ep, :]
    logit_rows = jnp.where(iota((sz.ep, sz.rows), 0) < sz.experts, logit_rows, -1e30)
    e_rows = jnp.exp(logit_rows - jnp.max(logit_rows, 0, keepdims=True))
    prob_rows = e_rows / jnp.sum(e_rows, 0, keepdims=True)
    hi = prob_rows.astype(BF)
    left = prob_rows - hi.astype(F32)
    mid = left.astype(BF)
    rest_low = (left - mid.astype(F32)).astype(BF)
    for e in range(sz.experts):
        block = picks(e)
        gates[e] = mm_nt(hi, block) + mm_nt(mid, block) + mm_nt(rest_low, block)
    for k in range(1, n):
        to_peer(gates.at[lax.rem(me + k, n)], gater.at[me], ga_sem, k).start()
    gater[me] = gates[me]
    logit_cols = mm_nt(low, small_low)
    col = iota((sz.rows, sz.small), 1)
    logit_cols = jnp.where((col >= 8) & (col < 8 + sz.experts), logit_cols, -1e30)
    e_cols = jnp.exp(logit_cols - jnp.max(logit_cols, 1, keepdims=True))
    probs[...] = e_cols / jnp.sum(e_cols, 1, keepdims=True)
    for pair in range(max(sz.pairs - 2, 0), sz.pairs):
        save_probs(pair).wait()

    lower = 1 - lax.div(z, (nz + 1) // 2)
    xta = res_send.at[0:d, :]
    bias2[...] = jnp.zeros_like(bias2)
    load_w2.wait()
    load_w1.wait()

    def w1_part(f):
        return dw[:, pl.ds(pl.multiple_of(f * fs, 128), fs)]

    square = iota((sz.slots, sz.slots), 0) == iota((sz.slots, sz.slots), 1)

    def peer_slots(k):
        return rows_at(lax.rem(me + k, n), sz.slots)

    def send_back(k):
        rows = peer_slots(k)
        row_send[rows, :] = row_acc[rows, :].astype(BF)
        out = (res_acc[rows, :] + b2_ref[...].astype(F32)).astype(BF).astype(F32)
        column = jnp.sum(out * dres[rows, :].astype(F32), 1, keepdims=True)
        line = jnp.sum(jnp.where(square, column, 0.0), 0, keepdims=True)
        qs[k] = jnp.broadcast_to(line, (8, sz.slots))
        if k == 0:
            bck[slots_me, :] = row_send[rows, :]
            qr[me] = qs[k]
        else:
            to_peer(row_send.at[rows, :], bck.at[slots_me, :], bck_sem, k).start()
            to_peer(qs.at[k], qr.at[me], q_sem, k).start()

    def prepare(k):
        src = lax.rem(me + k, n)
        rows = rows_at(src, sz.slots)
        if k:
            at = n - k
            to_peer(gs.at[peer_slots(at), :], dres.at[rows, :], g_sem, at).wait()
            to_peer(gates.at[lax.rem(me + at, n)], gater.at[src], ga_sem, at).wait()
        row = gater[src, pl.ds(me, 1), :]
        gate = jnp.sum(jnp.where(square, row, 0.0), 1, keepdims=True)
        value = (gate * dres[rows, :].astype(F32)).astype(BF)
        dres[rows, :] = value
        bias2[...] += jnp.sum(value.astype(F32), 0, keepdims=True)
        if k:
            to_peer(xs.at[peer_slots(at), :], xr.at[rows, :], x_sem, at).wait()

    def compute(f, order, flag, ahead=None, behind=None):
        w2f_rows = pl.ds(pl.multiple_of(f * fs, 16), fs)
        bias = b1_ref[:, pl.ds(pl.multiple_of(f * fs, 128), fs)].astype(F32)
        for k in order:
            rows = peer_slots(k)
            if ahead is not None:
                pl.when(flag)(partial(ahead, k))
            h = mm(xr[rows, :], w1_part(f)) + bias
            cdf, pdf = gelu_parts(h)
            da = mm_nt(dres[rows, :], w2[w2f_rows, :])
            a = (h * cdf).astype(BF)
            dh = (da * (cdf + h * pdf)).astype(BF)
            act[rows, :] = a
            dhid[rows, :] = dh
            res_acc[rows, :] += mm(a, w2[w2f_rows, :])
            row_acc[rows, :] += mm_nt(dh, w1_part(f))
            if behind is not None:
                pl.when(flag)(partial(behind, k))

    def grad1(rows):
        part = mm(xta[rows, :], dhid[0:d, :])
        return part + mm(xt[rows, :], dhid[d:, :])

    def grad2(cols):
        return mm_tn(act[:, cols], dres[...])

    def extra():
        gb = jnp.sum(dhid[...].astype(F32), 0, keepdims=True)
        row = iota((16, d), 0)
        line = jnp.concatenate([gb, jnp.zeros((1, d - fs), F32)], 1)
        return jnp.where(row == 0, line, jnp.where(row == 1, bias2[...], 0.0))

    def t_copies(dest):
        return (
            remote(t1, v1.at[dest], t_sem.at[0, 0, dest], t_sem.at[1, 0, dest], sibling, me),
            remote(t2, v2.at[dest], t_sem.at[0, 1, dest], t_sem.at[1, 1, dest], sibling, me),
        )

    def landing(way, step, at):
        if way == 0:
            return nz - 2 - step + at
        return at + step + 2 - nz if step < nz - 2 else nz

    def u_copies(src1, src2, way, step, target, slot):
        return (
            remote(src1, u1.at[slot], u_sem.at[0, 0, way, step], u_sem.at[1, 0, way, step], target, me),
            remote(src2, u2.at[slot], u_sem.at[0, 1, way, step], u_sem.at[1, 1, way, step], target, me),
        )

    res_acc[...] = jnp.zeros_like(res_acc)
    row_acc[...] = jnp.zeros_like(row_acc)

    parts1 = [slice(i, i + d // 2) for i in (0, d // 2)]
    parts2 = [slice(i, i + 128) for i in range(0, fs, 128)]

    def dest_of(i):
        return lower * (nz - 1 - i) + (1 - lower) * i

    def slice_step(i, carry):
        dest = dest_of(i)

        compute(dest * 2 + 1 - core, range(n), i == 0, prepare)

        @pl.when(i == 0)
        def _():
            xta[...] = xr[0:d, :].T
            xt[...] = xr[d:, :].T

        for rows in parts1:
            t1[rows, :] = grad1(rows).astype(BF)
        for rows in parts2:
            t2[rows, :] = grad2(rows).astype(BF)
        t2[fs:, :] = extra().astype(BF)
        for cp in t_copies(dest):
            cp.start()
        compute(dest * 2 + core, [*range(1, n), 0], i == nz - 1, None, send_back)
        for cp in t_copies(dest):
            cp.wait()
        for rows in parts1:
            v1[dest, rows, :] = (v1[dest, rows, :].astype(F32) + grad1(rows)).astype(BF)
        for rows in parts2:
            v2[dest, rows, :] = (v2[dest, rows, :].astype(F32) + grad2(rows)).astype(BF)
        v2[dest, fs:, :] = (v2[dest, fs:, :].astype(F32) + extra()).astype(BF)

        @pl.when((z == 0) & (i <= nz - 2))
        def _():
            for cp in u_copies(v1.at[dest], v2.at[dest], 0, i, me_r + 2, dest):
                cp.start()

        @pl.when((z == nz - 1) & (i < nz - 2))
        def _():
            for cp in u_copies(v1.at[dest], v2.at[dest], 1, i, me_r - 2, dest):
                cp.start()

        @pl.when((z == nz - 1) & (i == nz - 2))
        def _():
            for cp in u_copies(v1.at[dest], v2.at[dest], 1, i, me_r - 2, nz):
                cp.start()

        return carry

    lax.fori_loop(0, nz, slice_step, 0)

    res_send[...] = (res_acc[...] + b2_ref[...].astype(F32)).astype(BF)
    for k in range(1, n):
        to_peer(res_send.at[peer_slots(k), :], ret.at[slots_me, :], ret_sem, k).start()
    ret[slots_me, :] = res_send[slots_me, :]
    dense_load = pltpu.make_async_copy(o_save, dw, wsem.at[0])
    dense_load.start()

    def z_round(s):
        for way in range(2):
            zz = z if way == 0 else nz - 1 - z
            dest = nz - 1 - s + zz if way == 0 else z - (nz - 1 - s)
            target = me_r + 2 if way == 0 else me_r - 2

            @pl.when((zz >= 1) & (zz <= s))
            def _():
                here = landing(way, s - 1, z)
                there = landing(way, s, z + 1 if way == 0 else z - 1)
                a1, a2 = u1.at[here], u2.at[here]
                for cp in u_copies(a1, a2, way, s - 1, target, here):
                    cp.wait_recv()
                u1[here] = (u1[here].astype(F32) + v1[dest].astype(F32)).astype(BF)
                u2[here] = (u2[here].astype(F32) + v2[dest].astype(F32)).astype(BF)
                for cp in u_copies(a1, a2, way, s, target, there):
                    cp.start()

    if nz > 2:
        z_round(1)

    for k in range(1, n):
        src = lax.rem(me + n - k, n)
        theirs = rows_at(src, sz.slots)
        to_peer(row_send.at[peer_slots(k), :], bck.at[theirs, :], bck_sem, k).wait()
        to_peer(qs.at[k], qr.at[src], q_sem, k).wait()
    mixed = res_acc.at[0 : sz.rows, :]
    sgrad = res_acc.at[sz.rows : 2 * sz.rows, :]
    lane = iota((sz.rows, sz.small), 1)
    weighted = jnp.zeros((sz.rows, sz.small), F32)
    for e in range(sz.experts):
        q = jnp.sum(comb[e].astype(F32) * qr[e, 0:1, :], 1, keepdims=True)
        weighted = jnp.where(lane == 8 + e, q, weighted)
    total = jnp.sum(weighted, 1, keepdims=True)
    logit_low = (weighted - probs[...] * total).astype(BF)
    sgrad[...] = mm(logit_low, smf[...].astype(BF))
    for e in range(sz.experts):
        sgrad[...] += mm(comb[e], bck[e * sz.slots : (e + 1) * sz.slots, :])
    back2, gain2, shift2 = normalize_back(resid[...], smf[1:2, :], sgrad[...])
    rgrad = row_acc.at[0 : sz.rows, :]
    rgrad[...] = gpad[...].astype(F32) + back2
    low = rgrad[...].astype(BF)
    bias_out = jnp.sum(low.astype(F32), 0, keepdims=True)

    dense = w2
    wide = d // 2
    keep = pl.ds(pl.multiple_of(core * wide, 128), wide)
    give = pl.ds(pl.multiple_of((1 - core) * wide, 128), wide)
    part = sz.part

    def chunk_rows(j, start, size):
        return pl.ds(pl.multiple_of(j * d + start, 16), size)

    def part_rows(zi):
        return pl.ds(pl.multiple_of(zi * part, 16), part)

    def to_sibling(j):
        return remote(
            dense.at[chunk_rows(j, 0, d), give],
            r1.at[j],
            d1_sem.at[0, j],
            d1_sem.at[1, j],
            sibling,
            me,
        )

    def to_owner(j, k):
        e = lax.rem(me + k, n)
        return remote(
            dense.at[chunk_rows(j, e * sz.shard, sz.shard), keep],
            r2.at[k - 1, j],
            d2_sem.at[0, j, k],
            d2_sem.at[1, j, k],
            me_r,
            e,
        )

    def to_layer(j, k):
        return remote(
            z1.at[j, part_rows(lax.rem(z + k, nz)), :],
            z2.at[k - 1, j],
            z1_sem.at[0, j, k],
            z1_sem.at[1, j, k],
            lax.rem(me_r + 2 * k, 2 * nz),
            me,
        )

    def from_layer(j, k, owner):
        piece = o_dense.at[j, part_rows(owner), keep]
        return remote(
            piece,
            piece,
            z2_sem.at[0, j, k],
            z2_sem.at[1, j, k],
            lax.rem(me_r + 2 * k, 2 * nz),
            me,
        )

    def to_twin(j, cols):
        piece = o_dense.at[j, :, cols]
        return remote(piece, piece, z3_sem.at[0, j], z3_sem.at[1, j], sibling, me)

    def stage1(j):
        to_sibling(j).wait()
        rows = chunk_rows(j, 0, d)
        dense[rows, keep] = (dense[rows, keep].astype(F32) + r1[j].astype(F32)).astype(BF)
        for k in range(1, n):
            to_owner(j, k).start()

    def stage2(j):
        acc = dense[chunk_rows(j, me * sz.shard, sz.shard), keep].astype(F32)
        for k in range(1, n):
            to_owner(j, k).wait()
            acc = acc + r2[k - 1, j].astype(F32)
        z1[j] = acc.astype(BF)
        for k in range(1, nz):
            to_layer(j, k).start()

    def stage3(j):
        acc = z1[j, part_rows(z), :].astype(F32)
        for k in range(1, nz):
            to_layer(j, k).wait()
            acc = acc + z2[k - 1, j].astype(F32)
        o_dense[j, part_rows(z), keep] = acc.astype(BF)
        for k in range(1, nz):
            from_layer(j, k, z).start()

    def stage4(j):
        for k in range(1, nz):
            from_layer(j, k, z).wait_send()
            from_layer(j, k, lax.rem(z + nz - k, nz)).wait_recv()
        to_twin(j, keep).start()

    def stage5(j):
        to_twin(j, keep).wait_send()
        to_twin(j, give).wait_recv()

    dense[chunk_rows(0, 0, d), :] = mm(ctx_t[...], low).astype(BF)
    to_sibling(0).start()
    dense_load.wait()
    for k in range(1, n):
        theirs = rows_at(lax.rem(me + n - k, n), sz.slots)
        to_peer(res_send.at[peer_slots(k), :], ret.at[theirs, :], ret_sem, k).wait()
    dq_ref = res_send.at[0 : sz.rows, :]
    dk_ref = res_send.at[sz.rows : 2 * sz.rows, :]
    dv_ref = row_send.at[0 : sz.rows, :]
    cgrad = row_send.at[sz.rows : 2 * sz.rows, :]
    dqkv = (dq_ref, dk_ref, dv_ref)

    def load_probs(pair):
        slot = lax.rem(pair, 2)
        return pltpu.make_async_copy(o_probs.at[pair], pbuf.at[slot], psem.at[slot])

    load_probs(0).start()
    cgrad[...] = mm_nt(low, dw[:, 3 * d : 4 * d]).astype(BF)
    sm[...] = mm_tn(logit_low, second[...])

    for s in range(2, nz - 1):
        z_round(s)

    scale = 1.0 / math.sqrt(HEAD_DIM)
    half_lane = iota((sz.seq, 128), 1)

    def pair_step(pair, carry):
        load_probs(pair).wait()

        @pl.when(pair + 1 < sz.pairs)
        def _():
            load_probs(pair + 1).start()

        for image in range(sz.images):
            rows = slice(image * sz.seq, (image + 1) * sz.seq)
            at = [pl.ds(pl.multiple_of(j * d + pair * 128, 128), 128) for j in range(3)]
            q2, k2, v2_ = (qkv[rows, at[j]] for j in range(3))
            c2 = cgrad[rows, at[0]]
            dq = jnp.zeros((sz.seq, 128), F32)
            dk = jnp.zeros((sz.seq, 128), F32)
            dv = jnp.zeros((sz.seq, 128), F32)
            for half in range(2):
                mask = (half_lane >= half * 64) & (half_lane < half * 64 + 64)
                zero = jnp.zeros_like(q2)
                ch = jnp.where(mask, c2, zero)
                p = pbuf[lax.rem(pair, 2), image * 2 + half]
                dv = dv + mm_tn(p, ch)
                pb = mm_nt(ch, v2_)
                p32 = p.astype(F32)
                mix = jnp.sum(pb * p32, -1, keepdims=True)
                ds = (p32 * (pb - mix)).astype(BF)
                dq = dq + mm(ds, jnp.where(mask, k2, zero))
                dk = dk + mm_tn(ds, jnp.where(mask, q2, zero))
            dq_ref[rows, at[0]] = (dq * scale).astype(BF)
            dk_ref[rows, at[0]] = (dk * scale).astype(BF)
            dv_ref[rows, at[0]] = dv.astype(BF)
        return carry

    def group_step(g, carry):
        lax.fori_loop(2 * g, 2 * g + 2, pair_step, 0)
        cols = pl.ds(pl.multiple_of(g * 256, 128), 256)
        for j in range(3):
            dense[chunk_rows(g + 1, 0, d), j * 256 : (j + 1) * 256] = mm(
                normed_t[...], dqkv[j][:, cols]
            ).astype(BF)
        to_sibling(g + 1).start()
        stage1(g)
        return carry

    lax.fori_loop(0, sz.groups, group_step, 0)
    stage1(sz.groups)

    ngrad = sgrad
    ngrad[...] = mm_nt(dq_ref[...], dw[:, 0:d])
    for j in range(1, 3):
        ngrad[...] += mm_nt(dqkv[j][...], dw[:, j * d : (j + 1) * d])
    stage2(0)
    x = mm(pad_matrix(sz), tok_ref[...])
    back1, gain1, shift1 = normalize_back(x, smf[0:1, :], ngrad[...])
    stage[...] = mm(unpad_matrix(sz), (rgrad[...] + back1).astype(BF)).astype(BF)
    store = pltpu.make_async_copy(stage, o_gin, wsem.at[2])
    store.start()
    bias_q = jnp.sum(dq_ref[...].astype(F32), 0, keepdims=True)
    bias_v = jnp.sum(dv_ref[...].astype(F32), 0, keepdims=True)
    row = iota((sz.small, d), 0)
    small = sm[...]
    for i, value in enumerate((gain1, gain2, shift1, bias_q, bias_v, bias_out, shift2)):
        small = jnp.where(row == i, value, small)
    sm[...] = small
    smb = sme.at[n]
    smb[...] = small.astype(BF)
    s_first = remote(smb, smr, s1_sem.at[0], s1_sem.at[1], sibling, me)
    s_first.start()

    stage2(1)
    stage3(0)
    mixed[...] = resid[...]
    for e in range(sz.experts):
        block = slice(e * sz.slots, (e + 1) * sz.slots)
        mixed[...] += probs[:, 8 + e : 9 + e] * mm(comb[e], ret[block, :])
    store.wait()
    stage[...] = mm(unpad_matrix(sz), mixed[...].astype(BF)).astype(BF)
    store = pltpu.make_async_copy(stage, o_out, wsem.at[2])
    store.start()

    s_first.wait()
    chip_small = (sm[...] + smr[...].astype(F32)).astype(BF)
    for e in range(n):
        r = iota((sz.shard_pad, d), 0)
        c = iota((sz.shard_pad, d), 1)
        pick = ((c == r + e * sz.shard) & (r < sz.shard)).astype(F32).astype(BF)
        sme[e, :, 0 : sz.shard_pad] = mm_nt(chip_small, pick).astype(BF)

    def small_peer(k):
        piece = sme.at[lax.rem(me + k, n), :, 0 : sz.shard_pad]
        return to_peer(piece, sme_r.at[k], s2_sem, k)

    for k in range(1, n):
        small_peer(k).start()
    stage2(2)
    stage3(1)
    stage4(0)
    acc = sme[me, :, 0 : sz.shard_pad].astype(F32)
    for k in range(1, n):
        small_peer(k).wait()
        acc = acc + sme_r[k].astype(F32)
    smz_r[0] = acc.astype(BF)
    for k in range(1, nz):
        to_z(smz_r.at[0], smz_r.at[k], s3_sem, k).start()
    stage2(3)
    stage3(2)
    stage4(1)

    for way in range(2):
        zz = z if way == 0 else nz - 1 - z
        target = me_r + 2 if way == 0 else me_r - 2

        @pl.when(zz >= 1)
        def _():
            here = landing(way, nz - 2, z)
            for cp in u_copies(u1.at[here], u2.at[here], way, nz - 2, target, here):
                cp.wait_recv()
            v1[z] = (v1[z].astype(F32) + u1[here].astype(F32)).astype(BF)
            v2[z] = (v2[z].astype(F32) + u2[here].astype(F32)).astype(BF)

    stores = [
        pltpu.make_async_copy(v1.at[z], o_w1, wsem.at[0]),
        pltpu.make_async_copy(v2.at[z], o_w2, wsem.at[1]),
    ]
    for cp in stores:
        cp.start()
    stage3(3)
    stage4(2)
    acc = smz_r[0].astype(F32)
    for k in range(1, nz):
        to_z(smz_r.at[0], smz_r.at[k], s3_sem, k).wait()
        acc = acc + smz_r[k].astype(F32)
    o_small[...] = acc
    stage4(3)
    for j in range(sz.chunks):
        stage5(j)

    for cp in stores:
        cp.wait()
    store.wait()
    for s in range(nz - 1):
        for way in range(2):
            zz = z if way == 0 else nz - 1 - z
            target = me_r + 2 if way == 0 else me_r - 2

            @pl.when(zz <= s)
            def _():
                for cp in u_copies(v1.at[0], v2.at[0], way, s, target, 0):
                    cp.wait_send()
    for k in range(1, n):
        for cp in small_sends(k):
            cp.wait_send()


def block(sz, tokens, routes, router, gains, biases, b1, b2, grad, wq, wp, w1, w2):
    vmem = pl.BlockSpec(memory_space=pltpu.VMEM)
    hbm = pl.BlockSpec(memory_space=pl.ANY)
    rows, d, slots, fs, nz, n = sz.rows, sz.d, sz.all_slots, sz.fs, sz.nz, sz.n_exp
    half = d // 2
    dma = pltpu.SemaphoreType.DMA
    outs = [
        ((sz.chunks, sz.shard, d), BF),
        ((sz.small, sz.shard_pad), F32),
        ((sz.tok, d), BF),
        ((sz.tok, d), BF),
        ((d, fs), BF),
        ((sz.fs_rows, d), BF),
        ((sz.pairs, sz.images * 2, sz.seq, sz.seq), BF),
        ((d, 4 * d), BF),
    ]
    buffers = [
        ((d, 4 * d), BF),
        (w2.shape, BF),
        ((sz.tok, d), BF),
        ((slots, d), BF),
        ((slots, d), BF),
        ((rows, 3 * d), BF),
        ((d, rows), BF),
        ((rows, d), F32),
        ((rows, d), BF),
        ((d, rows), BF),
        ((rows, sz.small), F32),
        ((sz.small, d), F32),
        ((rows, d), BF),
        ((sz.experts, rows, sz.slots), BF),
        ((n, sz.ep, sz.slots), F32),
        ((n, sz.ep, sz.slots), F32),
        ((n, *router.shape), BF),
        ((n, *gains.shape), BF),
        ((n, *biases.shape), BF),
        ((1, d), F32),
        ((d, slots - d), BF),
        ((slots, fs), BF),
        ((slots, fs), BF),
        ((slots, d), F32),
        ((slots, d), F32),
        ((slots, d), BF),
        ((slots, d), BF),
        ((slots, d), BF),
        ((slots, d), BF),
        ((n, 8, sz.slots), F32),
        ((n, 8, sz.slots), F32),
        ((d, fs), BF),
        ((sz.fs_rows, d), BF),
        ((nz, d, fs), BF),
        ((nz, sz.fs_rows, d), BF),
        ((nz + 1, d, fs), BF),
        ((nz + 1, sz.fs_rows, d), BF),
        ((2, 2 * sz.images, sz.seq, sz.seq), BF),
        ((sz.chunks, d, half), BF),
        ((n - 1, sz.chunks, sz.shard, half), BF),
        ((sz.chunks, sz.shard, half), BF),
        ((nz - 1, sz.chunks, sz.part, half), BF),
        ((sz.small, d), F32),
        ((sz.small, d), BF),
        ((n + 1, sz.small, d), BF),
        ((n, sz.small, sz.shard_pad), BF),
        ((nz, sz.small, sz.shard_pad), BF),
    ]
    sems = (
        [dma((4,)), dma((2,))]
        + [dma((2, n))] * 4
        + [dma((2, 2, n))] * 2
        + [dma((3, 2, n))]
        + [dma((2, n))] * 3
        + [dma((2, 2, nz)), dma((2, 2, 2, nz - 1))]
        + [dma((2, n))] * 3
        + [dma((2, sz.chunks)), dma((2, sz.chunks, n))]
        + [dma((2, sz.chunks, nz))] * 2
        + [dma((2, sz.chunks)), dma((2,)), dma((2, n)), dma((2, nz))]
    )
    return pl.pallas_call(
        partial(block_kernel, sz),
        name="block",
        out_shape=[jax.ShapeDtypeStruct(s, t) for s, t in outs],
        in_specs=[vmem] * 7 + [hbm] * 5,
        out_specs=[vmem] * 2 + [hbm] * 6,
        scratch_shapes=[pltpu.VMEM(s, t) for s, t in buffers] + sems,
        compiler_params=pltpu.CompilerParams(
            collective_id=1, has_side_effects=True, vmem_limit_bytes=62 << 20
        ),
    )(tokens, routes, router, gains, biases, b1, b2, grad, wq, wp, w1, w2)


def plain_rest(sz, state, tokens, w1, b1, w2, b2):
    xr, dres, qkv, pall, ctx_t, resid, second, normed_t, probs, wq, wp, smf, gpad, comb = state
    d, n = sz.d, sz.experts
    scale = 1.0 / math.sqrt(HEAD_DIM)
    h = mm(xr, w1) + b1
    cdf, pdf = gelu_parts(h)
    act = (h * cdf).astype(BF)
    result = (mm(act, w2) + b2).astype(BF)
    dhid = (mm_nt(dres, w2) * (cdf + h * pdf)).astype(BF)
    row_grad = mm_nt(dhid, w1).astype(BF)
    swap = partial(
        lax.all_to_all, axis_name="exp", split_axis=0, concat_axis=0, tiled=True
    )
    ret = swap(result).reshape(n, sz.slots, d)
    bck = swap(row_grad).reshape(n, sz.slots, d)
    g32 = gpad.astype(F32)
    p = probs[:, 8 : 8 + n]
    picked = jnp.einsum("ets,esd->etd", comb, ret, preferred_element_type=F32)
    mixed = resid + jnp.einsum("te,etd->td", p, picked, precision="highest")
    pg = jnp.sum(g32[None] * picked, -1).T
    lg = (p * (pg - jnp.sum(pg * p, 1, keepdims=True))).astype(BF)
    sgrad = mm(lg, smf[8 : 8 + n].astype(BF))
    sgrad = sgrad + jnp.einsum("ets,esd->td", comb, bck, preferred_element_type=F32)
    back2, gain2, shift2 = normalize_back(resid, smf[1:2], sgrad)
    rgrad = g32 + back2
    low = rgrad.astype(BF)
    cgrad = mm_nt(low, wp).astype(BF)
    four = (sz.images, sz.seq, d // HEAD_DIM, HEAD_DIM)
    q, k, v, c = (
        a.reshape(four)
        for a in (qkv[:, :d], qkv[:, d : 2 * d], qkv[:, 2 * d :], cgrad)
    )
    prob = pall.reshape(sz.pairs, sz.images, 2, sz.seq, sz.seq)
    prob = prob.transpose(1, 0, 2, 3, 4).reshape(sz.images, -1, sz.seq, sz.seq)
    product = partial(jnp.einsum, preferred_element_type=F32)
    dv = product("ihst,ishd->ithd", prob, c).astype(BF)
    pb = product("ishd,ithd->ihst", c, v)
    p32 = prob.astype(F32)
    ds = (p32 * (pb - jnp.sum(pb * p32, -1, keepdims=True))).astype(BF)
    dq = (product("ihst,ithd->ishd", ds, k) * scale).astype(BF)
    dk = (product("ihst,ishd->ithd", ds, q) * scale).astype(BF)
    dqkv = jnp.concatenate([a.reshape(sz.rows, d) for a in (dq, dk, dv)], 1)
    x = mm(pad_matrix(sz), tokens)
    back1, gain1, shift1 = normalize_back(x, smf[0:1], mm_nt(dqkv, wq))
    gin = (rgrad + back1).astype(BF)
    sums = jnp.sum(dqkv.astype(F32), 0, keepdims=True)
    small = jnp.concatenate(
        [gain1, gain2, shift1, sums[:, :d], sums[:, 2 * d :]]
        + [jnp.sum(low.astype(F32), 0, keepdims=True), shift2, mm_tn(lg, second)]
    )

    def dense(grad, dim):
        total = lax.psum(grad.astype(BF), "rep")
        total = lax.psum_scatter(total, "exp", scatter_dimension=dim, tiled=True)
        return total.astype(F32)

    def owned(grad, dim):
        total = lax.psum_scatter(
            grad[None].astype(BF), "rep", scatter_dimension=dim, tiled=True
        )
        return total.astype(F32)

    def unpad(rows):
        return rows.reshape(sz.images, sz.seq, d)[:, :SEQ].reshape(sz.tok, d)

    sums = dense(small, 1)
    return (
        unpad(mixed.astype(BF)),
        unpad(gin),
        dense(mm(normed_t, dqkv), 0),
        dense(mm(ctx_t, low), 0),
        sums[7:].T,
        sums[0:2],
        sums[2:7],
        owned(mm_tn(xr, dhid), 2),
        owned(jnp.sum(dhid.astype(F32), 0), 1),
        owned(mm_tn(act, dres), 1),
        owned(jnp.sum(dres.astype(F32), 0), 1),
    )


def on_device(
    mesh,
    tokens,
    routes,
    out_grad,
    attn_qkv,
    attn_out,
    router,
    norm_gains,
    dense_biases,
    expert_in,
    expert_in_bias,
    expert_out,
    expert_out_bias,
):
    sz = Sizes(mesh, tokens.shape[0], tokens.shape[1], expert_in.shape[2])
    d, fs = sz.d, sz.fs
    w1, w2 = expert_in[0], expert_out[0]
    small = (router.T, norm_gains, dense_biases)
    if fs % 128 or sz.all_slots % 128 or sz.all_slots < 2 * sz.rows or sz.part % 16:
        state = front(sz, tokens, out_grad, routes.T, attn_qkv, attn_out, *small)
        bias1, bias2 = expert_in_bias.astype(F32), expert_out_bias.astype(F32)
        return plain_rest(sz, state, tokens, w1, bias1, w2, bias2)
    dense, sums, out, gin, g1, g2, _, _ = block(
        sz,
        tokens,
        routes.T,
        *small,
        expert_in_bias,
        expert_out_bias,
        out_grad,
        attn_qkv,
        attn_out,
        w1,
        w2,
    )
    return finish(sz, out, gin, g1, g2, dense, sums)


def solution(mesh):
    both = P(("rep", "exp"), None)
    rows = P("exp", None)
    cols = P(None, "exp")
    cube = P("exp", None, None)
    in_specs = (both, both, both, rows, rows, rows, cols, cols, cube, rows, cube, rows)
    out_specs = (
        both,
        both,
        rows,
        rows,
        rows,
        cols,
        cols,
        P("exp", None, "rep"),
        P("exp", "rep"),
        P("exp", "rep", None),
        P("exp", "rep"),
    )
    return jax.shard_map(
        partial(on_device, mesh),
        mesh=mesh,
        in_specs=in_specs,
        out_specs=out_specs,
        check_vma=False,
    )
```

time: 249 us -> 205 us (0.82)
  Pallas kernels: 233 us -> 204 us
  local copies, waits for them, and re-layouts: 10.7 us -> 0 us
  other arithmetic: 3.9 us -> 0 us
    pallas_call x2, Pallas kernels: 233 us -> 204 us  [the longest x1 200 us: block(): pl.pallas_call(partial(block_kernel, sz), name='block', out_shape=[jax.Sh...]
    slice x4 -> x0, local copies, waits for them, and re-layouts: 4 us -> none  [the longest x1 2.25 us: on_device(): dense[3]]
where the time goes in v3:
time: 205 us
  Pallas kernels  204 us (100%)
    pallas_call x1, Pallas kernels, block(): pl.pallas_call(partial(block_kernel, sz), name='block', out_shape=[jax.Sh...  200 us
    pallas_call x1, Pallas kernels, finish(): pl.pallas_call(partial(finish_kernel, sz), name='finish', out_shape=[jax....  4.65 us

profile of v3, /device:TPU:0, one launch (start us, length us, event | category | flops | bytes accessed | tf_op | source)
XLA Modules:
  0.0 205.2 jit_solution(13827580361857548962)
XLA Ops:
  0.6 199.7 %block.1 = (bf16[4,192,768]{2,1,0:T(8,128)(2,1)}, f32[16,256]{1,0:T(8,128)}, bf16[394,768]{1,0:T(8,128)(2,1)}, bf16[394,768]{1,0:T(8,128)(2,1)}, bf16[768,384]{1...) custom-call(bf16[394,768]{1,0:T(8,128)(2,1)} %tok_ref.1, ...), custom_call_target="tpu_custom_call" | custom-call | tf_op jit(solution)/shard_map/block/pallas_call | solution.py:1463
  200.3 4.6 %finish.1 = (bf16[394,768]{1,0:T(8,128)(2,1)}, bf16[394,768]{1,0:T(8,128)(2,1)}, f32[192,2304]{1,0:T(8,128)}, f32[192,768]{1,0:T(8,128)}, f32[4,192]{1,0:T(4,128...) custom-call(bf16[394,768]{1,0:T(8,128)(2,1)} %get-tuple-element.28.o, ...), custom_call_target="tpu_custom_call" | custom-call | tf_op jit(solution)/shard_map/finish/pallas_call | solution.py:492

commit v4 on v3

--- a/solution.py
+++ b/solution.py
@@ -568,24 +568,22 @@
     biases,
     bias2,
     xt,
-    act,
-    dhid,
-    res_acc,
-    row_acc,
-    res_send,
-    row_send,
+    xta,
+    acts,
+    dhids,
+    wide1,
+    wide2,
+    sends,
     ret,
     bck,
     qs,
     qr,
-    t1,
     t2,
     v1,
     v2,
     u1,
     u2,
     pbuf,
-    r1,
     r2,
     z1,
     z2,
@@ -596,12 +594,10 @@
     smz_r,
     wsem,
     psem,
-    wq_sem,
-    wp_sem,
-    zq_sem,
-    zp_sem,
-    cq_sem,
-    cp_sem,
+    f_sem,
+    l_sem,
+    c_sem,
+    o_sem,
     sm_sem,
     g_sem,
     x_sem,
@@ -671,85 +667,99 @@
 
     normed = bck.at[0 : sz.rows, :]
     ctx = bck.at[sz.rows : 2 * sz.rows, :]
+    res_send = sends.at[0 : sz.all_slots, :]
+    row_send = sends.at[sz.all_slots : 2 * sz.all_slots, :]
     xs, gs = res_send, row_send
 
-    class Gather:
-        def __init__(self, shard, base, width, own_sem, peer_sem, layer_sem, twin_sem):
-            self.shard = shard
-            self.base, self.width = base, width
-            self.piece = width // 6
-            self.own_sem = own_sem
-            self.peer_sem, self.layer_sem, self.twin_sem = peer_sem, layer_sem, twin_sem
-
-        def cols(self, side, first, count, base=0):
-            start = base + side * 3 * self.piece + first * self.piece
-            return pl.ds(pl.multiple_of(start, 128), count * self.piece)
-
-        def own(self):
-            return pltpu.make_async_copy(
-                self.shard,
-                dw.at[rows_at(me, sz.shard), self.base : self.base + self.width],
-                self.own_sem,
-            )
-
-        def save(self):
-            cols = slice(self.base, self.base + self.width)
-            return pltpu.make_async_copy(dw.at[:, cols], o_save.at[:, cols], self.own_sem)
-
-        def rows(self, k):
-            return rows_at(lax.rem(me + n - k, n), sz.shard)
-
-        def peer(self, k):
-            return to_peer(
-                self.shard.at[:, self.cols(core, odd, 2)],
-                dw.at[rows_at(me, sz.shard), self.cols(core, odd, 2, self.base)],
-                self.peer_sem,
-                k,
-            )
-
-        def layer(self, k, mine=True):
-            part = 2 * odd if mine else 2 - 2 * odd
-            piece = dw.at[self.rows(k), self.cols(core, part, 1, self.base)]
-            sem = self.layer_sem
-            return remote(piece, piece, sem.at[0, k], sem.at[1, k], partner, me)
-
-        def twin(self, k, late, side):
-            first, count = (2 - 2 * odd, 1) if late else (odd, 2)
-            piece = dw.at[self.rows(k), self.cols(side, first, count, self.base)]
-            sem = self.twin_sem
-            return remote(
-                piece, piece, sem.at[0, late, k], sem.at[1, late, k], sibling, me
-            )
-
-        def start(self):
-            for k in range(1, n):
-                self.peer(k).start()
-            self.own().start()
-
-        def forward(self):
-            for k in range(1, n):
-                self.peer(k).wait_recv()
-                self.layer(k).start()
-                self.twin(k, 0, core).start()
-
-        def finish(self):
-            self.own().wait()
-            for k in range(1, n):
-                self.layer(k, False).wait_recv()
-                self.twin(k, 1, core).start()
-            for k in range(1, n):
-                for late in range(2):
-                    self.twin(k, late, 1 - core).wait_recv()
-
-        def drain(self):
-            for k in range(1, n):
-                self.peer(k).wait_send()
-                self.layer(k).wait_send()
-                for late in range(2):
-                    self.twin(k, late, core).wait_send()
-
-    gather_q = Gather(wq_shard, 0, 3 * d, wsem.at[2], wq_sem, zq_sem, cq_sem)
-    gather_p = Gather(wp_shard, 3 * d, d, wsem.at[3], wp_sem, zp_sem, cp_sem)
+    piece = 128
+
+    def shard_cols(g, tile):
+        if isinstance(g, int) and g == sz.groups:
+            return wp_shard, tile * piece
+        return wq_shard, lax.div(tile, 2) * d + g * 256 + lax.rem(tile, 2) * piece
+
+    def dw_cols(g, tile, count):
+        return pl.ds(pl.multiple_of(g * d + tile * piece, 128), count * piece)
+
+    def dw_rows(k):
+        return rows_at(lax.rem(me + n - k, n), sz.shard)
+
+    def fetch(g, i, k):
+        tile = 3 * core + odd + i
+        shard, start = shard_cols(g, tile)
+        return remote(
+            shard.at[:, pl.ds(pl.multiple_of(start, 128), piece)],
+            dw.at[rows_at(me, sz.shard), dw_cols(g, tile, 1)],
+            f_sem.at[0, g, i, k],
+            f_sem.at[1, g, i, k],
+            me_r,
+            lax.rem(me + k, n),
+        )
+
+    def fetched(g, i, k):
+        ref = dw.at[dw_rows(k), dw_cols(g, 3 * core + odd + i, 1)]
+        return remote(
+            ref,
+            ref,
+            f_sem.at[0, g, i, k],
+            f_sem.at[1, g, i, k],
+            me_r,
+            lax.rem(me + k, n),
+        )
+
+    def layer(g, k, mine):
+        part = 2 * odd if mine else 2 - 2 * odd
+        ref = dw.at[dw_rows(k), dw_cols(g, 3 * core + part, 1)]
+        return remote(ref, ref, l_sem.at[0, g, k], l_sem.at[1, g, k], partner, me)
+
+    def twin(g, k, late, side):
+        first, count = (2 - 2 * odd, 1) if late else (odd, 2)
+        ref = dw.at[dw_rows(k), dw_cols(g, 3 * side + first, count)]
+        return remote(
+            ref, ref, c_sem.at[0, g, late, k], c_sem.at[1, g, late, k], sibling, me
+        )
+
+    def own_part(g, j):
+        if isinstance(g, int) and g == sz.groups:
+            src = wp_shard.at[:, j * 256 : (j + 1) * 256]
+        else:
+            src = wq_shard.at[:, pl.ds(pl.multiple_of(j * d + g * 256, 128), 256)]
+        dst = dw.at[
+            rows_at(me, sz.shard), pl.ds(pl.multiple_of(g * d + j * 256, 128), 256)
+        ]
+        return pltpu.make_async_copy(src, dst, o_sem.at[g, j])
+
+    def start_weights(g):
+        for k in range(1, n):
+            for i in range(2):
+                fetch(g, i, k).start()
+        for j in range(3):
+            own_part(g, j).start()
+
+    def forward_weights(g):
+        for k in range(1, n):
+            for i in range(2):
+                fetched(g, i, k).wait_recv()
+            layer(g, k, True).start()
+            twin(g, k, 0, core).start()
+
+    def finish_weights(g):
+        for j in range(3):
+            own_part(g, j).wait()
+        for k in range(1, n):
+            layer(g, k, False).wait_recv()
+            twin(g, k, 1, core).start()
+        for k in range(1, n):
+            for late in range(2):
+                twin(g, k, late, 1 - core).wait_recv()
+
+    def drain_weights(g):
+        for k in range(1, n):
+            for i in range(2):
+                fetch(g, i, k).wait_send()
+            layer(g, k, True).wait_send()
+            for late in range(2):
+                twin(g, k, late, core).wait_send()
 
     def small_sends(k):
         return [
@@ -762,7 +772,8 @@
     for k in range(1, n):
         for cp in small_sends(k):
             cp.start()
-    gather_q.start()
+    for g in range(sz.groups):
+        start_weights(g)
     gains[me] = gains_ref[...]
     biases[me] = biases_ref[...]
     routers[me] = router_ref[...]
@@ -796,10 +807,20 @@
     x = mm(pad_matrix(sz), tok_ref[...])
     load_grad.wait()
     gpad[...] = mm(pad_matrix(sz), stage[...]).astype(BF)
-    for e in range(sz.experts):
-        gs[e * sz.slots : (e + 1) * sz.slots, :] = mm(picks(e), gpad[...]).astype(BF)
     slots_me = rows_at(me, sz.slots)
-    dres[slots_me, :] = gs[slots_me, :]
+
+    def at_peer(k):
+        return slice(k * sz.slots, (k + 1) * sz.slots)
+
+    def picks_for(k):
+        line = slot[0:1, :]
+        for e in range(1, sz.experts):
+            line = jnp.where(lax.rem(me + k, n) == e, slot[e : e + 1, :], line)
+        return (slot_ids == line).astype(F32).astype(BF)
+
+    for k in range(n):
+        gs[at_peer(k), :] = mm(picks_for(k), gpad[...]).astype(BF)
+    dres[at_peer(0), :] = gs[at_peer(0), :]
 
     for k in range(1, n):
         for cp in small_sends(k):
@@ -815,23 +836,14 @@
     normed[...] = normalize(x, smf[0:1, :], smf[2:3, :]).astype(BF)
     normed_t[...] = normed[...].T
 
-    gather_q.forward()
-    gather_p.start()
-    gather_q.finish()
-    gather_q.save().start()
-    for j, bias_row in ((0, 3), (1, None), (2, 4)):
-        cols = slice(j * d, (j + 1) * d)
-        value = mm(normed[...], dw[:, cols])
-        if bias_row is not None:
-            value = value + smf[bias_row : bias_row + 1, :]
-        qkv[:, cols] = value.astype(BF)
-    for k in range(1, n):
-        dst = rows_at(lax.rem(me + k, n), sz.slots)
-        to_peer(gs.at[dst, :], dres.at[slots_me, :], g_sem, k).start()
-
     scale = 1.0 / math.sqrt(HEAD_DIM)
     half_lane = iota((sz.seq, 128), 1)
     live = iota((sz.seq, sz.seq), 1) < SEQ
+
+    def pair_cols(pair, j, base=None):
+        group = lax.div(pair, 2) * d if base is None else base
+        start = group + j * 256 + lax.rem(pair, 2) * 128
+        return pl.ds(pl.multiple_of(start, 128), 128)
 
     def save_probs(pair):
         slot = lax.rem(pair, 2)
@@ -844,8 +856,7 @@
 
         for image in range(sz.images):
             rows = slice(image * sz.seq, (image + 1) * sz.seq)
-            at = [pl.ds(pl.multiple_of(j * d + pair * 128, 128), 128) for j in range(3)]
-            q2, k2, v2_ = (qkv[rows, at[j]] for j in range(3))
+            q2, k2, v2_ = (qkv[rows, pair_cols(pair, j)] for j in range(3))
             total = jnp.zeros((sz.seq, 128), F32)
             for half in range(2):
                 mask = (half_lane >= half * 64) & (half_lane < half * 64 + 64)
@@ -856,15 +867,36 @@
                 p = (e / jnp.sum(e, -1, keepdims=True)).astype(BF)
                 pbuf[lax.rem(pair, 2), image * 2 + half] = p
                 total = total + mm(p, jnp.where(mask, v2_, zero))
-            ctx[rows, at[0]] = total.astype(BF)
+            ctx[rows, pl.ds(pl.multiple_of(pair * 128, 128), 128)] = total.astype(BF)
         save_probs(pair).start()
         return carry
 
-    lax.fori_loop(0, sz.pairs, forward_pair, 0)
-
-    gather_p.forward()
-    gather_p.finish()
-    gather_p.save().start()
+    def forward_group(g, carry):
+        finish_weights(g)
+        cols = pl.ds(pl.multiple_of(g * d, 128), d)
+        of_bias = pl.ds(pl.multiple_of(g * 256, 128), 256)
+        bias = jnp.concatenate(
+            [smf[3:4, of_bias], jnp.zeros((1, 256), F32), smf[4:5, of_bias]], 1
+        )
+        qkv[:, cols] = (mm(normed[...], dw[:, cols]) + bias).astype(BF)
+        lax.fori_loop(2 * g, 2 * g + 2, forward_pair, 0)
+
+        @pl.when(g + 2 < sz.groups)
+        def _():
+            forward_weights(g + 2)
+
+        return carry
+
+    forward_weights(0)
+    forward_weights(1)
+    start_weights(sz.groups)
+    for k in range(1, n):
+        to_peer(gs.at[at_peer(k), :], dres.at[at_peer(n - k), :], g_sem, k).start()
+    lax.fori_loop(0, sz.groups, forward_group, 0)
+    forward_weights(sz.groups)
+    finish_weights(sz.groups)
+    save = pltpu.make_async_copy(dw, o_save, wsem.at[2])
+    save.start()
     res = (
         mm(pad_matrix(sz), tok_ref[...])
         + mm(ctx[...], dw[:, 3 * d : 4 * d])
@@ -874,19 +906,14 @@
     second[...] = normalize(res, smf[1:2, :], smf[6:7, :]).astype(BF)
     ctx_t[...] = ctx[...].T
     for k in [*range(1, n), 0]:
-        rows = rows_at(lax.rem(me + k, n), sz.slots)
-        line = slot[0:1, :]
-        for e in range(1, sz.experts):
-            line = jnp.where(lax.rem(me + k, n) == e, slot[e : e + 1, :], line)
-        pick = (slot_ids == line).astype(F32).astype(BF)
-        xs[rows, :] = mm(pick, second[...]).astype(BF)
+        xs[at_peer(k), :] = mm(picks_for(k), second[...]).astype(BF)
         if k:
-            to_peer(xs.at[rows, :], xr.at[slots_me, :], x_sem, k).start()
+            to_peer(xs.at[at_peer(k), :], xr.at[at_peer(n - k), :], x_sem, k).start()
         else:
-            xr[slots_me, :] = xs[slots_me, :]
-    for gather in (gather_q, gather_p):
-        gather.drain()
-        gather.save().wait()
+            xr[at_peer(0), :] = xs[at_peer(0), :]
+    for g in range(sz.groups + 1):
+        drain_weights(g)
+    save.wait()
     load_w1 = pltpu.make_async_copy(w1_hbm, dw, wsem.at[0])
     load_w1.start()
 
@@ -904,8 +931,8 @@
         block = picks(e)
         gates[e] = mm_nt(hi, block) + mm_nt(mid, block) + mm_nt(rest_low, block)
     for k in range(1, n):
-        to_peer(gates.at[lax.rem(me + k, n)], gater.at[me], ga_sem, k).start()
-    gater[me] = gates[me]
+        to_peer(gates.at[lax.rem(me + k, n)], gater.at[n - k], ga_sem, k).start()
+    gater[0] = gates[me]
     logit_cols = mm_nt(low, small_low)
     col = iota((sz.rows, sz.small), 1)
     logit_cols = jnp.where((col >= 8) & (col < 8 + sz.experts), logit_cols, -1e30)
@@ -915,83 +942,104 @@
         save_probs(pair).wait()
 
     lower = 1 - lax.div(z, (nz + 1) // 2)
-    xta = res_send.at[0:d, :]
+    span = 2 * fs
+    per = span // 256
+    everyone, others = slice(0, sz.all_slots), slice(sz.slots, sz.all_slots)
+    square = iota((sz.slots, sz.slots), 0) == iota((sz.slots, sz.slots), 1)
     bias2[...] = jnp.zeros_like(bias2)
-    load_w2.wait()
-    load_w1.wait()
-
-    def w1_part(f):
-        return dw[:, pl.ds(pl.multiple_of(f * fs, 128), fs)]
-
-    square = iota((sz.slots, sz.slots), 0) == iota((sz.slots, sz.slots), 1)
-
-    def peer_slots(k):
-        return rows_at(lax.rem(me + k, n), sz.slots)
-
-    def send_back(k):
-        rows = peer_slots(k)
-        row_send[rows, :] = row_acc[rows, :].astype(BF)
-        out = (res_acc[rows, :] + b2_ref[...].astype(F32)).astype(BF).astype(F32)
-        column = jnp.sum(out * dres[rows, :].astype(F32), 1, keepdims=True)
-        line = jnp.sum(jnp.where(square, column, 0.0), 0, keepdims=True)
-        qs[k] = jnp.broadcast_to(line, (8, sz.slots))
-        if k == 0:
-            bck[slots_me, :] = row_send[rows, :]
-            qr[me] = qs[k]
-        else:
-            to_peer(row_send.at[rows, :], bck.at[slots_me, :], bck_sem, k).start()
-            to_peer(qs.at[k], qr.at[me], q_sem, k).start()
+    half_own = pl.ds(pl.multiple_of(core * fs, 128), fs)
+    half_other = pl.ds(pl.multiple_of((1 - core) * fs, 128), fs)
+
+    def dest_of(i):
+        return lower * (nz - 1 - i) + (1 - lower) * i
+
+    def hidden_at(i, first, size):
+        return pl.ds(pl.multiple_of(dest_of(i) * span + first, 128), size)
 
     def prepare(k):
-        src = lax.rem(me + k, n)
-        rows = rows_at(src, sz.slots)
+        rows = at_peer(k)
         if k:
-            at = n - k
-            to_peer(gs.at[peer_slots(at), :], dres.at[rows, :], g_sem, at).wait()
-            to_peer(gates.at[lax.rem(me + at, n)], gater.at[src], ga_sem, at).wait()
-        row = gater[src, pl.ds(me, 1), :]
+            j = n - k
+            to_peer(gs.at[at_peer(j), :], dres.at[rows, :], g_sem, j).wait()
+            to_peer(gates.at[lax.rem(me + j, n)], gater.at[k], ga_sem, j).wait()
+        row = gater[k, pl.ds(me, 1), :]
         gate = jnp.sum(jnp.where(square, row, 0.0), 1, keepdims=True)
         value = (gate * dres[rows, :].astype(F32)).astype(BF)
         dres[rows, :] = value
         bias2[...] += jnp.sum(value.astype(F32), 0, keepdims=True)
         if k:
-            to_peer(xs.at[peer_slots(at), :], xr.at[rows, :], x_sem, at).wait()
-
-    def compute(f, order, flag, ahead=None, behind=None):
-        w2f_rows = pl.ds(pl.multiple_of(f * fs, 16), fs)
-        bias = b1_ref[:, pl.ds(pl.multiple_of(f * fs, 128), fs)].astype(F32)
-        for k in order:
-            rows = peer_slots(k)
-            if ahead is not None:
-                pl.when(flag)(partial(ahead, k))
-            h = mm(xr[rows, :], w1_part(f)) + bias
-            cdf, pdf = gelu_parts(h)
-            da = mm_nt(dres[rows, :], w2[w2f_rows, :])
-            a = (h * cdf).astype(BF)
-            dh = (da * (cdf + h * pdf)).astype(BF)
-            act[rows, :] = a
-            dhid[rows, :] = dh
-            res_acc[rows, :] += mm(a, w2[w2f_rows, :])
-            row_acc[rows, :] += mm_nt(dh, w1_part(f))
-            if behind is not None:
-                pl.when(flag)(partial(behind, k))
-
-    def grad1(rows):
-        part = mm(xta[rows, :], dhid[0:d, :])
-        return part + mm(xt[rows, :], dhid[d:, :])
-
-    def grad2(cols):
-        return mm_tn(act[:, cols], dres[...])
-
-    def extra():
-        gb = jnp.sum(dhid[...].astype(F32), 0, keepdims=True)
+            to_peer(xs.at[at_peer(j), :], xr.at[rows, :], x_sem, j).wait()
+
+    def cell(t, rows):
+        i, c = lax.div(t, per), lax.rem(t, per)
+        hidden = hidden_at(i, c * 256, 256)
+        here = pl.ds(pl.multiple_of(c * 256, 128), 256)
+        h = mm(xr[rows, :], dw[:, hidden]) + b1_ref[:, hidden].astype(F32)
+        cdf, pdf = gelu_parts(h)
+        da = mm_nt(dres[rows, :], w2[hidden, :])
+        acts[i, rows, here] = (h * cdf).astype(BF)
+        dhids[i, rows, here] = (da * (cdf + h * pdf)).astype(BF)
+
+    def cells(first, last, rows):
+        lax.fori_loop(first * per, last * per, lambda t, c: (cell(t, rows), c)[1], 0)
+
+    def row_copy(c, k, land):
+        cols = pl.ds(pl.multiple_of(c * 256, 128), 256)
+        return remote(
+            row_send.at[at_peer(k), cols],
+            bck.at[land, cols],
+            bck_sem.at[0, c, k],
+            bck_sem.at[1, c, k],
+            me_r,
+            lax.rem(me + k, n),
+        )
+
+    def back_rows(c, carry):
+        cols = pl.ds(pl.multiple_of(c * 256, 128), 256)
+        total = mm_nt(dhids[0], dw[cols, hidden_at(0, 0, span)])
+        for i in range(1, nz):
+            total = total + mm_nt(dhids[i], dw[cols, hidden_at(i, 0, span)])
+        row_send[:, cols] = total.astype(BF)
+        for k in range(1, n):
+            row_copy(c, k, slots_me).start()
+        bck[slots_me, cols] = row_send[at_peer(0), cols]
+        return carry
+
+    def back_results(c, column):
+        cols = pl.ds(pl.multiple_of(c * 256, 128), 256)
+        total = mm(acts[0], w2[hidden_at(0, 0, span), cols])
+        for i in range(1, nz):
+            total = total + mm(acts[i], w2[hidden_at(i, 0, span), cols])
+        out = (total + b2_ref[:, cols].astype(F32)).astype(BF)
+        res_send[:, cols] = out
+        return column + jnp.sum(
+            out.astype(F32) * dres[:, cols].astype(F32), 1, keepdims=True
+        )
+
+    parts1 = [slice(i, i + d // 2) for i in (0, d // 2)]
+    parts2 = range(0, fs, 128)
+
+    def grad1(i, half, rows):
+        part = mm(xta[rows, :], dhids[i, 0:d, half])
+        return part + mm(xt[rows, :], dhids[i, d:, half])
+
+    def grad2(i, start, first):
+        cols = pl.ds(pl.multiple_of(start + first, 128), 128)
+        return mm_tn(acts[i, :, cols], dres[...])
+
+    def extra(i, half):
+        gb = jnp.sum(dhids[i, :, half].astype(F32), 0, keepdims=True)
         row = iota((16, d), 0)
         line = jnp.concatenate([gb, jnp.zeros((1, d - fs), F32)], 1)
         return jnp.where(row == 0, line, jnp.where(row == 1, bias2[...], 0.0))
 
-    def t_copies(dest):
+    def leaving(i):
+        return r2.at[0] if isinstance(i, int) else acts.at[i, 0:d, half_other]
+
+    def t_copies(i):
+        dest = dest_of(i)
         return (
-            remote(t1, v1.at[dest], t_sem.at[0, 0, dest], t_sem.at[1, 0, dest], sibling, me),
+            remote(leaving(i), v1.at[dest], t_sem.at[0, 0, dest], t_sem.at[1, 0, dest], sibling, me),
             remote(t2, v2.at[dest], t_sem.at[0, 1, dest], t_sem.at[1, 1, dest], sibling, me),
         )
 
@@ -1006,64 +1054,79 @@
             remote(src2, u2.at[slot], u_sem.at[0, 1, way, step], u_sem.at[1, 1, way, step], target, me),
         )
 
-    res_acc[...] = jnp.zeros_like(res_acc)
-    row_acc[...] = jnp.zeros_like(row_acc)
-
-    parts1 = [slice(i, i + d // 2) for i in (0, d // 2)]
-    parts2 = [slice(i, i + 128) for i in range(0, fs, 128)]
-
-    def dest_of(i):
-        return lower * (nz - 1 - i) + (1 - lower) * i
-
-    def slice_step(i, carry):
-        dest = dest_of(i)
-
-        compute(dest * 2 + 1 - core, range(n), i == 0, prepare)
-
-        @pl.when(i == 0)
-        def _():
+    def other_grads(i):
+        for first in parts2:
+            value = grad2(i, (1 - core) * fs, first)
+            t2[first : first + 128, :] = value.astype(BF)
+        t2[fs:, :] = extra(i, half_other).astype(BF)
+        t_copies(i)[1].start()
+        if isinstance(i, int):
             xta[...] = xr[0:d, :].T
             xt[...] = xr[d:, :].T
-
         for rows in parts1:
-            t1[rows, :] = grad1(rows).astype(BF)
-        for rows in parts2:
-            t2[rows, :] = grad2(rows).astype(BF)
-        t2[fs:, :] = extra().astype(BF)
-        for cp in t_copies(dest):
-            cp.start()
-        compute(dest * 2 + core, [*range(1, n), 0], i == nz - 1, None, send_back)
-        for cp in t_copies(dest):
-            cp.wait()
+            leaving(i)[rows, :] = grad1(i, half_other, rows).astype(BF)
+        t_copies(i)[0].start()
+
+    def own_grads(i):
+        dest = dest_of(i)
+        t_copies(i)[1].wait()
+        for first in parts2:
+            rows = slice(first, first + 128)
+            value = v2[dest, rows, :].astype(F32) + grad2(i, core * fs, first)
+            v2[dest, rows, :] = value.astype(BF)
+        v2[dest, fs:, :] = (v2[dest, fs:, :].astype(F32) + extra(i, half_own)).astype(BF)
+        leave(i, 1)
+        t_copies(i)[0].wait()
         for rows in parts1:
-            v1[dest, rows, :] = (v1[dest, rows, :].astype(F32) + grad1(rows)).astype(BF)
-        for rows in parts2:
-            v2[dest, rows, :] = (v2[dest, rows, :].astype(F32) + grad2(rows)).astype(BF)
-        v2[dest, fs:, :] = (v2[dest, fs:, :].astype(F32) + extra()).astype(BF)
+            value = v1[dest, rows, :].astype(F32) + grad1(i, half_own, rows)
+            v1[dest, rows, :] = value.astype(BF)
+        leave(i, 0)
+
+    def leave(i, which):
+        dest = dest_of(i)
 
         @pl.when((z == 0) & (i <= nz - 2))
         def _():
-            for cp in u_copies(v1.at[dest], v2.at[dest], 0, i, me_r + 2, dest):
-                cp.start()
+            u_copies(v1.at[dest], v2.at[dest], 0, i, me_r + 2, dest)[which].start()
 
         @pl.when((z == nz - 1) & (i < nz - 2))
         def _():
-            for cp in u_copies(v1.at[dest], v2.at[dest], 1, i, me_r - 2, dest):
-                cp.start()
+            u_copies(v1.at[dest], v2.at[dest], 1, i, me_r - 2, dest)[which].start()
 
         @pl.when((z == nz - 1) & (i == nz - 2))
         def _():
-            for cp in u_copies(v1.at[dest], v2.at[dest], 1, i, me_r - 2, nz):
-                cp.start()
-
+            u_copies(v1.at[dest], v2.at[dest], 1, i, me_r - 2, nz)[which].start()
+
+    prepare(0)
+    load_w2.wait()
+    load_w1.wait()
+    cells(0, nz, at_peer(0))
+    for k in range(1, n):
+        prepare(k)
+    cells(0, 1, others)
+    other_grads(0)
+    own_grads(0)
+    cells(1, nz, others)
+    lax.fori_loop(0, d // 256, back_rows, 0)
+    column = lax.fori_loop(
+        0, d // 256, back_results, jnp.zeros((sz.all_slots, 1), F32)
+    )
+    for k in range(n):
+        line = jnp.where(square, column[at_peer(k), :], 0.0)
+        qs[k] = jnp.broadcast_to(jnp.sum(line, 0, keepdims=True), (8, sz.slots))
+    qr[me] = qs[0]
+    ret[slots_me, :] = res_send[at_peer(0), :]
+    for k in range(1, n):
+        to_peer(qs.at[k], qr.at[me], q_sem, k).start()
+    for k in range(1, n):
+        to_peer(res_send.at[at_peer(k), :], ret.at[slots_me, :], ret_sem, k).start()
+
+    def slice_step(i, carry):
+        other_grads(i)
+        own_grads(i)
         return carry
 
-    lax.fori_loop(0, nz, slice_step, 0)
-
-    res_send[...] = (res_acc[...] + b2_ref[...].astype(F32)).astype(BF)
-    for k in range(1, n):
-        to_peer(res_send.at[peer_slots(k), :], ret.at[slots_me, :], ret_sem, k).start()
-    ret[slots_me, :] = res_send[slots_me, :]
+    lax.fori_loop(1, nz, slice_step, 0)
     dense_load = pltpu.make_async_copy(o_save, dw, wsem.at[0])
     dense_load.start()
 
@@ -1090,11 +1153,10 @@
 
     for k in range(1, n):
         src = lax.rem(me + n - k, n)
-        theirs = rows_at(src, sz.slots)
-        to_peer(row_send.at[peer_slots(k), :], bck.at[theirs, :], bck_sem, k).wait()
+        for c in range(d // 256):
+            row_copy(c, k, rows_at(src, sz.slots)).wait()
         to_peer(qs.at[k], qr.at[src], q_sem, k).wait()
-    mixed = res_acc.at[0 : sz.rows, :]
-    sgrad = res_acc.at[sz.rows : 2 * sz.rows, :]
+    mixed = sgrad = wide2
     lane = iota((sz.rows, sz.small), 1)
     weighted = jnp.zeros((sz.rows, sz.small), F32)
     for e in range(sz.experts):
@@ -1106,7 +1168,7 @@
     for e in range(sz.experts):
         sgrad[...] += mm(comb[e], bck[e * sz.slots : (e + 1) * sz.slots, :])
     back2, gain2, shift2 = normalize_back(resid[...], smf[1:2, :], sgrad[...])
-    rgrad = row_acc.at[0 : sz.rows, :]
+    rgrad = wide1
     rgrad[...] = gpad[...].astype(F32) + back2
     low = rgrad[...].astype(BF)
     bias_out = jnp.sum(low.astype(F32), 0, keepdims=True)
@@ -1123,10 +1185,14 @@
     def part_rows(zi):
         return pl.ds(pl.multiple_of(zi * part, 16), part)
 
+    def parked(j):
+        cols = pl.ds(pl.multiple_of(lax.rem(j, 2) * wide, 128), wide)
+        return acts.at[lax.div(j, 2), 0:d, cols]
+
     def to_sibling(j):
         return remote(
             dense.at[chunk_rows(j, 0, d), give],
-            r1.at[j],
+            parked(j),
             d1_sem.at[0, j],
             d1_sem.at[1, j],
             sibling,
@@ -1137,7 +1203,7 @@
         e = lax.rem(me + k, n)
         return remote(
             dense.at[chunk_rows(j, e * sz.shard, sz.shard), keep],
-            r2.at[k - 1, j],
+            r2.at[k - 1, pl.ds(pl.multiple_of(j * sz.shard, 16), sz.shard), :],
             d2_sem.at[0, j, k],
             d2_sem.at[1, j, k],
             me_r,
@@ -1172,7 +1238,7 @@
     def stage1(j):
         to_sibling(j).wait()
         rows = chunk_rows(j, 0, d)
-        dense[rows, keep] = (dense[rows, keep].astype(F32) + r1[j].astype(F32)).astype(BF)
+        dense[rows, keep] = (dense[rows, keep].astype(F32) + parked(j)[...].astype(F32)).astype(BF)
         for k in range(1, n):
             to_owner(j, k).start()
 
@@ -1180,7 +1246,7 @@
         acc = dense[chunk_rows(j, me * sz.shard, sz.shard), keep].astype(F32)
         for k in range(1, n):
             to_owner(j, k).wait()
-            acc = acc + r2[k - 1, j].astype(F32)
+            acc = acc + r2[k - 1, j * sz.shard : (j + 1) * sz.shard, :].astype(F32)
         z1[j] = acc.astype(BF)
         for k in range(1, nz):
             to_layer(j, k).start()
@@ -1209,12 +1275,8 @@
     dense_load.wait()
     for k in range(1, n):
         theirs = rows_at(lax.rem(me + n - k, n), sz.slots)
-        to_peer(res_send.at[peer_slots(k), :], ret.at[theirs, :], ret_sem, k).wait()
-    dq_ref = res_send.at[0 : sz.rows, :]
-    dk_ref = res_send.at[sz.rows : 2 * sz.rows, :]
-    dv_ref = row_send.at[0 : sz.rows, :]
-    cgrad = row_send.at[sz.rows : 2 * sz.rows, :]
-    dqkv = (dq_ref, dk_ref, dv_ref)
+        to_peer(res_send.at[at_peer(k), :], ret.at[theirs, :], ret_sem, k).wait()
+    cgrad = sends.at[3 * sz.rows : 4 * sz.rows, :]
 
     def load_probs(pair):
         slot = lax.rem(pair, 2)
@@ -1224,9 +1286,6 @@
     cgrad[...] = mm_nt(low, dw[:, 3 * d : 4 * d]).astype(BF)
     sm[...] = mm_tn(logit_low, second[...])
 
-    for s in range(2, nz - 1):
-        z_round(s)
-
     scale = 1.0 / math.sqrt(HEAD_DIM)
     half_lane = iota((sz.seq, 128), 1)
 
@@ -1239,9 +1298,11 @@
 
         for image in range(sz.images):
             rows = slice(image * sz.seq, (image + 1) * sz.seq)
-            at = [pl.ds(pl.multiple_of(j * d + pair * 128, 128), 128) for j in range(3)]
-            q2, k2, v2_ = (qkv[rows, at[j]] for j in range(3))
-            c2 = cgrad[rows, at[0]]
+            q2, k2, v2_ = (qkv[rows, pair_cols(pair, j)] for j in range(3))
+            c2 = cgrad[rows, pl.ds(pl.multiple_of(pair * 128, 128), 128)]
+            there = pl.ds(
+                pl.multiple_of(lax.div(pair, 2) * sz.rows + image * sz.seq, 16), sz.seq
+            )
             dq = jnp.zeros((sz.seq, 128), F32)
             dk = jnp.zeros((sz.seq, 128), F32)
             dv = jnp.zeros((sz.seq, 128), F32)
@@ -1257,37 +1318,42 @@
                 ds = (p32 * (pb - mix)).astype(BF)
                 dq = dq + mm(ds, jnp.where(mask, k2, zero))
                 dk = dk + mm_tn(ds, jnp.where(mask, q2, zero))
-            dq_ref[rows, at[0]] = (dq * scale).astype(BF)
-            dk_ref[rows, at[0]] = (dk * scale).astype(BF)
-            dv_ref[rows, at[0]] = dv.astype(BF)
+            sends[there, pair_cols(pair, 0, 0)] = (dq * scale).astype(BF)
+            sends[there, pair_cols(pair, 1, 0)] = (dk * scale).astype(BF)
+            sends[there, pair_cols(pair, 2, 0)] = dv.astype(BF)
         return carry
 
     def group_step(g, carry):
         lax.fori_loop(2 * g, 2 * g + 2, pair_step, 0)
-        cols = pl.ds(pl.multiple_of(g * 256, 128), 256)
-        for j in range(3):
-            dense[chunk_rows(g + 1, 0, d), j * 256 : (j + 1) * 256] = mm(
-                normed_t[...], dqkv[j][:, cols]
-            ).astype(BF)
+        dense[chunk_rows(g + 1, 0, d), :] = mm(
+            normed_t[...], sends[rows_at(g, sz.rows), :]
+        ).astype(BF)
         to_sibling(g + 1).start()
         stage1(g)
         return carry
 
     lax.fori_loop(0, sz.groups, group_step, 0)
+    for s in range(2, nz - 1):
+        z_round(s)
     stage1(sz.groups)
 
     ngrad = sgrad
-    ngrad[...] = mm_nt(dq_ref[...], dw[:, 0:d])
-    for j in range(1, 3):
-        ngrad[...] += mm_nt(dqkv[j][...], dw[:, j * d : (j + 1) * d])
+    ngrad[...] = mm_nt(sends[0 : sz.rows, :], dw[:, 0:d])
+    for g in range(1, sz.groups):
+        grads = sends[g * sz.rows : (g + 1) * sz.rows, :]
+        ngrad[...] += mm_nt(grads, dw[:, g * d : (g + 1) * d])
     stage2(0)
     x = mm(pad_matrix(sz), tok_ref[...])
     back1, gain1, shift1 = normalize_back(x, smf[0:1, :], ngrad[...])
     stage[...] = mm(unpad_matrix(sz), (rgrad[...] + back1).astype(BF)).astype(BF)
     store = pltpu.make_async_copy(stage, o_gin, wsem.at[2])
     store.start()
-    bias_q = jnp.sum(dq_ref[...].astype(F32), 0, keepdims=True)
-    bias_v = jnp.sum(dv_ref[...].astype(F32), 0, keepdims=True)
+    sums = [
+        jnp.sum(sends[g * sz.rows : (g + 1) * sz.rows, :].astype(F32), 0, keepdims=True)
+        for g in range(sz.groups)
+    ]
+    bias_q = jnp.concatenate([total[:, 0:256] for total in sums], 1)
+    bias_v = jnp.concatenate([total[:, 512:768] for total in sums], 1)
     row = iota((sz.small, d), 0)
     small = sm[...]
     for i, value in enumerate((gain1, gain2, shift1, bias_q, bias_v, bias_out, shift2)):
@@ -1421,25 +1487,23 @@
         ((n, *biases.shape), BF),
         ((1, d), F32),
         ((d, slots - d), BF),
-        ((slots, fs), BF),
-        ((slots, fs), BF),
-        ((slots, d), F32),
-        ((slots, d), F32),
-        ((slots, d), BF),
-        ((slots, d), BF),
+        ((d, d), BF),
+        ((nz, slots, 2 * fs), BF),
+        ((nz, slots, 2 * fs), BF),
+        ((rows, d), F32),
+        ((rows, d), F32),
+        ((2 * slots, d), BF),
         ((slots, d), BF),
         ((slots, d), BF),
         ((n, 8, sz.slots), F32),
         ((n, 8, sz.slots), F32),
-        ((d, fs), BF),
         ((sz.fs_rows, d), BF),
         ((nz, d, fs), BF),
         ((nz, sz.fs_rows, d), BF),
         ((nz + 1, d, fs), BF),
         ((nz + 1, sz.fs_rows, d), BF),
         ((2, 2 * sz.images, sz.seq, sz.seq), BF),
-        ((sz.chunks, d, half), BF),
-        ((n - 1, sz.chunks, sz.shard, half), BF),
+        ((n - 1, d, half), BF),
         ((sz.chunks, sz.shard, half), BF),
         ((nz - 1, sz.chunks, sz.part, half), BF),
         ((sz.small, d), F32),
@@ -1450,12 +1514,12 @@
     ]
     sems = (
         [dma((4,)), dma((2,))]
-        + [dma((2, n))] * 4
-        + [dma((2, 2, n))] * 2
+        + [dma((2, sz.chunks, 2, n)), dma((2, sz.chunks, n))]
+        + [dma((2, sz.chunks, 2, n)), dma((sz.chunks, 3))]
         + [dma((3, 2, n))]
         + [dma((2, n))] * 3
         + [dma((2, 2, nz)), dma((2, 2, 2, nz - 1))]
-        + [dma((2, n))] * 3
+        + [dma((2, n)), dma((2, d // 256, n)), dma((2, n))]
         + [dma((2, sz.chunks)), dma((2, sz.chunks, n))]
         + [dma((2, sz.chunks, nz))] * 2
         + [dma((2, sz.chunks)), dma((2,)), dma((2, n)), dma((2, nz))]

time: 205 us -> 193 us (0.941)
  Pallas kernels: 204 us -> 192 us
    pallas_call x1, Pallas kernels: 200 us -> 188 us  [block(): pl.pallas_call(partial(block_kernel, sz), name='block', out_shape=[jax.Sh...]
where the time goes in v4:
time: 193 us
  Pallas kernels  192 us (99%)
    pallas_call x1, Pallas kernels, block(): pl.pallas_call(partial(block_kernel, sz), name='block', out_shape=[jax.Sh...  188 us
    pallas_call x1, Pallas kernels, finish(): pl.pallas_call(partial(finish_kernel, sz), name='finish', out_shape=[jax....  4.65 us

profile of v4, /device:TPU:0, one launch (start us, length us, event | category | flops | bytes accessed | tf_op | source)
XLA Modules:
  0.0 193.1 jit_solution(6714421935536230084)
XLA Ops:
  0.6 187.6 %block.1 = (bf16[4,192,768]{2,1,0:T(8,128)(2,1)}, f32[16,256]{1,0:T(8,128)}, bf16[394,768]{1,0:T(8,128)(2,1)}, bf16[394,768]{1,0:T(8,128)(2,1)}, bf16[768,384]{1...) custom-call(bf16[394,768]{1,0:T(8,128)(2,1)} %tok_ref.1, ...), custom_call_target="tpu_custom_call" | custom-call | tf_op jit(solution)/shard_map/block/pallas_call | solution.py:1527
  188.2 4.6 %finish.1 = (bf16[394,768]{1,0:T(8,128)(2,1)}, bf16[394,768]{1,0:T(8,128)(2,1)}, f32[192,2304]{1,0:T(8,128)}, f32[192,768]{1,0:T(8,128)}, f32[4,192]{1,0:T(4,128...) custom-call(bf16[394,768]{1,0:T(8,128)(2,1)} %get-tuple-element.28.o, ...), custom_call_target="tpu_custom_call" | custom-call | tf_op jit(solution)/shard_map/finish/pallas_call | solution.py:492

commit v5 on v4

--- a/solution.py
+++ b/solution.py
@@ -68,7 +68,6 @@
         self.nz = self.n_rep // 2
         self.fs = ff // self.n_rep
         self.fs_rows = self.fs + 16
-        self.part = self.shard // self.nz
         self.groups = self.pairs // 2
         self.chunks = self.groups + 1
 
@@ -527,13 +526,13 @@
 
 def block_kernel(
     sz,
-    tok_ref,
-    routes_ref,
+    tok_hbm,
+    routes_hbm,
     router_ref,
     gains_ref,
     biases_ref,
-    b1_ref,
-    b2_ref,
+    b1_hbm,
+    b2_hbm,
     grad_hbm,
     wq_shard,
     wp_shard,
@@ -547,6 +546,11 @@
     o_w2,
     o_probs,
     o_save,
+    tok_ref,
+    routes_ref,
+    b1_ref,
+    b2_ref,
+    od,
     dw,
     w2,
     stage,
@@ -592,6 +596,7 @@
     sme,
     sme_r,
     smz_r,
+    isem,
     wsem,
     psem,
     f_sem,
@@ -625,6 +630,22 @@
     odd = lax.rem(z, 2)
     partner = me_r + 2 - 4 * odd
 
+    loads = [
+        pltpu.make_async_copy(src, dst, isem.at[i])
+        for i, (src, dst) in enumerate(
+            (
+                (tok_hbm, tok_ref),
+                (gains_ref, gains.at[me]),
+                (biases_ref, biases.at[me]),
+                (router_ref, routers.at[me]),
+                (routes_hbm, routes_ref),
+                (b1_hbm, b1_ref),
+                (b2_hbm, b2_ref),
+            )
+        )
+    ]
+    for cp in loads:
+        cp.start()
     load_grad = pltpu.make_async_copy(grad_hbm, stage, wsem.at[0])
     load_grad.start()
     load_w2 = pltpu.make_async_copy(w2_hbm, w2, wsem.at[1])
@@ -665,8 +686,8 @@
             src, dst, sems.at[0, k], sems.at[1, k], lax.rem(me_r + 2 * k, 2 * nz), me
         )
 
-    normed = bck.at[0 : sz.rows, :]
-    ctx = bck.at[sz.rows : 2 * sz.rows, :]
+    normed = acts.at[nz - 1, sz.slots : sz.slots + sz.rows, :]
+    ctx = xta.at[0 : sz.rows, :]
     res_send = sends.at[0 : sz.all_slots, :]
     row_send = sends.at[sz.all_slots : 2 * sz.all_slots, :]
     xs, gs = res_send, row_send
@@ -772,12 +793,25 @@
     for k in range(1, n):
         for cp in small_sends(k):
             cp.start()
-    for g in range(sz.groups):
+    for g in range(sz.groups + 1):
         start_weights(g)
-    gains[me] = gains_ref[...]
-    biases[me] = biases_ref[...]
-    routers[me] = router_ref[...]
-
+    loads[0].wait()
+    wide1[...] = mm(pad_matrix(sz), tok_ref[...])
+    for cp in loads[1:]:
+        cp.wait()
+    for k in range(1, n):
+        for cp in small_sends(k):
+            cp.wait_recv()
+    smf[...] = jnp.zeros_like(smf)
+    for j in range(n):
+        r = iota((sz.shard, d), 0)
+        c = iota((sz.shard, d), 1)
+        pick = (c == r + j * sz.shard).astype(F32).astype(BF)
+        smf[0:2, :] += mm(gains[j], pick)
+        smf[2:7, :] += mm(biases[j], pick)
+        smf[8 : 8 + sz.experts, :] += mm(routers[j], pick)
+    normed[...] = normalize(wide1[...], smf[0:1, :], smf[2:3, :]).astype(BF)
+    forward_weights(0)
     choice = (routes_ref[...].astype(F32) + 1.0).astype(BF)
     lines = mm_nt(choice, pad_matrix(sz)).astype(jnp.int32) - 1
     ids = iota((sz.ep, sz.rows), 0)
@@ -798,13 +832,8 @@
     def picks(e):
         return (slot_ids == slot[e : e + 1, :]).astype(F32).astype(BF)
 
-    eye = (iota((sz.rows, sz.rows), 0) == iota((sz.rows, sz.rows), 1)).astype(F32)
-    slot_cols = mm_nt(eye.astype(BF), slot.astype(F32).astype(BF)).astype(jnp.int32)
-    lane_ids = iota((sz.rows, sz.slots), 1)
-    for e in range(sz.experts):
-        comb[e] = (slot_cols[:, e : e + 1] == lane_ids).astype(F32).astype(BF)
-
-    x = mm(pad_matrix(sz), tok_ref[...])
+    forward_weights(1)
+
     load_grad.wait()
     gpad[...] = mm(pad_matrix(sz), stage[...]).astype(BF)
     slots_me = rows_at(me, sz.slots)
@@ -821,20 +850,9 @@
     for k in range(n):
         gs[at_peer(k), :] = mm(picks_for(k), gpad[...]).astype(BF)
     dres[at_peer(0), :] = gs[at_peer(0), :]
-
-    for k in range(1, n):
-        for cp in small_sends(k):
-            cp.wait_recv()
-    smf[...] = jnp.zeros_like(smf)
-    for j in range(n):
-        r = iota((sz.shard, d), 0)
-        c = iota((sz.shard, d), 1)
-        pick = (c == r + j * sz.shard).astype(F32).astype(BF)
-        smf[0:2, :] += mm(gains[j], pick)
-        smf[2:7, :] += mm(biases[j], pick)
-        smf[8 : 8 + sz.experts, :] += mm(routers[j], pick)
-    normed[...] = normalize(x, smf[0:1, :], smf[2:3, :]).astype(BF)
-    normed_t[...] = normed[...].T
+    forward_weights(2)
+    for k in range(1, n):
+        to_peer(gs.at[at_peer(k), :], dres.at[at_peer(n - k), :], g_sem, k).start()
 
     scale = 1.0 / math.sqrt(HEAD_DIM)
     half_lane = iota((sz.seq, 128), 1)
@@ -861,10 +879,10 @@
             for half in range(2):
                 mask = (half_lane >= half * 64) & (half_lane < half * 64 + 64)
                 zero = jnp.zeros_like(q2)
-                s = mm_nt(jnp.where(mask, q2, zero), k2) * scale
+                s = mm_nt(jnp.where(mask, q2 * jnp.asarray(scale, BF), zero), k2)
                 s = jnp.where(live, s, -1e30)
                 e = jnp.exp(s - jnp.max(s, -1, keepdims=True))
-                p = (e / jnp.sum(e, -1, keepdims=True)).astype(BF)
+                p = (e * (1.0 / jnp.sum(e, -1, keepdims=True))).astype(BF)
                 pbuf[lax.rem(pair, 2), image * 2 + half] = p
                 total = total + mm(p, jnp.where(mask, v2_, zero))
             ctx[rows, pl.ds(pl.multiple_of(pair * 128, 128), 128)] = total.astype(BF)
@@ -881,42 +899,29 @@
         qkv[:, cols] = (mm(normed[...], dw[:, cols]) + bias).astype(BF)
         lax.fori_loop(2 * g, 2 * g + 2, forward_pair, 0)
 
-        @pl.when(g + 2 < sz.groups)
+        @pl.when(g == 0)
         def _():
-            forward_weights(g + 2)
+            forward_weights(sz.groups)
 
         return carry
 
-    forward_weights(0)
-    forward_weights(1)
-    start_weights(sz.groups)
-    for k in range(1, n):
-        to_peer(gs.at[at_peer(k), :], dres.at[at_peer(n - k), :], g_sem, k).start()
     lax.fori_loop(0, sz.groups, forward_group, 0)
-    forward_weights(sz.groups)
     finish_weights(sz.groups)
     save = pltpu.make_async_copy(dw, o_save, wsem.at[2])
     save.start()
     res = (
-        mm(pad_matrix(sz), tok_ref[...])
+        wide1[...]
         + mm(ctx[...], dw[:, 3 * d : 4 * d])
         + smf[5:6, :]
     )
     resid[...] = res
     second[...] = normalize(res, smf[1:2, :], smf[6:7, :]).astype(BF)
-    ctx_t[...] = ctx[...].T
     for k in [*range(1, n), 0]:
         xs[at_peer(k), :] = mm(picks_for(k), second[...]).astype(BF)
         if k:
             to_peer(xs.at[at_peer(k), :], xr.at[at_peer(n - k), :], x_sem, k).start()
         else:
             xr[at_peer(0), :] = xs[at_peer(0), :]
-    for g in range(sz.groups + 1):
-        drain_weights(g)
-    save.wait()
-    load_w1 = pltpu.make_async_copy(w1_hbm, dw, wsem.at[0])
-    load_w1.start()
-
     small_low = smf[...].astype(BF)
     low = second[...]
     logit_rows = mm_nt(small_low, low)[8 : 8 + sz.ep, :]
@@ -933,6 +938,18 @@
     for k in range(1, n):
         to_peer(gates.at[lax.rem(me + k, n)], gater.at[n - k], ga_sem, k).start()
     gater[0] = gates[me]
+    for g in range(sz.groups + 1):
+        drain_weights(g)
+    save.wait()
+    load_w1 = pltpu.make_async_copy(w1_hbm, dw, wsem.at[0])
+    load_w1.start()
+    normed_t[...] = normed[...].T
+    ctx_t[...] = ctx[...].T
+    eye = (iota((sz.rows, sz.rows), 0) == iota((sz.rows, sz.rows), 1)).astype(F32)
+    slot_cols = mm_nt(eye.astype(BF), slot.astype(F32).astype(BF)).astype(jnp.int32)
+    lane_ids = iota((sz.rows, sz.slots), 1)
+    for e in range(sz.experts):
+        comb[e] = (slot_cols[:, e : e + 1] == lane_ids).astype(F32).astype(BF)
     logit_cols = mm_nt(low, small_low)
     col = iota((sz.rows, sz.small), 1)
     logit_cols = jnp.where((col >= 8) & (col < 8 + sz.experts), logit_cols, -1e30)
@@ -967,8 +984,6 @@
         value = (gate * dres[rows, :].astype(F32)).astype(BF)
         dres[rows, :] = value
         bias2[...] += jnp.sum(value.astype(F32), 0, keepdims=True)
-        if k:
-            to_peer(xs.at[at_peer(j), :], xr.at[rows, :], x_sem, j).wait()
 
     def cell(t, rows):
         i, c = lax.div(t, per), lax.rem(t, per)
@@ -1097,12 +1112,31 @@
         def _():
             u_copies(v1.at[dest], v2.at[dest], 1, i, me_r - 2, nz)[which].start()
 
+    def z_round(s, which):
+        v, u = ((v1, u1), (v2, u2))[which]
+        for way in range(2):
+            zz = z if way == 0 else nz - 1 - z
+            dest = nz - 1 - s + zz if way == 0 else z - (nz - 1 - s)
+            target = me_r + 2 if way == 0 else me_r - 2
+
+            @pl.when((zz >= 1) & (zz <= s))
+            def _():
+                here = landing(way, s - 1, z)
+                there = landing(way, s, z + 1 if way == 0 else z - 1)
+                at_here, at_there = (u1.at[here], u2.at[here]), there
+                u_copies(*at_here, way, s - 1, target, here)[which].wait_recv()
+                u[here] = (u[here].astype(F32) + v[dest].astype(F32)).astype(BF)
+                u_copies(*at_here, way, s, target, at_there)[which].start()
+
     prepare(0)
     load_w2.wait()
     load_w1.wait()
     cells(0, nz, at_peer(0))
     for k in range(1, n):
         prepare(k)
+    for k in range(1, n):
+        to_peer(xs.at[at_peer(k), :], xr.at[at_peer(n - k), :], x_sem, k).wait_send()
+        to_peer(xs.at[at_peer(n - k), :], xr.at[at_peer(k), :], x_sem, n - k).wait_recv()
     cells(0, 1, others)
     other_grads(0)
     own_grads(0)
@@ -1126,30 +1160,13 @@
         own_grads(i)
         return carry
 
+    if nz > 2:
+        z_round(1, 1)
     lax.fori_loop(1, nz, slice_step, 0)
+    if nz > 2:
+        z_round(1, 0)
     dense_load = pltpu.make_async_copy(o_save, dw, wsem.at[0])
     dense_load.start()
-
-    def z_round(s):
-        for way in range(2):
-            zz = z if way == 0 else nz - 1 - z
-            dest = nz - 1 - s + zz if way == 0 else z - (nz - 1 - s)
-            target = me_r + 2 if way == 0 else me_r - 2
-
-            @pl.when((zz >= 1) & (zz <= s))
-            def _():
-                here = landing(way, s - 1, z)
-                there = landing(way, s, z + 1 if way == 0 else z - 1)
-                a1, a2 = u1.at[here], u2.at[here]
-                for cp in u_copies(a1, a2, way, s - 1, target, here):
-                    cp.wait_recv()
-                u1[here] = (u1[here].astype(F32) + v1[dest].astype(F32)).astype(BF)
-                u2[here] = (u2[here].astype(F32) + v2[dest].astype(F32)).astype(BF)
-                for cp in u_copies(a1, a2, way, s, target, there):
-                    cp.start()
-
-    if nz > 2:
-        z_round(1)
 
     for k in range(1, n):
         src = lax.rem(me + n - k, n)
@@ -1177,13 +1194,9 @@
     wide = d // 2
     keep = pl.ds(pl.multiple_of(core * wide, 128), wide)
     give = pl.ds(pl.multiple_of((1 - core) * wide, 128), wide)
-    part = sz.part
 
     def chunk_rows(j, start, size):
         return pl.ds(pl.multiple_of(j * d + start, 16), size)
-
-    def part_rows(zi):
-        return pl.ds(pl.multiple_of(zi * part, 16), part)
 
     def parked(j):
         cols = pl.ds(pl.multiple_of(lax.rem(j, 2) * wide, 128), wide)
@@ -1210,29 +1223,25 @@
             e,
         )
 
-    def to_layer(j, k):
+    outer = (z == 0) | (z == nz - 1)
+    across = me_r - 2 + 4 * odd
+
+    def inward(j):
         return remote(
-            z1.at[j, part_rows(lax.rem(z + k, nz)), :],
-            z2.at[k - 1, j],
-            z1_sem.at[0, j, k],
-            z1_sem.at[1, j, k],
-            lax.rem(me_r + 2 * k, 2 * nz),
-            me,
-        )
-
-    def from_layer(j, k, owner):
-        piece = o_dense.at[j, part_rows(owner), keep]
+            z1.at[j], z2.at[0, j], z1_sem.at[0, 0, j], z1_sem.at[1, 0, j], partner, me
+        )
+
+    def swap(j):
         return remote(
-            piece,
-            piece,
-            z2_sem.at[0, j, k],
-            z2_sem.at[1, j, k],
-            lax.rem(me_r + 2 * k, 2 * nz),
-            me,
-        )
+            z1.at[j], z2.at[1, j], z1_sem.at[0, 1, j], z1_sem.at[1, 1, j], across, me
+        )
+
+    def outward(j):
+        piece = od.at[j, :, keep]
+        return remote(piece, piece, z2_sem.at[0, j], z2_sem.at[1, j], partner, me)
 
     def to_twin(j, cols):
-        piece = o_dense.at[j, :, cols]
+        piece = od.at[j, :, cols]
         return remote(piece, piece, z3_sem.at[0, j], z3_sem.at[1, j], sibling, me)
 
     def stage1(j):
@@ -1248,27 +1257,35 @@
             to_owner(j, k).wait()
             acc = acc + r2[k - 1, j * sz.shard : (j + 1) * sz.shard, :].astype(F32)
         z1[j] = acc.astype(BF)
-        for k in range(1, nz):
-            to_layer(j, k).start()
+        pl.when(outer)(lambda: inward(j).start())
 
     def stage3(j):
-        acc = z1[j, part_rows(z), :].astype(F32)
-        for k in range(1, nz):
-            to_layer(j, k).wait()
-            acc = acc + z2[k - 1, j].astype(F32)
-        o_dense[j, part_rows(z), keep] = acc.astype(BF)
-        for k in range(1, nz):
-            from_layer(j, k, z).start()
+        @pl.when(jnp.logical_not(outer))
+        def _():
+            inward(j).wait_recv()
+            z1[j] = (z1[j].astype(F32) + z2[0, j].astype(F32)).astype(BF)
+            swap(j).start()
 
     def stage4(j):
-        for k in range(1, nz):
-            from_layer(j, k, z).wait_send()
-            from_layer(j, k, lax.rem(z + nz - k, nz)).wait_recv()
-        to_twin(j, keep).start()
+        @pl.when(jnp.logical_not(outer))
+        def _():
+            swap(j).wait()
+            od[j, :, keep] = (z1[j].astype(F32) + z2[1, j].astype(F32)).astype(BF)
+            outward(j).start()
+            to_twin(j, keep).start()
 
     def stage5(j):
+        @pl.when(outer)
+        def _():
+            inward(j).wait_send()
+            outward(j).wait_recv()
+            to_twin(j, keep).start()
+
+    def stage6(j):
+        pl.when(jnp.logical_not(outer))(lambda: outward(j).wait_send())
         to_twin(j, keep).wait_send()
         to_twin(j, give).wait_recv()
+        pltpu.make_async_copy(od.at[j], o_dense.at[j], isem.at[j]).start()
 
     dense[chunk_rows(0, 0, d), :] = mm(ctx_t[...], low).astype(BF)
     to_sibling(0).start()
@@ -1334,7 +1351,8 @@
 
     lax.fori_loop(0, sz.groups, group_step, 0)
     for s in range(2, nz - 1):
-        z_round(s)
+        z_round(s, 1)
+        z_round(s, 0)
     stage1(sz.groups)
 
     ngrad = sgrad
@@ -1431,6 +1449,10 @@
     stage4(3)
     for j in range(sz.chunks):
         stage5(j)
+    for j in range(sz.chunks):
+        stage6(j)
+    for j in range(sz.chunks):
+        pltpu.make_async_copy(od.at[j], o_dense.at[j], isem.at[j]).wait()
 
     for cp in stores:
         cp.wait()
@@ -1466,6 +1488,10 @@
         ((d, 4 * d), BF),
     ]
     buffers = [
+        (tokens.shape, BF),
+        (b1.shape, BF),
+        (b2.shape, BF),
+        ((sz.chunks, sz.shard, d), BF),
         ((d, 4 * d), BF),
         (w2.shape, BF),
         ((sz.tok, d), BF),
@@ -1505,7 +1531,7 @@
         ((2, 2 * sz.images, sz.seq, sz.seq), BF),
         ((n - 1, d, half), BF),
         ((sz.chunks, sz.shard, half), BF),
-        ((nz - 1, sz.chunks, sz.part, half), BF),
+        ((2, sz.chunks, sz.shard, half), BF),
         ((sz.small, d), F32),
         ((sz.small, d), BF),
         ((n + 1, sz.small, d), BF),
@@ -1513,7 +1539,7 @@
         ((nz, sz.small, sz.shard_pad), BF),
     ]
     sems = (
-        [dma((4,)), dma((2,))]
+        [dma((7,)), dma((4,)), dma((2,))]
         + [dma((2, sz.chunks, 2, n)), dma((2, sz.chunks, n))]
         + [dma((2, sz.chunks, 2, n)), dma((sz.chunks, 3))]
         + [dma((3, 2, n))]
@@ -1521,16 +1547,19 @@
         + [dma((2, 2, nz)), dma((2, 2, 2, nz - 1))]
         + [dma((2, n)), dma((2, d // 256, n)), dma((2, n))]
         + [dma((2, sz.chunks)), dma((2, sz.chunks, n))]
-        + [dma((2, sz.chunks, nz))] * 2
+        + [dma((2, 2, sz.chunks)), dma((2, sz.chunks))]
         + [dma((2, sz.chunks)), dma((2,)), dma((2, n)), dma((2, nz))]
     )
     return pl.pallas_call(
         partial(block_kernel, sz),
         name="block",
         out_shape=[jax.ShapeDtypeStruct(s, t) for s, t in outs],
-        in_specs=[vmem] * 7 + [hbm] * 5,
-        out_specs=[vmem] * 2 + [hbm] * 6,
-        scratch_shapes=[pltpu.VMEM(s, t) for s, t in buffers] + sems,
+        in_specs=[hbm] * 12,
+        out_specs=[hbm, vmem] + [hbm] * 6,
+        scratch_shapes=[pltpu.VMEM(s, t) for s, t in buffers[:1]]
+        + [pltpu.VMEM(routes.shape, jnp.int32)]
+        + [pltpu.VMEM(s, t) for s, t in buffers[1:]]
+        + sems,
         compiler_params=pltpu.CompilerParams(
             collective_id=1, has_side_effects=True, vmem_limit_bytes=62 << 20
         ),
@@ -1637,7 +1666,7 @@
     d, fs = sz.d, sz.fs
     w1, w2 = expert_in[0], expert_out[0]
     small = (router.T, norm_gains, dense_biases)
-    if fs % 128 or sz.all_slots % 128 or sz.all_slots < 2 * sz.rows or sz.part % 16:
+    if (sz.nz, sz.chunks * sz.shard, 2 * fs) != (4, d, d) or sz.all_slots < 2 * sz.rows:
         state = front(sz, tokens, out_grad, routes.T, attn_qkv, attn_out, *small)
         bias1, bias2 = expert_in_bias.astype(F32), expert_out_bias.astype(F32)
         return plain_rest(sz, state, tokens, w1, bias1, w2, bias2)

time: 193 us -> 180 us (0.933)
  Pallas kernels: 192 us -> 179 us
    pallas_call x1, Pallas kernels: 188 us -> 174 us  [block(): pl.pallas_call(partial(block_kernel, sz), name='block', out_shape=[jax.Sh...]
where the time goes in v5:
time: 180 us; the launch traced here: 179 us
  Pallas kernels  179 us (99%)
    pallas_call x1, Pallas kernels, block(): pl.pallas_call(partial(block_kernel, sz), name='block', out_shape=[jax.Sh...  174 us
    pallas_call x1, Pallas kernels, finish(): pl.pallas_call(partial(finish_kernel, sz), name='finish', out_shape=[jax....  4.65 us

profile of v5, /device:TPU:0, one launch (start us, length us, event | category | flops | bytes accessed | tf_op | source)
XLA Modules:
  0.0 179.4 jit_solution(8849221606996367509)
XLA Ops:
  0.6 173.9 %block.1 = (bf16[4,192,768]{2,1,0:T(8,128)(2,1)}, f32[16,256]{1,0:T(8,128)}, bf16[394,768]{1,0:T(8,128)(2,1)}, bf16[394,768]{1,0:T(8,128)(2,1)}, bf16[768,384]{1...) custom-call(bf16[394,768]{1,0:T(8,128)(2,1)} %tok_hbm.1, ...), custom_call_target="tpu_custom_call" | custom-call | tf_op jit(solution)/shard_map/block/pallas_call | solution.py:1553
  174.5 4.6 %finish.1 = (bf16[394,768]{1,0:T(8,128)(2,1)}, bf16[394,768]{1,0:T(8,128)(2,1)}, f32[192,2304]{1,0:T(8,128)}, f32[192,768]{1,0:T(8,128)}, f32[4,192]{1,0:T(4,128...) custom-call(bf16[394,768]{1,0:T(8,128)(2,1)} %get-tuple-element.28.o, ...), custom_call_target="tpu_custom_call" | custom-call | tf_op jit(solution)/shard_map/finish/pallas_call | solution.py:491

commit v6 on v5

--- a/solution.py
+++ b/solution.py
@@ -450,30 +450,56 @@
     )(tokens, grad, routes, wq, wp, router, gains, biases)
 
 
-def finish_kernel(sz, out, gin, g1, g2, dense, sg, *refs):
-    o_out, o_gin, o_qkv, o_proj, o_router, o_gains, o_biases, o_w1, o_b1, o_w2, o_b2 = refs
-    o_out[...] = out[...]
-    o_gin[...] = gin[...]
+def finish_kernel(sz, *refs):
+    sources, targets = refs[:6], refs[6:17]
+    ins, outs = refs[17:23], refs[23:32]
+    in_sem, out_sem = refs[32:]
+    out, gin, g1, g2, dense, sg = ins
+    o_qkv, o_proj, o_router, o_gains, o_biases, o_w1, o_b1, o_w2, o_b2 = outs
+    loads = [
+        pltpu.make_async_copy(src, dst, in_sem.at[i])
+        for i, (src, dst) in enumerate(zip(sources, ins))
+    ]
+    stores = [
+        pltpu.make_async_copy(src, dst, out_sem.at[i])
+        for i, (src, dst) in enumerate(zip((out, gin, *outs), targets))
+    ]
+    for i in (2, 3, 4, 0, 1, 5):
+        loads[i].start()
     fs, sh = sz.fs, sz.shard
+    loads[2].wait()
     o_w1[0] = g1[...].astype(F32)
+    stores[7].start()
+    loads[3].wait()
     o_w2[0] = g2[0:fs, :].astype(F32)
+    stores[9].start()
+    loads[4].wait()
+    for g in range(sz.groups):
+        for j in range(3):
+            cols = slice(j * sz.d + g * 256, j * sz.d + (g + 1) * 256)
+            o_qkv[:, cols] = dense[g + 1, :, j * 256 : (j + 1) * 256].astype(F32)
+    stores[2].start()
+    o_proj[...] = dense[0].astype(F32)
+    stores[3].start()
+    for i in range(2):
+        loads[i].wait()
+        stores[i].start()
+    loads[5].wait()
+    o_router[...] = sg[8 : 8 + sz.experts, 0:sh]
+    o_gains[...] = sg[0:2, 0:sh]
+    o_biases[...] = sg[2:7, 0:sh]
     o_b1[...] = g2[fs : fs + 16, :].astype(F32)[0:1, 0:fs]
     own = o_b2.shape[1]
     first = lax.axis_index("rep") * own
     pick = iota((sz.d, own), 0) == iota((sz.d, own), 1) + first
     o_b2[...] = mm(g2[fs : fs + 16, :], pick.astype(F32).astype(BF))[1:2, :]
-    o_proj[...] = dense[0].astype(F32)
-    for g in range(sz.groups):
-        for j in range(3):
-            cols = slice(j * sz.d + g * 256, j * sz.d + (g + 1) * 256)
-            o_qkv[:, cols] = dense[g + 1, :, j * 256 : (j + 1) * 256].astype(F32)
-    o_router[...] = sg[8 : 8 + sz.experts, 0:sh]
-    o_gains[...] = sg[0:2, 0:sh]
-    o_biases[...] = sg[2:7, 0:sh]
+    for i in (4, 5, 6, 8, 10):
+        stores[i].start()
+    for store in stores:
+        store.wait()
 
 
 def finish(sz, out, gin, g1, g2, dense, sg):
-    vmem = pl.BlockSpec(memory_space=pltpu.VMEM)
     d, fs, sh = sz.d, sz.fs, sz.shard
     outs = [
         ((sz.tok, d), BF),
@@ -488,14 +514,19 @@
         ((1, fs, d), F32),
         ((1, d // sz.n_rep), F32),
     ]
+    sources = (out, gin, g1, g2, dense, sg)
+    hbm = pl.BlockSpec(memory_space=pl.ANY)
     grads = pl.pallas_call(
         partial(finish_kernel, sz),
         name="finish",
         out_shape=[jax.ShapeDtypeStruct(s, t) for s, t in outs],
-        in_specs=[vmem] * 6,
-        out_specs=[vmem] * len(outs),
+        in_specs=[hbm] * 6,
+        out_specs=[hbm] * len(outs),
+        scratch_shapes=[pltpu.VMEM(a.shape, a.dtype) for a in sources]
+        + [pltpu.VMEM(s, t) for s, t in outs[2:]]
+        + [pltpu.SemaphoreType.DMA((6,)), pltpu.SemaphoreType.DMA((11,))],
         compiler_params=pltpu.CompilerParams(vmem_limit_bytes=62 << 20),
-    )(out, gin, g1, g2, dense, sg)
+    )(*sources)
     return (*grads[:4], grads[4].T, *grads[5:])
 
 
@@ -1114,6 +1145,10 @@
 
     def z_round(s, which):
         v, u = ((v1, u1), (v2, u2))[which]
+        pieces = [
+            [slice(i, min(i + 128, size)) for i in range(0, size, 128)]
+            for size in (d, sz.fs_rows)
+        ]
         for way in range(2):
             zz = z if way == 0 else nz - 1 - z
             dest = nz - 1 - s + zz if way == 0 else z - (nz - 1 - s)
@@ -1125,7 +1160,9 @@
                 there = landing(way, s, z + 1 if way == 0 else z - 1)
                 at_here, at_there = (u1.at[here], u2.at[here]), there
                 u_copies(*at_here, way, s - 1, target, here)[which].wait_recv()
-                u[here] = (u[here].astype(F32) + v[dest].astype(F32)).astype(BF)
+                for rows in pieces[which]:
+                    value = u[here, rows, :].astype(F32) + v[dest, rows, :].astype(F32)
+                    u[here, rows, :] = value.astype(BF)
                 u_copies(*at_here, way, s, target, at_there)[which].start()
 
     prepare(0)
@@ -1347,11 +1384,16 @@
         ).astype(BF)
         to_sibling(g + 1).start()
         stage1(g)
+
+        @pl.when(g == sz.groups - 2)
+        def _():
+            for s in range(2, nz - 1):
+                z_round(s, 1)
+
         return carry
 
     lax.fori_loop(0, sz.groups, group_step, 0)
     for s in range(2, nz - 1):
-        z_round(s, 1)
         z_round(s, 0)
     stage1(sz.groups)
 

time: 180 us -> 177 us (0.983)
  Pallas kernels: 179 us -> 176 us
where the time goes in v6:
time: 177 us
  Pallas kernels  176 us (99%)
    pallas_call x1, Pallas kernels, block(): pl.pallas_call(partial(block_kernel, sz), name='block', out_shape=[jax.Sh...  172 us
    pallas_call x1, Pallas kernels, finish(): pl.pallas_call(partial(finish_kernel, sz), name='finish', out_shape=[jax....  3.87 us

profile of v6, /device:TPU:0, one launch (start us, length us, event | category | flops | bytes accessed | tf_op | source)
XLA Modules:
  0.0 177.1 jit_solution(9190036712626665882)
XLA Ops:
  0.6 172.4 %block.1 = (bf16[4,192,768]{2,1,0:T(8,128)(2,1)}, f32[16,256]{1,0:T(8,128)}, bf16[394,768]{1,0:T(8,128)(2,1)}, bf16[394,768]{1,0:T(8,128)(2,1)}, bf16[768,384]{1...) custom-call(bf16[394,768]{1,0:T(8,128)(2,1)} %tok_hbm.1, ...), custom_call_target="tpu_custom_call" | custom-call | tf_op jit(solution)/shard_map/block/pallas_call | solution.py:1595
  173.0 3.9 %finish.1 = (bf16[394,768]{1,0:T(8,128)(2,1)}, bf16[394,768]{1,0:T(8,128)(2,1)}, f32[192,2304]{1,0:T(8,128)}, f32[192,768]{1,0:T(8,128)}, f32[4,192]{1,0:T(4,128...) custom-call(bf16[394,768]{1,0:T(8,128)(2,1)} %get-tuple-element.28.r, ...), custom_call_target="tpu_custom_call" | custom-call | tf_op jit(solution)/shard_map/finish/pallas_call | solution.py:519

commit v7 on v6

--- a/solution.py
+++ b/solution.py
@@ -824,7 +824,7 @@
     for k in range(1, n):
         for cp in small_sends(k):
             cp.start()
-    for g in range(sz.groups + 1):
+    for g in range(sz.groups):
         start_weights(g)
     loads[0].wait()
     wide1[...] = mm(pad_matrix(sz), tok_ref[...])
@@ -864,6 +864,7 @@
         return (slot_ids == slot[e : e + 1, :]).astype(F32).astype(BF)
 
     forward_weights(1)
+    start_weights(sz.groups)
 
     load_grad.wait()
     gpad[...] = mm(pad_matrix(sz), stage[...]).astype(BF)
@@ -881,9 +882,9 @@
     for k in range(n):
         gs[at_peer(k), :] = mm(picks_for(k), gpad[...]).astype(BF)
     dres[at_peer(0), :] = gs[at_peer(0), :]
+    for k in range(1, n):
+        to_peer(gs.at[at_peer(k), :], dres.at[at_peer(n - k), :], g_sem, k).start()
     forward_weights(2)
-    for k in range(1, n):
-        to_peer(gs.at[at_peer(k), :], dres.at[at_peer(n - k), :], g_sem, k).start()
 
     scale = 1.0 / math.sqrt(HEAD_DIM)
     half_lane = iota((sz.seq, 128), 1)
@@ -1179,6 +1180,8 @@
     own_grads(0)
     cells(1, nz, others)
     lax.fori_loop(0, d // 256, back_rows, 0)
+    if nz > 2:
+        z_round(1, 1)
     column = lax.fori_loop(
         0, d // 256, back_results, jnp.zeros((sz.all_slots, 1), F32)
     )
@@ -1197,8 +1200,6 @@
         own_grads(i)
         return carry
 
-    if nz > 2:
-        z_round(1, 1)
     lax.fori_loop(1, nz, slice_step, 0)
     if nz > 2:
         z_round(1, 0)

time: 177 us -> 177 us (level)
  no operation moved by 1% of the time
where the time goes in v7:
time: 177 us
  Pallas kernels  176 us (99%)
    pallas_call x1, Pallas kernels, block(): pl.pallas_call(partial(block_kernel, sz), name='block', out_shape=[jax.Sh...  172 us
    pallas_call x1, Pallas kernels, finish(): pl.pallas_call(partial(finish_kernel, sz), name='finish', out_shape=[jax....  3.87 us

profile of v7, /device:TPU:0, one launch (start us, length us, event | category | flops | bytes accessed | tf_op | source)
XLA Modules:
  0.0 177.0 jit_solution(1460497172198764891)
XLA Ops:
  0.6 172.3 %block.1 = (bf16[4,192,768]{2,1,0:T(8,128)(2,1)}, f32[16,256]{1,0:T(8,128)}, bf16[394,768]{1,0:T(8,128)(2,1)}, bf16[394,768]{1,0:T(8,128)(2,1)}, bf16[768,384]{1...) custom-call(bf16[394,768]{1,0:T(8,128)(2,1)} %tok_hbm.1, ...), custom_call_target="tpu_custom_call" | custom-call | tf_op jit(solution)/shard_map/block/pallas_call | solution.py:1596
  172.9 3.9 %finish.1 = (bf16[394,768]{1,0:T(8,128)(2,1)}, bf16[394,768]{1,0:T(8,128)(2,1)}, f32[192,2304]{1,0:T(8,128)}, f32[192,768]{1,0:T(8,128)}, f32[4,192]{1,0:T(4,128...) custom-call(bf16[394,768]{1,0:T(8,128)(2,1)} %get-tuple-element.28.r, ...), custom_call_target="tpu_custom_call" | custom-call | tf_op jit(solution)/shard_map/finish/pallas_call | solution.py:519
